TPU v7x, 512 devices: a whole 4x8x8 slice. The times are simulated.
512 devices in a mesh: outer: 32 (over z_hi, y, core), inner: 16 (over x, z_lo).
Axes of the slice: x: 4, y: 8, z: 8 (z_hi: 2, z_lo: 4; z = z_hi * 4 + z_lo), core: 2. Of those that a mesh axis runs over, the one named last changes fastest.
Arguments:
- projected: bfloat16 [262144, 384], P(('outer', 'inner')), may hold values from -6 to 6
- short_taps: float32 [3, 384], replicated, may hold values from -3.5 to 3.5
- skip_gain: float32 [128], replicated, may hold values from 0.5 to 1.5
- long_filter: bfloat16 [262144], P(('outer', 'inner')), may hold values from -0.01171875 to 0.01171875
Outputs:
- output: float32 [262144, 128], P(('outer', 'inner'))
All inputs are finite; a program needn't handle non-finite values.
Results may differ from a plain program's by a relative error of at most 0.0045.
Values may be sent and summed in bfloat16 or wider, within the bound.
No kernel may reach another device: no remote copies, remote signals or barrier semaphores. Data moves between devices by JAX's collectives and lax.ppermute only.
A program may use at most 64 MiB of HBM per device.

v0:
```python
import math

import jax
import jax.numpy as jnp
from jax import lax
from jax.sharding import PartitionSpec as P

dense_side = 128
highest = lax.Precision.HIGHEST


def passed_along(value, axis, steps):
    count = lax.axis_size(axis)
    leading, last = (max(0, -steps), min(count, count - steps))
    return lax.ppermute(value, axis, [(source, source + steps) for source in range(leading, last)])


def phase_table(row_count, col_count, modulus, turning):
    left_index = lax.broadcasted_iota(jnp.int32, (row_count, col_count), 0)
    right_index = lax.broadcasted_iota(jnp.int32, (row_count, col_count), 1)
    angles = (left_index * right_index % modulus).astype(jnp.float32) * (
        turning * 2.0 * math.pi / modulus
    )
    return (jnp.cos(angles), jnp.sin(angles))


def apply_table(form, table, real_part, imag_part):
    cos_table, sin_table = table
    real_out = jnp.einsum(form, cos_table, real_part, precision=highest)
    imag_out = jnp.einsum(form, sin_table, real_part, precision=highest)
    real_out = real_out - jnp.einsum(form, sin_table, imag_part, precision=highest)
    imag_out = imag_out + jnp.einsum(form, cos_table, imag_part, precision=highest)
    return (real_out, imag_out)


def rotate(real_part, imag_part, cos_table, sin_table):
    return (
        real_part * cos_table - imag_part * sin_table,
        real_part * sin_table + imag_part * cos_table,
    )


def local_transform(real_part, imag_part, turning):
    extent = real_part.shape[0]
    breadth = real_part.shape[1]
    outer_side = extent // dense_side
    shaped_real = real_part.reshape(outer_side, dense_side, breadth)
    shaped_imag = imag_part.reshape(outer_side, dense_side, breadth)
    first_real, first_imag = apply_table(
        "ka,abx->kbx",
        phase_table(outer_side, outer_side, outer_side, turning),
        shaped_real,
        shaped_imag,
    )
    cos_turn, sin_turn = phase_table(outer_side, dense_side, extent, turning)
    turned_real, turned_imag = rotate(
        first_real, first_imag, cos_turn[:, :, None], sin_turn[:, :, None]
    )
    last_real, last_imag = apply_table(
        "jb,kbx->jkx",
        phase_table(dense_side, dense_side, dense_side, turning),
        turned_real,
        turned_imag,
    )
    return (last_real.reshape(extent, breadth), last_imag.reshape(extent, breadth))


def split_channels(values_in):
    return (values_in, jnp.zeros_like(values_in))


def doubled(real_part, imag_part, block_index, block_count):
    angles = block_index.astype(jnp.float32) * (-math.pi / block_count)
    turned_real, turned_imag = rotate(real_part, imag_part, jnp.cos(angles), jnp.sin(angles))
    return (
        jnp.concatenate([real_part, turned_real], axis=-1),
        jnp.concatenate([imag_part, turned_imag], axis=-1),
    )


def twist_angles(seg_len, residues, double_length):
    row_index = lax.broadcasted_iota(jnp.int32, (seg_len, 1), 0)
    return (row_index * residues % double_length).astype(jnp.float32) * (
        2.0 * math.pi / double_length
    )


def residue_row(position, width):
    first = jnp.full((1, width), 2, jnp.int32) * position
    return jnp.concatenate([first, first + 1], axis=1)


def on_device(projected, short_taps, skip_gain, long_filter):
    seg_len = projected.shape[0]
    channels = skip_gain.shape[0]
    outer_count = lax.axis_size("outer")
    inner_count = lax.axis_size("inner")
    block_count = outer_count * inner_count
    group_rows = seg_len // block_count
    full_length = seg_len * block_count
    double_length = 2 * full_length
    position = lax.axis_index(("outer", "inner"))
    tap_count = short_taps.shape[0]
    reach = tap_count - 1
    earlier = passed_along(projected[seg_len - reach :], ("outer", "inner"), 1)
    extended = jnp.concatenate([earlier, projected], axis=0).astype(jnp.float32)
    filtered = short_taps[0] * extended[reach:]
    for tap_number in range(1, tap_count):
        filtered = (
            filtered
            + short_taps[tap_number] * extended[reach - tap_number : reach - tap_number + seg_len]
        )
    queries = filtered[:, :channels]
    mixture = (filtered[:, channels : 2 * channels] * filtered[:, 2 * channels :]).astype(
        jnp.bfloat16
    )
    blocked = mixture.reshape(outer_count, inner_count, group_rows, channels)
    filter_blocked = long_filter.reshape(outer_count, inner_count, group_rows, 1)
    spread, filter_spread = (
        lax.all_to_all(
            lax.all_to_all(blocked, "outer", split_axis=0, concat_axis=0, tiled=True),
            "inner",
            split_axis=1,
            concat_axis=1,
            tiled=True,
        ),
        lax.all_to_all(
            lax.all_to_all(filter_blocked, "outer", split_axis=0, concat_axis=0, tiled=True),
            "inner",
            split_axis=1,
            concat_axis=1,
            tiled=True,
        ),
    )
    real_in, imag_in = split_channels(
        spread.astype(jnp.float32).reshape(block_count, group_rows, channels)
    )
    lane = real_in.shape[-1]
    block_index = lax.broadcasted_iota(jnp.int32, (block_count, 1, 1), 0)
    twin_real, twin_imag = doubled(real_in, imag_in, block_index, block_count)
    wave_real, wave_imag = local_transform(
        twin_real.reshape(block_count, -1), twin_imag.reshape(block_count, -1), -1.0
    )
    tap_real = filter_spread.astype(jnp.float32).reshape(block_count, group_rows, 1)
    tap_real, tap_imag = doubled(tap_real, jnp.zeros_like(tap_real), block_index, block_count)
    fwave_real, fwave_imag = local_transform(
        tap_real.reshape(block_count, -1), tap_imag.reshape(block_count, -1), -1.0
    )
    block_shape = (outer_count, inner_count, group_rows, 2 * lane)
    filter_shape = (outer_count, inner_count, group_rows, 2)
    stacked = jnp.stack([wave_real.reshape(block_shape), wave_imag.reshape(block_shape)])
    filter_stacked = jnp.stack([fwave_real.reshape(filter_shape), fwave_imag.reshape(filter_shape)])
    arrived, filter_arrived = (
        lax.all_to_all(
            lax.all_to_all(stacked, "outer", split_axis=1, concat_axis=1, tiled=True),
            "inner",
            split_axis=2,
            concat_axis=2,
            tiled=True,
        ),
        lax.all_to_all(
            lax.all_to_all(filter_stacked, "outer", split_axis=1, concat_axis=1, tiled=True),
            "inner",
            split_axis=2,
            concat_axis=2,
            tiled=True,
        ),
    )
    line_real = arrived[0].reshape(seg_len, 2 * lane)
    line_imag = arrived[1].reshape(seg_len, 2 * lane)
    twist = twist_angles(seg_len, residue_row(position, lane), double_length)
    cos_twist = jnp.cos(twist)
    sin_twist = jnp.sin(twist)
    line_real, line_imag = rotate(line_real, line_imag, cos_twist, -sin_twist)
    freq_real, freq_imag = local_transform(line_real, line_imag, -1.0)
    filter_twist = twist_angles(seg_len, residue_row(position, 1), double_length)
    fline_real, fline_imag = rotate(
        filter_arrived[0].reshape(seg_len, 2),
        filter_arrived[1].reshape(seg_len, 2),
        jnp.cos(filter_twist),
        -jnp.sin(filter_twist),
    )
    fresp_real, fresp_imag = local_transform(fline_real, fline_imag, -1.0)
    filter_real = jnp.repeat(fresp_real, lane, axis=1)
    filter_imag = jnp.repeat(fresp_imag, lane, axis=1)
    prod_real = freq_real * filter_real - freq_imag * filter_imag
    prod_imag = freq_real * filter_imag + freq_imag * filter_real
    back_real, back_imag = local_transform(prod_real, prod_imag, 1.0)
    back_real, back_imag = rotate(back_real, back_imag, cos_twist, sin_twist)
    packed = jnp.stack([back_real.reshape(block_shape), back_imag.reshape(block_shape)])
    returned = lax.all_to_all(
        lax.all_to_all(packed, "outer", split_axis=1, concat_axis=1, tiled=True),
        "inner",
        split_axis=2,
        concat_axis=2,
        tiled=True,
    )
    final_real, final_imag = local_transform(
        returned[0].reshape(block_count, -1), returned[1].reshape(block_count, -1), 1.0
    )
    final_real = final_real.reshape(block_count, group_rows, 2 * lane)
    final_imag = final_imag.reshape(block_count, group_rows, 2 * lane)
    back_index = lax.broadcasted_iota(jnp.int32, (block_count, 1, 1), 0).astype(jnp.float32) * (
        math.pi / block_count
    )
    cos_back = jnp.cos(back_index)
    sin_back = jnp.sin(back_index)
    odd_real, odd_imag = rotate(final_real[..., lane:], final_imag[..., lane:], cos_back, sin_back)
    sum_real = final_real[..., :lane] + odd_real
    home_shape = (outer_count, inner_count, group_rows, channels)
    settled_in = sum_real * (1.0 / double_length)
    settled = lax.all_to_all(
        lax.all_to_all(
            settled_in.reshape(home_shape), "outer", split_axis=0, concat_axis=0, tiled=True
        ),
        "inner",
        split_axis=1,
        concat_axis=1,
        tiled=True,
    )
    convolved = settled.reshape(seg_len, channels)
    return queries * (convolved + skip_gain * mixture.astype(jnp.float32))


def solution(mesh):
    placed = (P(("outer", "inner"), None), P(), P(), P(("outer", "inner")))
    return jax.shard_map(
        on_device,
        mesh=mesh,
        in_specs=placed,
        out_specs=P(("outer", "inner"), None),
        check_vma=False,
    )
```

profile of v0, /device:TPU:8, one launch (start us, length us, event | category | flops | bytes accessed | tf_op | source)
XLA Modules:
  0.0 328.8 jit_solution(16251342890230687821)
XLA Ops:
  0.7 4.3 %collective-permute-start = (bf16[2,384]{1,0:T(2,128)(2,1)S(1)}, bf16[2,384]{1,0:T(2,128)(2,1)S(1)}, u32[]{:S(2)}, u32[]{:S(2)}) collective-permute-start(bf16[2,384]{1,0:T(2,128)(2,1)S(1)} %slice.58), channel_id=1, source_target_pairs={{0,1},{1,2},{2,3},{3,4},{4,5},{5,6},{6,7},{7,8},{8,9},{9,10},{10,1... | collective-permute-start | bytes 4616 | tf_op jit(solution)/shard_map/ppermute | solution.py:15
  5.7 15.4 %all-to-all-start.4 = ((bf16[32,16,1,1]{1,3,2,0:T(2,128)(2,1)}), bf16[32,16,1,1]{1,3,2,0:T(2,128)(2,1)S(1)}, u32[]{:S(2)}, u32[]{:S(2)}) async-start(bf16[32,16,1,1]{1,3,2,0:T(2,128)(2,1)} %reshape.464), calls=%async_computation.4 | async-start | bytes 32768 | tf_op jit(solution)/shard_map/all_to_all | solution.py:128
  21.2 1.1 maximum_convert_fusion
  22.5 9.6 %all-to-all-done.4 = bf16[32,16,1,1]{1,3,2,0:T(2,128)(2,1)S(1)} async-done(((bf16[32,16,1,1]{1,3,2,0:T(2,128)(2,1)}), bf16[32,16,1,1]{1,3,2,0:T(2,128)(2,1)S(1)}, u32[]{:S(2)}, u32[]{:S(2)}) %all-to-all-start.4) | async-done | bytes 1056 | tf_op jit(solution)/shard_map/all_to_all | solution.py:128
  32.8 6.8 %all-to-all-start.5 = ((bf16[32,16,1,1]{0,3,2,1:T(2,128)(2,1)}), bf16[32,16,1,1]{0,3,2,1:T(2,128)(2,1)S(1)}, u32[]{:S(2)}, u32[]{:S(2)}) async-start(bf16[32,16,1,1]{0,3,2,1:T(2,128)(2,1)} %copy.245), calls=%async_computation.5 | async-start | bytes 16384 | tf_op jit(solution)/shard_map/all_to_all | solution.py:127
  40.4 7.2 %all-to-all-done.5 = bf16[32,16,1,1]{0,3,2,1:T(2,128)(2,1)S(1)} async-done(((bf16[32,16,1,1]{0,3,2,1:T(2,128)(2,1)}), bf16[32,16,1,1]{0,3,2,1:T(2,128)(2,1)S(1)}, u32[]{:S(2)}, u32[]{:S(2)}) %all-to-all-start.5) | async-done | bytes 1056 | tf_op jit(solution)/shard_map/all_to_all | solution.py:127
  47.6 4.9 %all-to-all-start = ((bf16[32,16,1,128]{3,1,2,0:T(8,128)(2,1)}), bf16[32,16,1,128]{3,1,2,0:T(8,128)(2,1)S(1)}, u32[]{:S(2)}, u32[]{:S(2)}) async-start(bf16[32,16,1,128]{3,1,2,0:T(8,128)(2,1)} %bitcast.5), calls=%async_computation | async-start | bytes 262144 | tf_op jit(solution)/shard_map/all_to_all | solution.py:121
  56.8 9.1 %all-to-all-done = bf16[32,16,1,128]{3,1,2,0:T(8,128)(2,1)S(1)} async-done(((bf16[32,16,1,128]{3,1,2,0:T(8,128)(2,1)}), bf16[32,16,1,128]{3,1,2,0:T(8,128)(2,1)S(1)}, u32[]{:S(2)}, u32[]{:S(2)}) %all-to-all-start) | async-done | bytes 131104 | tf_op jit(solution)/shard_map/all_to_all | solution.py:121
  65.8 4.8 %all-to-all-start.6 = ((f32[2,32,16,1,2]{2,4,3,0,1:T(2,128)}), f32[2,32,16,1,2]{2,4,3,0,1:T(2,128)S(1)}, u32[]{:S(2)}, u32[]{:S(2)}) async-start(f32[2,32,16,1,2]{2,4,3,0,1:T(2,128)} %copy.251), calls=%async_computation.6 | async-start | bytes 131072 | tf_op jit(solution)/shard_map/all_to_all | solution.py:162
  71.4 11.2 %all-to-all-done.6 = f32[2,32,16,1,2]{2,4,3,0,1:T(2,128)S(1)} async-done(((f32[2,32,16,1,2]{2,4,3,0,1:T(2,128)}), f32[2,32,16,1,2]{2,4,3,0,1:T(2,128)S(1)}, u32[]{:S(2)}, u32[]{:S(2)}) %all-to-all-start.6) | async-done | bytes 8224 | tf_op jit(solution)/shard_map/all_to_all | solution.py:162
  82.6 3.5 %all-to-all-start.1 = ((bf16[32,16,1,128]{3,0,2,1:T(8,128)(2,1)}), bf16[32,16,1,128]{3,0,2,1:T(8,128)(2,1)S(1)}, u32[]{:S(2)}, u32[]{:S(2)}) async-start(bf16[32,16,1,128]{3,0,2,1:T(8,128)(2,1)} %copy.217), calls=%async_computation.1 | async-start | bytes 262144 | tf_op jit(solution)/shard_map/all_to_all | solution.py:120
  87.5 6.9 %all-to-all-done.1 = bf16[32,16,1,128]{3,0,2,1:T(8,128)(2,1)S(1)} async-done(((bf16[32,16,1,128]{3,0,2,1:T(8,128)(2,1)}), bf16[32,16,1,128]{3,0,2,1:T(8,128)(2,1)S(1)}, u32[]{:S(2)}, u32[]{:S(2)}) %all-to-all-start.1) | async-done | bytes 131104 | tf_op jit(solution)/shard_map/all_to_all | solution.py:120
  94.5 3.6 %all-to-all-start.7 = ((f32[16,1,128]{2,1,0:T(1,128)}), f32[16,1,128]{2,1,0:T(1,128)S(1)}, u32[]{:S(2)}, u32[]{:S(2)}) async-start(f32[16,1,128]{2,1,0:T(1,128)} %reshape.468), calls=%async_computation.7 | async-start | bytes 16384 | tf_op jit(solution)/shard_map/all_to_all | solution.py:161
  98.4 1.0 fusion.53
  99.5 1.0 fusion.52
  100.8 1.3 convolution_subtract_fusion.3
  102.1 1.6 multiply_add_fusion.6
  106.8 0.9 convolution_subtract_fusion.7
  108.4 1.1 copy.233
  109.4 5.0 %all-to-all-start.2 = ((f32[2,32,16,1,256]{4,2,3,0,1:T(8,128)}), f32[2,32,16,1,256]{4,2,3,0,1:T(8,128)S(1)}, u32[]{:S(2)}, u32[]{:S(2)}) async-start(f32[2,32,16,1,256]{4,2,3,0,1:T(8,128)} %copy.233), calls=%async_computation.2 | async-start | bytes 2097152 | tf_op jit(solution)/shard_map/all_to_all | solution.py:155
  117.1 30.3 %all-to-all-done.2 = f32[2,32,16,1,256]{4,2,3,0,1:T(8,128)S(1)} async-done(((f32[2,32,16,1,256]{4,2,3,0,1:T(8,128)}), f32[2,32,16,1,256]{4,2,3,0,1:T(8,128)S(1)}, u32[]{:S(2)}, u32[]{:S(2)}) %all-to-all-start.2) | async-done | bytes 1048608 | tf_op jit(solution)/shard_map/all_to_all | solution.py:155
  147.4 1.6 copy.234
  149.0 7.9 %all-to-all-start.3 = ((f32[2,32,16,1,256]{4,1,3,0,2:T(8,128)}), f32[2,32,16,1,256]{4,1,3,0,2:T(8,128)S(1)}, u32[]{:S(2)}, u32[]{:S(2)}) async-start(f32[2,32,16,1,256]{4,1,3,0,2:T(8,128)} %copy.234), calls=%async_computation.3 | async-start | bytes 2097152 | tf_op jit(solution)/shard_map/all_to_all | solution.py:154
  162.3 21.3 %all-to-all-done.3 = f32[2,32,16,1,256]{4,1,3,0,2:T(8,128)S(1)} async-done(((f32[2,32,16,1,256]{4,1,3,0,2:T(8,128)}), f32[2,32,16,1,256]{4,1,3,0,2:T(8,128)S(1)}, u32[]{:S(2)}, u32[]{:S(2)}) %all-to-all-start.3) | async-done | bytes 1048608 | tf_op jit(solution)/shard_map/all_to_all | solution.py:154
  185.1 2.3 multiply_add_fusion.5
  187.4 1.2 fusion.48
  188.7 1.3 fusion.46
  189.9 1.3 convolution_subtract_fusion.2
  191.2 1.6 multiply_add_fusion.4
  195.8 1.0 reshape.449
  196.8 0.9 convolution_subtract_fusion.6
  199.2 1.3 fusion.42
  200.5 1.4 fusion.40
  201.9 1.3 convolution_subtract_fusion.1
  203.2 1.6 multiply_add_fusion.2
  208.0 0.9 convolution_subtract_fusion.5
  209.9 2.3 multiply_subtract_fusion.1
  212.4 37.4 %all_to_all.60 = f32[2,32,16,1,256]{4,2,3,0,1:T(8,128)S(1)} all-to-all(f32[2,32,16,1,256]{4,2,3,0,1:T(8,128)S(1)} %copy.274), channel_id=1, replica_groups=mesh['outer'=32,'inner'=16] {'outer'}, dimensions={1} | all-to-all | bytes 2097152 | tf_op jit(solution)/shard_map/all_to_all | solution.py:192
  249.8 1.6 copy.275
  251.4 3.9 %all-to-all-start.9 = ((f32[2,32,16,1,256]{4,1,3,0,2:T(8,128)}), f32[2,32,16,1,256]{4,1,3,0,2:T(8,128)S(1)}, u32[]{:S(2)}, u32[]{:S(2)}) async-start(f32[2,32,16,1,256]{4,1,3,0,2:T(8,128)} %copy.275), calls=%async_computation.9 | async-start | bytes 2097152 | tf_op jit(solution)/shard_map/all_to_all | solution.py:191
  255.3 26.8 %all-to-all-done.9 = f32[2,32,16,1,256]{4,1,3,0,2:T(8,128)S(1)} async-done(((f32[2,32,16,1,256]{4,1,3,0,2:T(8,128)}), f32[2,32,16,1,256]{4,1,3,0,2:T(8,128)S(1)}, u32[]{:S(2)}, u32[]{:S(2)}) %all-to-all-start.9) | async-done | bytes 1048608 | tf_op jit(solution)/shard_map/all_to_all | solution.py:191
  282.5 1.2 fusion.36
  283.8 1.2 fusion.34
  285.3 1.3 convolution_subtract_fusion
  286.6 1.6 multiply_add_fusion
  291.4 0.9 convolution_subtract_fusion.4
  293.0 20.7 %all_to_all.61 = f32[32,16,1,128]{3,1,2,0:T(8,128)S(1)} all-to-all(f32[32,16,1,128]{3,1,2,0:T(8,128)S(1)} %bitcast.176), channel_id=1, replica_groups=mesh['outer'=32,'inner'=16] {'outer'}, dimensions={0} | all-to-all | bytes 524288 | tf_op jit(solution)/shard_map/all_to_all | solution.py:213
  313.8 13.3 %all_to_all.62 = f32[32,16,1,128]{3,0,2,1:T(8,128)S(1)} all-to-all(f32[32,16,1,128]{3,0,2,1:T(8,128)S(1)} %copy.289), channel_id=1, replica_groups=mesh['outer'=32,'inner'=16] {'inner'}, dimensions={1} | all-to-all | bytes 524288 | tf_op jit(solution)/shard_map/all_to_all | solution.py:212
  (143 shorter events, 37.9 us)
Async XLA Ops:
  0.0 5.0 %copy-start.10 = (bf16[512]{0:T(512)(128)(2,1)S(1)}, bf16[512]{0:T(512)(128)(2,1)}, u32[]{:S(2)}) copy-start(bf16[512]{0:T(512)(128)(2,1)} %param.7) | copy-start | bytes 3076
  0.7 20.5 %collective-permute-start = (bf16[2,384]{1,0:T(2,128)(2,1)S(1)}, bf16[2,384]{1,0:T(2,128)(2,1)S(1)}, u32[]{:S(2)}, u32[]{:S(2)}) collective-permute-start(bf16[2,384]{1,0:T(2,128)(2,1)S(1)} %slice.58), channel_id=1, source_target_pairs={{0,1},{1,2},{2,3},{3,4},{4,5},{5,6},{6,7},{7,8},{8,9},{9,10},{10,1... | collective-permute-start | bytes 4616 | tf_op jit(solution)/shard_map/ppermute | solution.py:15
  5.7 15.4 %copy-start.9 = (f32[3,384]{1,0:T(4,128)S(1)}, f32[3,384]{1,0:T(4,128)}, u32[]{:S(2)}) copy-start(f32[3,384]{1,0:T(4,128)} %param.5) | copy-start | bytes 13828
  5.7 26.5 %all-to-all-start.4 = ((bf16[32,16,1,1]{1,3,2,0:T(2,128)(2,1)}), bf16[32,16,1,1]{1,3,2,0:T(2,128)(2,1)S(1)}, u32[]{:S(2)}, u32[]{:S(2)}) async-start(bf16[32,16,1,1]{1,3,2,0:T(2,128)(2,1)} %reshape.464), calls=%async_computation.4 | async-start | bytes 32768 | tf_op jit(solution)/shard_map/all_to_all | solution.py:128
  32.8 14.7 %all-to-all-start.5 = ((bf16[32,16,1,1]{0,3,2,1:T(2,128)(2,1)}), bf16[32,16,1,1]{0,3,2,1:T(2,128)(2,1)S(1)}, u32[]{:S(2)}, u32[]{:S(2)}) async-start(bf16[32,16,1,1]{0,3,2,1:T(2,128)(2,1)} %copy.245), calls=%async_computation.5 | async-start | bytes 16384 | tf_op jit(solution)/shard_map/all_to_all | solution.py:127
  47.6 18.3 %all-to-all-start = ((bf16[32,16,1,128]{3,1,2,0:T(8,128)(2,1)}), bf16[32,16,1,128]{3,1,2,0:T(8,128)(2,1)S(1)}, u32[]{:S(2)}, u32[]{:S(2)}) async-start(bf16[32,16,1,128]{3,1,2,0:T(8,128)(2,1)} %bitcast.5), calls=%async_computation | async-start | bytes 262144 | tf_op jit(solution)/shard_map/all_to_all | solution.py:121
  65.8 16.8 %all-to-all-start.6 = ((f32[2,32,16,1,2]{2,4,3,0,1:T(2,128)}), f32[2,32,16,1,2]{2,4,3,0,1:T(2,128)S(1)}, u32[]{:S(2)}, u32[]{:S(2)}) async-start(f32[2,32,16,1,2]{2,4,3,0,1:T(2,128)} %copy.251), calls=%async_computation.6 | async-start | bytes 131072 | tf_op jit(solution)/shard_map/all_to_all | solution.py:162
  82.6 11.9 %all-to-all-start.1 = ((bf16[32,16,1,128]{3,0,2,1:T(8,128)(2,1)}), bf16[32,16,1,128]{3,0,2,1:T(8,128)(2,1)S(1)}, u32[]{:S(2)}, u32[]{:S(2)}) async-start(bf16[32,16,1,128]{3,0,2,1:T(8,128)(2,1)} %copy.217), calls=%async_computation.1 | async-start | bytes 262144 | tf_op jit(solution)/shard_map/all_to_all | solution.py:120
  86.3 15.8 %copy-start.1 = (f32[4,128]{0,1:T(8,128)}, f32[4,128]{0,1:T(8,128)S(1)}, u32[]{:S(2)}) copy-start(f32[4,128]{0,1:T(8,128)S(1)} %copy.226) | copy-start | bytes 6148
  86.4 15.6 %copy-start.3 = (f32[4,128]{0,1:T(8,128)}, f32[4,128]{0,1:T(8,128)S(1)}, u32[]{:S(2)}) copy-start(f32[4,128]{0,1:T(8,128)S(1)} %copy.224) | copy-start | bytes 6148
  94.5 15.0 %all-to-all-start.7 = ((f32[16,1,128]{2,1,0:T(1,128)}), f32[16,1,128]{2,1,0:T(1,128)S(1)}, u32[]{:S(2)}, u32[]{:S(2)}) async-start(f32[16,1,128]{2,1,0:T(1,128)} %reshape.468), calls=%async_computation.7 | async-start | bytes 16384 | tf_op jit(solution)/shard_map/all_to_all | solution.py:161
  109.4 38.0 %all-to-all-start.2 = ((f32[2,32,16,1,256]{4,2,3,0,1:T(8,128)}), f32[2,32,16,1,256]{4,2,3,0,1:T(8,128)S(1)}, u32[]{:S(2)}, u32[]{:S(2)}) async-start(f32[2,32,16,1,256]{4,2,3,0,1:T(8,128)} %copy.233), calls=%async_computation.2 | async-start | bytes 2097152 | tf_op jit(solution)/shard_map/all_to_all | solution.py:155
  115.4 42.3 %copy-start.5 = (s32[4,128]{1,0:T(4,128)}, s32[4,128]{1,0:T(4,128)S(1)}, u32[]{:S(2)}) copy-start(s32[4,128]{1,0:T(4,128)S(1)} %multiply_add_fusion.12) | copy-start | bytes 6148
  149.0 34.6 %all-to-all-start.3 = ((f32[2,32,16,1,256]{4,1,3,0,2:T(8,128)}), f32[2,32,16,1,256]{4,1,3,0,2:T(8,128)S(1)}, u32[]{:S(2)}, u32[]{:S(2)}) async-start(f32[2,32,16,1,256]{4,1,3,0,2:T(8,128)} %copy.234), calls=%async_computation.3 | async-start | bytes 2097152 | tf_op jit(solution)/shard_map/all_to_all | solution.py:154
  184.4 0.7 copy-start.6
  184.4 0.7 copy-start.7
  189.9 1.3 copy-start.2
  189.9 1.3 copy-start.4
  198.0 1.0 copy-start
  209.2 0.7 copy-start.8
  251.4 30.7 %all-to-all-start.9 = ((f32[2,32,16,1,256]{4,1,3,0,2:T(8,128)}), f32[2,32,16,1,256]{4,1,3,0,2:T(8,128)S(1)}, u32[]{:S(2)}, u32[]{:S(2)}) async-start(f32[2,32,16,1,256]{4,1,3,0,2:T(8,128)} %copy.275), calls=%async_computation.9 | async-start | bytes 2097152 | tf_op jit(solution)/shard_map/all_to_all | solution.py:191
  327.1 0.7 copy-start.11
where the time goes:
time: 334 us; the launch traced here: 329 us
  waiting for transfers between devices  123 us (37%)
  blocking collectives  71.4 us (21%)
  starting transfers between devices  60.1 us (18%)
  matrix products  40.4 us (12%)
  local copies, waits for them, and re-layouts  23.4 us (7%)
  other arithmetic  9.85 us (3%)
    all_to_all x1, blocking collectives, on_device(): lax.all_to_all(packed, 'outer', split_axis=1, concat_axis=1, tiled=True)  37.4 us
    all_to_all x1, waiting for transfers between devices, on_device(): lax.all_to_all(stacked, 'outer', split_axis=1, concat_axis=1, tiled=True)  30.3 us
    all_to_all x1, waiting for transfers between devices, on_device(): lax.all_to_all(lax.all_to_all(packed, 'outer', split_axis=1, concat_axis=...  26.8 us
    all_to_all x1, waiting for transfers between devices, on_device(): lax.all_to_all(lax.all_to_all(stacked, 'outer', split_axis=1, concat_axis...  21.3 us
    all_to_all x1, blocking collectives, on_device(): lax.all_to_all(settled_in.reshape(home_shape), 'outer', split_axis=0, con...  20.7 us
    all_to_all x1, starting transfers between devices, on_device(): lax.all_to_all(filter_blocked, 'outer', split_axis=0, concat_axis=0, tile...  15.4 us
    all_to_all x1, blocking collectives, on_device(): lax.all_to_all(lax.all_to_all(settled_in.reshape(home_shape), 'outer', sp...  13.3 us
    dot_general x12, matrix products, apply_table(): jnp.einsum(form, cos_table, imag_part, precision=highest)  11.2 us
  transfers between devices with their start and end apart: 10, of which 8 were waited for; matrix products, arithmetic and copies ran while one was open for 9% of the time, Pallas kernels for 0%

commit v1 on v0

v1 whole, which is shorter than its diff:
```python
import numpy as np

import jax
import jax.numpy as jnp
from jax import lax
from jax.experimental import pallas as pl
from jax.experimental.pallas import tpu as pltpu
from jax.sharding import PartitionSpec as P

LANE = 128
highest = lax.Precision.HIGHEST


def unit(phase):
    turn = 2.0 * np.pi * np.asarray(phase, np.float64)
    return np.cos(turn), np.sin(turn)


def tables(outer, inner, seg):
    span = inner * seg
    high = seg // LANE
    lines = span // LANE
    theta = (np.arange(outer) + 0.25) / outer
    place = np.arange(outer)[None, None, :] + np.arange(inner)[:, None, None] / inner
    cos, sin = unit(theta[None, :, None] * place)
    gather = np.concatenate([cos, sin], axis=1)
    spread = np.concatenate([cos, sin], axis=1).transpose(0, 2, 1) / (outer * span)
    cos, sin = unit(theta[:, None] * np.arange(seg)[None, :] / span)
    edge = np.concatenate([cos, sin], axis=1)
    row = (np.arange(high)[:, None] + high * np.arange(inner)[None, :]).reshape(-1)
    cos, sin = unit(np.outer(np.arange(lines), row) % lines / lines)
    first = np.block([[cos, -sin], [sin, cos]])
    first_back = first.T
    cos, sin = unit(np.outer(np.arange(lines), np.arange(LANE)) / span)
    turn = np.concatenate([cos, sin], axis=1)
    cos, sin = unit(np.outer(np.arange(LANE), np.arange(LANE)) % LANE / LANE)
    second = np.block([[cos, sin], [-sin, cos]])
    second_back = second.T
    named = (gather, spread, edge, first, first_back, turn, second, second_back)
    return tuple(item.astype(np.float32) for item in named)


def dot(left, right):
    return jnp.dot(left, right, precision=highest, preferred_element_type=jnp.float32)


def short_filter(projected_ref, earlier_ref, taps_ref, ext_ref):
    seg = projected_ref.shape[0]
    ext_ref[0:8, :] = earlier_ref[...].astype(jnp.float32)
    ext_ref[8 : 8 + seg, :] = projected_ref[...].astype(jnp.float32)
    total = taps_ref[0:1, :] * ext_ref[8 : 8 + seg, :]
    for tap in range(1, taps_ref.shape[0]):
        total = total + taps_ref[tap : tap + 1, :] * ext_ref[8 - tap : 8 - tap + seg, :]
    return total


def mix_of(filtered):
    width = filtered.shape[1] // 3
    return (filtered[:, width : 2 * width] * filtered[:, 2 * width :]).astype(jnp.bfloat16)


def pack_kernel(projected_ref, earlier_ref, taps_ref, filter_ref, out_ref, ext_ref):
    outer = out_ref.shape[0]
    high = filter_ref.shape[0]
    groups = LANE // outer
    mixture = mix_of(short_filter(projected_ref, earlier_ref, taps_ref, ext_ref))
    mixture = mixture.astype(jnp.float32)
    for hi in range(high):
        flipped = mixture[hi * LANE : (hi + 1) * LANE, :].T.astype(jnp.bfloat16)
        for ch in range(groups):
            at = (hi * (groups + 1) + ch) * LANE
            out_ref[:, at : at + LANE] = flipped[ch * outer : (ch + 1) * outer, :]
        at = (hi * (groups + 1) + groups) * LANE
        taps = filter_ref[hi : hi + 1, :].astype(jnp.float32)
        out_ref[:, at : at + LANE] = jnp.broadcast_to(taps, (outer, LANE)).astype(jnp.bfloat16)


def gather_kernel(data_ref, gather_ref, edge_ref, out_ref):
    outer, width = data_ref.shape
    inner = out_ref.shape[0]
    seg = edge_ref.shape[1] // 2
    high = seg // LANE
    series = width // seg
    sums = dot(gather_ref[...], data_ref[...].astype(jnp.float32))
    half = out_ref.shape[1] // (outer // inner)
    for hi in range(high):
        cos = edge_ref[:, hi * LANE : (hi + 1) * LANE]
        sin = edge_ref[:, seg + hi * LANE : seg + (hi + 1) * LANE]
        for ch in range(series):
            at = (hi * series + ch) * LANE
            real = sums[:outer, at : at + LANE]
            imag = sums[outer:, at : at + LANE]
            turned = (real * cos - imag * sin, real * sin + imag * cos)
            for part in range(2):
                value = turned[part].astype(jnp.bfloat16)
                for kk in range(outer // inner):
                    to = kk * half + ((part * high + hi) * series + ch) * LANE
                    out_ref[:, to : to + LANE] = value[kk * inner : (kk + 1) * inner, :]


def wave_kernel(data_ref, first_ref, first_back_ref, turn_ref, second_ref, second_back_ref, out_ref, *, copies, high):
    inner = data_ref.shape[0]
    in_half = data_ref.shape[1] // copies
    out_half = out_ref.shape[1] // copies
    in_width = in_half // (2 * high)
    out_width = out_half // (2 * high)
    series = in_width // LANE
    lines = turn_ref.shape[0]
    cos = turn_ref[:, :LANE]
    sin = turn_ref[:, LANE:]
    for kk in range(copies):
        rows = [data_ref[:, kk * in_half + q * in_width : kk * in_half + (q + 1) * in_width] for q in range(2 * high)]
        block = jnp.concatenate(rows, axis=0).astype(jnp.float32)
        waves = dot(first_ref[...], block)
        stacked = []
        for ch in range(series):
            real = waves[:lines, ch * LANE : (ch + 1) * LANE]
            imag = waves[lines:, ch * LANE : (ch + 1) * LANE]
            stacked.append(jnp.concatenate([real * cos - imag * sin, real * sin + imag * cos], axis=1))
        freq = dot(jnp.concatenate(stacked, axis=0), second_ref[...])
        last = freq[(series - 1) * lines :, :]
        tap_real = last[:, :LANE]
        tap_imag = last[:, LANE:]
        products = []
        for ch in range(series - 1):
            real = freq[ch * lines : (ch + 1) * lines, :LANE]
            imag = freq[ch * lines : (ch + 1) * lines, LANE:]
            products.append(
                jnp.concatenate([real * tap_real - imag * tap_imag, real * tap_imag + imag * tap_real], axis=1)
            )
        back = dot(jnp.concatenate(products, axis=0), second_back_ref[...])
        columns = []
        for ch in range(series - 1):
            real = back[ch * lines : (ch + 1) * lines, :LANE]
            imag = back[ch * lines : (ch + 1) * lines, LANE:]
            columns.append(jnp.concatenate([real * cos + imag * sin, imag * cos - real * sin], axis=0))
        done = dot(first_back_ref[...], jnp.concatenate(columns, axis=1)).astype(jnp.bfloat16)
        for q in range(2 * high):
            at = kk * out_half + q * out_width
            out_ref[:, at : at + out_width] = done[q * inner : (q + 1) * inner, :]


def spread_kernel(data_ref, spread_ref, edge_ref, out_ref):
    inner = data_ref.shape[0]
    outer, width = out_ref.shape
    seg = edge_ref.shape[1] // 2
    high = seg // LANE
    line = width // high
    half = data_ref.shape[1] // (outer // inner)
    for hi in range(high):
        cos = edge_ref[:, hi * LANE : (hi + 1) * LANE]
        sin = edge_ref[:, seg + hi * LANE : seg + (hi + 1) * LANE]

        def piece(part):
            at = (part * high + hi) * line
            rows = [data_ref[:, kk * half + at : kk * half + at + line] for kk in range(outer // inner)]
            return jnp.concatenate(rows, axis=0).astype(jnp.float32)

        real, imag = piece(0), piece(1)
        turned = []
        for ch in range(line // LANE):
            re = real[:, ch * LANE : (ch + 1) * LANE]
            im = imag[:, ch * LANE : (ch + 1) * LANE]
            turned.append(jnp.concatenate([re * cos + im * sin, im * cos - re * sin], axis=0))
        value = dot(spread_ref[...], jnp.concatenate(turned, axis=1))
        out_ref[:, hi * line : (hi + 1) * line] = value.astype(jnp.bfloat16)


def gate_kernel(projected_ref, earlier_ref, taps_ref, gain_ref, data_ref, out_ref, ext_ref):
    outer, width = data_ref.shape
    channels = out_ref.shape[1]
    filtered = short_filter(projected_ref, earlier_ref, taps_ref, ext_ref)
    mixture = mix_of(filtered).astype(jnp.float32)
    queries = filtered[:, :channels]
    groups = channels // outer
    high = width // (groups * LANE)
    for hi in range(high):
        rows = [
            data_ref[:, (hi * groups + ch) * LANE : (hi * groups + ch + 1) * LANE].astype(jnp.float32)
            for ch in range(groups)
        ]
        convolved = jnp.concatenate(rows, axis=0).T
        span = slice(hi * LANE, (hi + 1) * LANE)
        out_ref[span, :] = queries[span, :] * (convolved + gain_ref[...] * mixture[span, :])


def exchange(value, axis, count):
    shaped = value.reshape(count, -1, LANE)
    moved = lax.all_to_all(shaped, axis, split_axis=0, concat_axis=0, tiled=True)
    return moved.reshape(value.shape)


def on_device(projected, short_taps, skip_gain, long_filter):
    seg, wide = projected.shape
    channels = skip_gain.shape[0]
    outer = lax.axis_size("outer")
    inner = lax.axis_size("inner")
    count = outer * inner
    groups = channels // outer
    high = seg // LANE
    copies = outer // inner
    gather, spread, edge, first, first_back, turn, second, second_back = tables(outer, inner, seg)
    column = lax.axis_index("inner")
    gather = lax.dynamic_index_in_dim(jnp.asarray(gather), column, 0, keepdims=False)
    spread = lax.dynamic_index_in_dim(jnp.asarray(spread), column, 0, keepdims=False)

    earlier = lax.ppermute(projected[seg - 8 :], ("outer", "inner"), [(s, s + 1) for s in range(count - 1)])
    ext = pltpu.VMEM((seg + 8, wide), jnp.float32)
    packed = pl.pallas_call(
        pack_kernel,
        out_shape=jax.ShapeDtypeStruct((outer, (groups + 1) * seg), jnp.bfloat16),
        scratch_shapes=[ext],
        name="pack",
    )(projected, earlier, short_taps, long_filter.reshape(high, LANE))
    arrived = exchange(packed, "outer", outer)
    summed = pl.pallas_call(
        gather_kernel,
        out_shape=jax.ShapeDtypeStruct((inner, copies * 2 * (groups + 1) * seg), jnp.bfloat16),
        name="gather",
    )(arrived, gather, edge)
    lined = exchange(summed, "inner", inner)
    waves = pl.pallas_call(
        lambda *refs: wave_kernel(*refs, copies=copies, high=high),
        out_shape=jax.ShapeDtypeStruct((inner, copies * 2 * groups * seg), jnp.bfloat16),
        name="wave",
    )(lined, first, first_back, turn, second, second_back)
    returned = exchange(waves, "inner", inner)
    settled = pl.pallas_call(
        spread_kernel,
        out_shape=jax.ShapeDtypeStruct((outer, groups * seg), jnp.bfloat16),
        name="spread",
    )(returned, spread, edge)
    home = exchange(settled, "outer", outer)
    return pl.pallas_call(
        gate_kernel,
        out_shape=jax.ShapeDtypeStruct((seg, channels), jnp.float32),
        scratch_shapes=[ext],
        name="gate",
    )(projected, earlier, short_taps, skip_gain.reshape(1, channels), home)


def solution(mesh):
    placed = (P(("outer", "inner"), None), P(), P(), P(("outer", "inner")))
    return jax.shard_map(
        on_device,
        mesh=mesh,
        in_specs=placed,
        out_specs=P(("outer", "inner"), None),
        check_vma=False,
    )
```

time: 334 us -> 113 us (0.34)
  the two profiles are of different devices: /device:TPU:8 before, /device:TPU:1 now
where the time goes in v1:
time: 113 us; the launch traced here: 112 us
  blocking collectives  33.6 us (30%)
  waiting for transfers between devices  27.6 us (24%)
  starting transfers between devices  24.4 us (22%)
  Pallas kernels  14 us (12%)
  local copies, waits for them, and re-layouts  12.4 us (11%)
    all_to_all x2, blocking collectives, exchange(): lax.all_to_all(shaped, axis, split_axis=0, concat_axis=0, tiled=True)  33.6 us
    all_to_all x2, waiting for transfers between devices, exchange(): lax.all_to_all(shaped, axis, split_axis=0, concat_axis=0, tiled=True)  19.9 us
    all_to_all x2, starting transfers between devices, exchange(): lax.all_to_all(shaped, axis, split_axis=0, concat_axis=0, tiled=True)  19.6 us
    ppermute x1, waiting for transfers between devices, on_device(): lax.ppermute(projected[seg - 8:], ('outer', 'inner'), [(s, s + 1) for s i...  7.67 us
    unnamed x9, local copies, waits for them, and re-layouts  7.28 us
    pallas_call x1, Pallas kernels, on_device(): pl.pallas_call(lambda *refs: wave_kernel(*refs, copies=copies, high=high)...  5.51 us
    ppermute x1, starting transfers between devices, on_device(): lax.ppermute(projected[seg - 8:], ('outer', 'inner'), [(s, s + 1) for s i...  4.81 us
    pallas_call x1, Pallas kernels, on_device(): pl.pallas_call(gather_kernel, out_shape=jax.ShapeDtypeStruct((inner, copi...  2.39 us
  transfers between devices with their start and end apart: 3, of which 3 were waited for; matrix products, arithmetic and copies ran while one was open for 2% of the time, Pallas kernels for 0%

profile of v1, /device:TPU:1, one launch (start us, length us, event | category | flops | bytes accessed | tf_op | source)
XLA Modules:
  0.0 112.1 jit_solution(10861524941941229347)
XLA Ops:
  0.0 0.7 slice.3
  0.7 4.8 %collective-permute-start = (bf16[8,384]{1,0:T(8,128)(2,1)S(1)}, bf16[8,384]{1,0:T(8,128)(2,1)S(1)}, u32[]{:S(2)}, u32[]{:S(2)}) collective-permute-start(bf16[8,384]{1,0:T(8,128)(2,1)S(1)} %slice.3), channel_id=1, source_target_pairs={{0,1},{1,2},{2,3},{3,4},{4,5},{5,6},{6,7},{7,8},{8,9},{9,10},{10,1... | collective-permute-start | bytes 18440 | tf_op jit(solution)/shard_map/ppermute | solution.py:207
  5.5 7.7 %collective-permute-done.earlier_ref = bf16[8,384]{1,0:T(8,128)(2,1)S(1)} collective-permute-done((bf16[8,384]{1,0:T(8,128)(2,1)S(1)}, bf16[8,384]{1,0:T(8,128)(2,1)S(1)}, u32[]{:S(2)}, u32[]{:S(2)}) %collective-permute-start) | collective-permute-done | bytes 6176 | tf_op jit(solution)/shard_map/ppermute | solution.py:207
  13.2 0.0 copy-start
  13.2 0.6 copy-done
  13.8 2.0 %pack.1 = bf16[32,2560]{1,0:T(8,128)(2,1)} custom-call(bf16[512,384]{1,0:T(8,128)(2,1)} %projected_ref.3, bf16[8,384]{1,0:T(8,128)(2,1)} %copy-done, f32[3,384]{1,0:T(4,128)} %taps_ref.3, bf16[4,128]{1,0:T(4,128)(2,1)} %bitcast.41), custom_call_target="tpu_custom_call" | custom-call | tf_op jit(solution)/shard_map/pack/pallas_call | solution.py:209
  15.7 1.7 %reshape.32 = bf16[32,20,128]{2,1,0:T(8,128)(2,1)} reshape(bf16[32,2560]{1,0:T(8,128)(2,1)} %pack.1) | data formatting | bytes 327680 | tf_op jit(solution)/shard_map/reshape | solution.py:188
  17.4 15.7 %all-to-all-start = ((bf16[32,20,128]{2,1,0:T(8,128)(2,1)}), bf16[32,20,128]{2,1,0:T(8,128)(2,1)S(1)}, u32[]{:S(2)}, u32[]{:S(2)}) async-start(bf16[32,20,128]{2,1,0:T(8,128)(2,1)} %reshape.32), calls=%async_computation | async-start | bytes 393216 | tf_op jit(solution)/shard_map/all_to_all | solution.py:189
  33.1 1.4 %dynamic-slice_bitcast_fusion.gather_ref = f32[64,32]{1,0:T(8,128)} fusion(f32[16,64,32]{2,1,0:T(8,128)} %constant.30.clone, s32[]{:T(128)S(6)} %select_n.6), kind=kLoop, calls=%fused_computation.4 | loop fusion | bytes 16388 | tf_op jit(solution)/shard_map/jit(dynamic_index_in_dim)/squeeze | solution.py:204
  34.5 12.7 %all-to-all-done = bf16[32,20,128]{2,1,0:T(8,128)(2,1)S(1)} async-done(((bf16[32,20,128]{2,1,0:T(8,128)(2,1)}), bf16[32,20,128]{2,1,0:T(8,128)(2,1)S(1)}, u32[]{:S(2)}, u32[]{:S(2)}) %all-to-all-start) | async-done | bytes 163872 | tf_op jit(solution)/shard_map/all_to_all | solution.py:189
  47.1 0.7 copy.26
  47.8 2.4 %gather.1 = bf16[16,10240]{1,0:T(8,128)(2,1)} custom-call(bf16[32,2560]{1,0:T(8,128)(2,1)} %bitcast.36, f32[64,32]{1,0:T(8,128)} %dynamic-slice_bitcast_fusion.gather_ref, f32[32,1024]{1,0:T(8,128)} %constant.32.clone.edge_ref), custom_call_target="tpu_custom_call" | custom-call | tf_op jit(solution)/shard_map/gather/pallas_call | solution.py:216
  50.2 1.0 copy.14
  51.2 13.5 %all_to_all.20 = bf16[16,80,128]{2,1,0:T(8,128)(2,1)S(1)} all-to-all(bf16[16,80,128]{2,1,0:T(8,128)(2,1)S(1)} %bitcast.30), channel_id=1, replica_groups=mesh['outer'=32,'inner'=16] {'inner'}, dimensions={0} | all-to-all | bytes 655360 | tf_op jit(solution)/shard_map/all_to_all | solution.py:189
  64.7 0.8 copy.24
  65.5 5.5 %wave.1 = bf16[16,8192]{1,0:T(8,128)(2,1)} custom-call(bf16[16,10240]{1,0:T(8,128)(2,1)} %bitcast.28, f32[128,128]{1,0:T(8,128)} %constant.33.clone.refs_1_, f32[128,128]{1,0:T(8,128)} %constant.34.clone.refs_2_, f32[64,256]{1,0:T(8,128)} %constant.35.clone.refs_3_, f32[256,256]{1,0:T(8,128)} %constant.36.clone.refs_4_, f32[256,256]{1,0:T(8,128)} %constant.37.clone.refs_5_), custom_call_target="tpu_custom_call" | custom-call | tf_op jit(solution)/shard_map/wave/pallas_call | solution.py:222
  71.0 1.7 %copy.16 = bf16[2,8,64,128]{3,2,1,0:T(8,128)(2,1)} copy(bf16[2,8,64,128]{3,1,2,0:T(8,128)(2,1)} %bitcast.32) | data formatting | bytes 524288
  72.7 4.0 %all-to-all-start.2 = ((bf16[16,64,128]{2,1,0:T(8,128)(2,1)}), bf16[16,64,128]{2,1,0:T(8,128)(2,1)S(1)}, u32[]{:S(2)}, u32[]{:S(2)}) async-start(bf16[16,64,128]{2,1,0:T(8,128)(2,1)} %bitcast.11), calls=%async_computation.2 | async-start | bytes 524288 | tf_op jit(solution)/shard_map/all_to_all | solution.py:189
  76.7 1.3 %dynamic-slice_bitcast_fusion.1.spread_ref = f32[32,64]{1,0:T(8,128)} fusion(f32[16,32,64]{2,1,0:T(8,128)} %constant.31.clone, s32[]{:T(128)S(6)} %select_n.6), kind=kLoop, calls=%fused_computation.5 | loop fusion | bytes 16388 | tf_op jit(solution)/shard_map/jit(dynamic_index_in_dim)/squeeze | solution.py:205
  78.1 7.3 %all-to-all-done.2 = bf16[16,64,128]{2,1,0:T(8,128)(2,1)S(1)} async-done(((bf16[16,64,128]{2,1,0:T(8,128)(2,1)}), bf16[16,64,128]{2,1,0:T(8,128)(2,1)S(1)}, u32[]{:S(2)}, u32[]{:S(2)}) %all-to-all-start.2) | async-done | bytes 262176 | tf_op jit(solution)/shard_map/all_to_all | solution.py:189
  85.3 0.9 copy.25
  86.2 2.0 %spread.1 = bf16[32,2048]{1,0:T(8,128)(2,1)} custom-call(bf16[16,8192]{1,0:T(8,128)(2,1)} %bitcast.34, f32[32,64]{1,0:T(8,128)} %dynamic-slice_bitcast_fusion.1.spread_ref, f32[32,1024]{1,0:T(8,128)} %constant.32.clone.edge_ref), custom_call_target="tpu_custom_call" | custom-call | tf_op jit(solution)/shard_map/spread/pallas_call | solution.py:228
  88.3 0.9 copy.18
  89.2 20.1 %all_to_all.21 = bf16[32,16,128]{2,1,0:T(8,128)(2,1)S(1)} all-to-all(bf16[32,16,128]{2,1,0:T(8,128)(2,1)S(1)} %bitcast.37), channel_id=1, replica_groups=mesh['outer'=32,'inner'=16] {'outer'}, dimensions={0} | all-to-all | bytes 262144 | tf_op jit(solution)/shard_map/all_to_all | solution.py:189
  109.3 0.7 copy.27
  110.0 2.1 %gate.1 = f32[512,128]{1,0:T(8,128)} custom-call(bf16[512,384]{1,0:T(8,128)(2,1)} %projected_ref.3, bf16[8,384]{1,0:T(8,128)(2,1)} %copy-done, f32[3,384]{1,0:T(4,128)} %taps_ref.3, f32[1,128]{1,0:T(1,128)} %bitcast.42, bf16[32,2048]{1,0:T(8,128)(2,1)} %bitcast.40), custom_call_target="tpu_custom_call" | custom-call | tf_op jit(solution)/shard_map/gate/pallas_call | solution.py:234
Async XLA Ops:
  0.7 12.5 %collective-permute-start = (bf16[8,384]{1,0:T(8,128)(2,1)S(1)}, bf16[8,384]{1,0:T(8,128)(2,1)S(1)}, u32[]{:S(2)}, u32[]{:S(2)}) collective-permute-start(bf16[8,384]{1,0:T(8,128)(2,1)S(1)} %slice.3), channel_id=1, source_target_pairs={{0,1},{1,2},{2,3},{3,4},{4,5},{5,6},{6,7},{7,8},{8,9},{9,10},{10,1... | collective-permute-start | bytes 18440 | tf_op jit(solution)/shard_map/ppermute | solution.py:207
  13.2 0.6 copy-start
  17.4 29.7 %all-to-all-start = ((bf16[32,20,128]{2,1,0:T(8,128)(2,1)}), bf16[32,20,128]{2,1,0:T(8,128)(2,1)S(1)}, u32[]{:S(2)}, u32[]{:S(2)}) async-start(bf16[32,20,128]{2,1,0:T(8,128)(2,1)} %reshape.32), calls=%async_computation | async-start | bytes 393216 | tf_op jit(solution)/shard_map/all_to_all | solution.py:189
  72.7 12.6 %all-to-all-start.2 = ((bf16[16,64,128]{2,1,0:T(8,128)(2,1)}), bf16[16,64,128]{2,1,0:T(8,128)(2,1)S(1)}, u32[]{:S(2)}, u32[]{:S(2)}) async-start(bf16[16,64,128]{2,1,0:T(8,128)(2,1)} %bitcast.11), calls=%async_computation.2 | async-start | bytes 524288 | tf_op jit(solution)/shard_map/all_to_all | solution.py:189

commit v2 on v1

v2 whole, which is shorter than its diff:
```python
import numpy as np

import jax
import jax.numpy as jnp
from jax import lax
from jax.experimental import pallas as pl
from jax.experimental.pallas import tpu as pltpu
from jax.sharding import Mesh, PartitionSpec as P

LANE = 128
FIRST = ("zh", "x", "zl")
SECOND = ("y", "core")
EVERY = ("zh", "y", "core", "x", "zl")
SPLIT = (2, 8, 2, 4, 4)
ZH = 2
INNER = 16
SPAN = 8192
LINES = 64
HIGH = 4
SERIES = ((0, 0), (0, 1), (0, 2), (1, 0), (1, 1))


def turn_of(phase):
    turn = 2.0 * np.pi * np.asarray(phase, np.float64)
    return np.cos(turn), np.sin(turn)


def halves(table):
    table = np.asarray(table, np.float32)
    upper = table.astype(jnp.bfloat16)
    lower = (table - upper.astype(np.float32)).astype(jnp.bfloat16)
    return np.stack([upper, lower])


def tables():
    line = np.arange(LINES)
    cos, sin = turn_of(np.outer(line + 0.25, line) / LINES)
    same = np.eye(ZH)

    def forward(part):
        small = part.reshape(INNER, HIGH, INNER, HIGH)
        return np.einsum("jkir,zw,cd->cjzkwidr", small, same, np.eye(2)).reshape(2, 128, 256)

    first = np.stack([forward(cos), forward(sin)], axis=1).reshape(512, 256)

    def backward(part):
        small = part.reshape(INNER, HIGH, INNER, HIGH) / SPAN
        return np.einsum("jkir,zw,cd->wicrdjzk", small, same, np.eye(2)).reshape(256, 2, 128)

    first_back = np.stack([backward(cos), backward(sin)], axis=2).reshape(256, 512)
    cos, sin = turn_of(np.outer(line + 0.25, np.arange(LANE)) / SPAN)
    rows = (np.arange(INNER)[:, None, None] * HIGH + np.zeros((1, ZH, 1), int) + np.arange(HIGH)).reshape(-1)
    twist = np.concatenate([cos[rows], sin[rows]], axis=1).astype(np.float32)
    cos, sin = turn_of(np.outer(np.arange(LANE), np.arange(LANE)) / LANE)
    second = np.block([[cos, sin], [-sin, cos]])
    return halves(first), halves(first_back), twist, halves(second), halves(second.T)


def mxu(left, right):
    return jnp.dot(left, right, preferred_element_type=jnp.float32)


def cut(value):
    upper = value.astype(jnp.bfloat16)
    return upper, (value - upper.astype(jnp.float32)).astype(jnp.bfloat16)


def short_filter(projected_ref, earlier_ref, taps_ref, ext_ref):
    seg = projected_ref.shape[0]
    ext_ref[0:8, :] = earlier_ref[...].astype(jnp.float32)
    ext_ref[8 : 8 + seg, :] = projected_ref[...].astype(jnp.float32)
    total = taps_ref[0:1, :] * ext_ref[8 : 8 + seg, :]
    for tap in range(1, taps_ref.shape[0]):
        total = total + taps_ref[tap : tap + 1, :] * ext_ref[8 - tap : 8 - tap + seg, :]
    return total


def mix_of(filtered):
    width = filtered.shape[1] // 3
    return (filtered[:, width : 2 * width] * filtered[:, 2 * width :]).astype(jnp.bfloat16)


def pack_kernel(projected_ref, earlier_ref, taps_ref, filter_ref, out_ref, ext_ref, rows_ref):
    mixture = mix_of(short_filter(projected_ref, earlier_ref, taps_ref, ext_ref)).astype(jnp.float32)
    for hi in range(HIGH):
        flipped = mixture[hi * LANE : (hi + 1) * LANE, :].T
        for ch in range(4):
            chh, at = SERIES[ch]
            rows_ref[at, pl.ds(chh * 4 + hi, 32, stride=8), :] = flipped[ch * 32 : (ch + 1) * 32, :]
        taps = jnp.broadcast_to(filter_ref[hi : hi + 1, :].astype(jnp.float32), (32, LANE))
        rows_ref[1, pl.ds(4 + hi, 32, stride=8), :] = taps
        rows_ref[2, pl.ds(4 + hi, 32, stride=8), :] = jnp.zeros((32, LANE), jnp.float32)
    for at in range(3):
        out_ref[:, :, at * LANE : (at + 1) * LANE] = rows_ref[at].reshape(32, 8, LANE).astype(jnp.bfloat16)


def ahead_kernel(data_ref, first_ref, twist_ref, second_ref, out_ref):
    data = data_ref[...].astype(jnp.float32).reshape(256, 3 * LANE).astype(jnp.bfloat16)
    waves = mxu(first_ref[0], data) + mxu(first_ref[1], data)
    cos = twist_ref[:, :LANE]
    sin = twist_ref[:, LANE:]
    for number, (chh, at) in enumerate(SERIES):
        real = waves[chh * 256 : chh * 256 + 128, at * LANE : (at + 1) * LANE]
        imag = waves[chh * 256 + 128 : chh * 256 + 256, at * LANE : (at + 1) * LANE]
        turned = jnp.concatenate([real * cos - imag * sin, real * sin + imag * cos], axis=1)
        upper, lower = cut(turned)
        freq = mxu(upper, second_ref[0]) + (mxu(lower, second_ref[0]) + mxu(upper, second_ref[1]))
        out_ref[:, :, number * 256 : (number + 1) * 256] = freq.reshape(16, 8, 256).astype(jnp.bfloat16)


def blocks_kernel(data_ref, out_ref, wave_ref, tap_ref):
    low = lax.broadcasted_iota(jnp.int32, (8, LANE), 0) < 4

    def value(yc, number, part):
        at = number * 256 + part * LANE
        return data_ref[yc, :, at : at + LANE].astype(jnp.float32)

    def swap(item):
        return pltpu.roll(item, 4, 0)

    previous = None
    blocks = [None] * 32
    for yc in range(16):
        real, imag = value(yc, 4, 0), value(yc, 4, 1)
        real_swap, imag_swap = swap(real), swap(imag)
        blocks[yc] = (jnp.where(low, real, real_swap), jnp.where(low, imag, imag_swap))
        blocks[16 + yc] = (jnp.where(low, real_swap, real), jnp.where(low, imag_swap, imag))
    for gap in range(32):
        real, imag = blocks[gap]
        if gap:
            real, imag = real + previous[1], imag - previous[0]
        tap_ref[0, gap] = real
        tap_ref[1, gap] = imag
        previous = blocks[gap]
    for pair in range(2):
        for yc in range(16):
            for part in range(2):
                even, odd = value(yc, 2 * pair, part), value(yc, 2 * pair + 1, part)
                wave_ref[part, yc] = jnp.where(low, even, swap(odd))
                wave_ref[part, 16 + yc] = jnp.where(low, swap(even), odd)
        sums = [None] * 32
        for start in range(0, 32, 4):
            total = [[None, None] for _ in range(4)]
            for source in range(start + 4):
                real, imag = wave_ref[0, source], wave_ref[1, source]
                for step in range(4):
                    gap = start + step - source
                    if gap < 0:
                        continue
                    tap_real, tap_imag = tap_ref[0, gap], tap_ref[1, gap]
                    new_real = real * tap_real - imag * tap_imag
                    new_imag = real * tap_imag + imag * tap_real
                    if total[step][0] is None:
                        total[step] = [new_real, new_imag]
                    else:
                        total[step] = [total[step][0] + new_real, total[step][1] + new_imag]
            for step in range(4):
                sums[start + step] = total[step]
                for part in range(2):
                    block = start + step
                    yc = block % 16
                    if block >= 16:
                        first = sums[yc][part]
                        second = total[step][part]
                        for member, joined in enumerate(
                            (jnp.where(low, first, swap(second)), jnp.where(low, swap(first), second))
                        ):
                            at = (2 * pair + member) * 256 + part * LANE
                            out_ref[yc, :, at : at + LANE] = joined.astype(jnp.bfloat16)


def behind_kernel(data_ref, second_ref, twist_ref, first_ref, out_ref):
    cos = twist_ref[:, :LANE]
    sin = twist_ref[:, LANE:]
    stacks = [[], []]
    for ch in range(4):
        block = data_ref[:, :, ch * 256 : (ch + 1) * 256].astype(jnp.float32).reshape(128, 256).astype(jnp.bfloat16)
        lines = mxu(block, second_ref[0]) + mxu(block, second_ref[1])
        real = lines[:, :LANE]
        imag = lines[:, LANE:]
        turned = jnp.concatenate([real * cos + imag * sin, imag * cos - real * sin], axis=0)
        stacks[ch // 2].append(turned)
    upper, lower = cut(jnp.concatenate([jnp.concatenate(side, axis=1) for side in stacks], axis=0))
    value = mxu(first_ref[0], upper) + (mxu(first_ref[0], lower) + mxu(first_ref[1], upper))
    out_ref[...] = value.reshape(32, 8, 2 * LANE).astype(jnp.bfloat16)


def gate_kernel(projected_ref, earlier_ref, taps_ref, gain_ref, data_ref, out_ref, ext_ref, rows_ref):
    filtered = short_filter(projected_ref, earlier_ref, taps_ref, ext_ref)
    mixture = mix_of(filtered).astype(jnp.float32)
    for at in range(2):
        rows_ref[at] = data_ref[:, :, at * LANE : (at + 1) * LANE].astype(jnp.float32).reshape(256, LANE)
    for hi in range(HIGH):
        rows = [rows_ref[ch % 2, pl.ds(ch // 2 * 4 + hi, 32, stride=8), :] for ch in range(4)]
        convolved = jnp.concatenate(rows, axis=0).T
        span = slice(hi * LANE, (hi + 1) * LANE)
        out_ref[span, :] = filtered[span, :LANE] * (convolved + gain_ref[...] * mixture[span, :])


def exchange(value, axis):
    return lax.all_to_all(value, axis, split_axis=0, concat_axis=0, tiled=True)


def on_device(projected, short_taps, skip_gain, long_filter):
    seg, wide = projected.shape
    channels = skip_gain.shape[0]
    count = lax.axis_size(EVERY)
    first, first_back, twist, second, second_back = tables()
    earlier = lax.ppermute(projected[seg - 8 :], EVERY, [(s, s + 1) for s in range(count - 1)])
    ext = pltpu.VMEM((seg + 8, wide), jnp.float32)
    packed = pl.pallas_call(
        pack_kernel,
        out_shape=jax.ShapeDtypeStruct((32, 8, 3 * LANE), jnp.bfloat16),
        scratch_shapes=[ext, pltpu.VMEM((3, 256, LANE), jnp.float32)],
        name="pack",
    )(projected, earlier, short_taps, long_filter.reshape(HIGH, LANE))
    arrived = exchange(packed, FIRST)
    ahead = pl.pallas_call(
        ahead_kernel,
        out_shape=jax.ShapeDtypeStruct((16, 8, 5 * 256), jnp.bfloat16),
        name="ahead",
    )(arrived, first, twist, second)
    lined = exchange(ahead, SECOND)
    blocks = pl.pallas_call(
        blocks_kernel,
        out_shape=jax.ShapeDtypeStruct((16, 8, 4 * 256), jnp.bfloat16),
        scratch_shapes=[pltpu.VMEM((2, 32, 8, LANE), jnp.float32), pltpu.VMEM((2, 32, 8, LANE), jnp.float32)],
        name="blocks",
    )(lined)
    returned = exchange(blocks, SECOND)
    behind = pl.pallas_call(
        behind_kernel,
        out_shape=jax.ShapeDtypeStruct((32, 8, 2 * LANE), jnp.bfloat16),
        name="behind",
    )(returned, second_back, twist, first_back)
    home = exchange(behind, FIRST)
    return pl.pallas_call(
        gate_kernel,
        out_shape=jax.ShapeDtypeStruct((seg, channels), jnp.float32),
        scratch_shapes=[ext, pltpu.VMEM((2, 256, LANE), jnp.float32)],
        name="gate",
    )(projected, earlier, short_taps, skip_gain.reshape(1, channels), home)


def solution(mesh):
    fine = Mesh(mesh.devices.reshape(SPLIT), EVERY)
    placed = (P(EVERY, None), P(), P(), P(EVERY))
    return jax.shard_map(on_device, mesh=fine, in_specs=placed, out_specs=P(EVERY, None), check_vma=False)
```

time: 113 us -> 99.4 us (0.88)
  blocking collectives: 33.6 us -> 72.7 us
  waiting for transfers between devices: 27.6 us -> 7.67 us
  starting transfers between devices: 24.4 us -> 4.81 us
  local copies, waits for them, and re-layouts: 12.4 us -> 1.27 us
  Pallas kernels: 14 us -> 12.4 us
    all_to_all x2 -> x4, blocking collectives: 33.6 us -> 72.7 us  [exchange(): return lax.all_to_all(value, axis, split_axis=0, concat_axis=0, tiled=True)]
    all_to_all x2 -> x0, waiting for transfers between devices: 19.9 us -> none  [exchange(): lax.all_to_all(shaped, axis, split_axis=0, concat_axis=0, tiled=True)]
    all_to_all x2 -> x0, starting transfers between devices: 19.6 us -> none  [exchange(): lax.all_to_all(shaped, axis, split_axis=0, concat_axis=0, tiled=True)]
    unnamed x9 -> x2, local copies, waits for them, and re-layouts: 7.28 us -> 0.58 us
    squeeze x2 -> x0, local copies, waits for them, and re-layouts: 2.7 us -> none  [the longest x1 1.37 us: on_device(): lax.dynamic_index_in_dim(jnp.asarray(gather), column, 0, keepdims=False)]
    reshape x1 -> x0, local copies, waits for them, and re-layouts: 1.7 us -> none  [exchange(): shaped = value.reshape(count, -1, LANE)]
    pallas_call x4, Pallas kernels: 11.9 us -> 10.2 us  [the longest x1 2.96 us: on_device(): pl.pallas_call(blocks_kernel, out_shape=jax.ShapeDtypeStruct((16, 8, 4 *...]
  transfers between devices with their start and end apart: 3 -> 1, of which waited for: 3 -> 1; matrix products, arithmetic and copies ran while one was open for 2% -> 0% of each run, Pallas kernels for 0% -> 0%
where the time goes in v2:
time: 99.4 us; the launch traced here: 98.8 us
  blocking collectives  72.7 us (73%)
  Pallas kernels  12.4 us (12%)
  waiting for transfers between devices  7.67 us (8%)
  starting transfers between devices  4.81 us (5%)
  local copies, waits for them, and re-layouts  1.27 us (1%)
    all_to_all x4, blocking collectives, exchange(): return lax.all_to_all(value, axis, split_axis=0, concat_axis=0, tiled=True)  72.7 us
    ppermute x1, waiting for transfers between devices, on_device(): lax.ppermute(projected[seg - 8:], EVERY, [(s, s + 1) for s in range(count...  7.67 us
    ppermute x1, starting transfers between devices, on_device(): lax.ppermute(projected[seg - 8:], EVERY, [(s, s + 1) for s in range(count...  4.81 us
    pallas_call x1, Pallas kernels, on_device(): pl.pallas_call(blocks_kernel, out_shape=jax.ShapeDtypeStruct((16, 8, 4 *...  2.96 us
    pallas_call x1, Pallas kernels, on_device(): pl.pallas_call(ahead_kernel, out_shape=jax.ShapeDtypeStruct((16, 8, 5 * 2...  2.68 us
    pallas_call x1, Pallas kernels, on_device(): pl.pallas_call(behind_kernel, out_shape=jax.ShapeDtypeStruct((32, 8, 2 *...  2.56 us
    pallas_call x1, Pallas kernels, on_device(): pl.pallas_call(gate_kernel, out_shape=jax.ShapeDtypeStruct((seg, channels...  2.15 us
    pallas_call x1, Pallas kernels, on_device(): pl.pallas_call(pack_kernel, out_shape=jax.ShapeDtypeStruct((32, 8, 3 * LA...  2 us
  transfers between devices with their start and end apart: 1, of which 1 were waited for; matrix products, arithmetic and copies ran while one was open for 0% of the time, Pallas kernels for 0%

profile of v2, /device:TPU:1, one launch (start us, length us, event | category | flops | bytes accessed | tf_op | source)
XLA Modules:
  0.0 98.8 jit_solution(6969595635089820741)
XLA Ops:
  0.0 0.7 slice.3
  0.7 4.8 %collective-permute-start = (bf16[8,384]{1,0:T(8,128)(2,1)S(1)}, bf16[8,384]{1,0:T(8,128)(2,1)S(1)}, u32[]{:S(2)}, u32[]{:S(2)}) collective-permute-start(bf16[8,384]{1,0:T(8,128)(2,1)S(1)} %slice.3), channel_id=1, source_target_pairs={{0,1},{1,2},{2,3},{3,4},{4,5},{5,6},{6,7},{7,8},{8,9},{9,10},{10,1... | collective-permute-start | bytes 18440 | tf_op jit(solution)/shard_map/ppermute | solution.py:209
  5.5 7.7 %collective-permute-done.earlier_ref = bf16[8,384]{1,0:T(8,128)(2,1)S(1)} collective-permute-done((bf16[8,384]{1,0:T(8,128)(2,1)S(1)}, bf16[8,384]{1,0:T(8,128)(2,1)S(1)}, u32[]{:S(2)}, u32[]{:S(2)}) %collective-permute-start) | collective-permute-done | bytes 6176 | tf_op jit(solution)/shard_map/ppermute | solution.py:209
  13.2 0.0 copy-start
  13.2 0.6 copy-done
  13.8 2.0 %pack.1 = bf16[32,8,384]{2,1,0:T(8,128)(2,1)} custom-call(bf16[512,384]{1,0:T(8,128)(2,1)} %projected_ref.3, bf16[8,384]{1,0:T(8,128)(2,1)} %copy-done, f32[3,384]{1,0:T(4,128)} %taps_ref.3, bf16[4,128]{1,0:T(4,128)(2,1)} %bitcast.2), custom_call_target="tpu_custom_call" | custom-call | tf_op jit(solution)/shard_map/pack/pallas_call | solution.py:211
  15.8 18.9 %all_to_all.20.data_ref = bf16[32,8,384]{2,1,0:T(8,128)(2,1)} all-to-all(bf16[32,8,384]{2,1,0:T(8,128)(2,1)} %pack.1), channel_id=1, replica_groups=mesh['zh'=2,'y'=8,'core'=2,'x'=4,'zl'=4] {'zh','x','zl'}, dimensions={0} | all-to-all | bytes 393216 | tf_op jit(solution)/shard_map/all_to_all | solution.py:201
  34.6 2.7 %ahead.1 = bf16[16,8,1280]{2,1,0:T(8,128)(2,1)} custom-call(bf16[32,8,384]{2,1,0:T(8,128)(2,1)} %all_to_all.20.data_ref, bf16[2,512,256]{2,1,0:T(8,128)(2,1)} %constant.10.clone.first_ref, f32[128,256]{1,0:T(8,128)} %constant.11.clone.twist_ref, bf16[2,256,256]{2,1,0:T(8,128)(2,1)} %constant.12.clone.second_ref), custom_call_target="tpu_custom_call" | custom-call | tf_op jit(solution)/shard_map/ahead/pallas_call | solution.py:218
  37.3 23.6 %all_to_all.21.data_ref = bf16[16,8,1280]{2,1,0:T(8,128)(2,1)} all-to-all(bf16[16,8,1280]{2,1,0:T(8,128)(2,1)} %ahead.1), channel_id=1, replica_groups=mesh['zh'=2,'y'=8,'core'=2,'x'=4,'zl'=4] {'y','core'}, dimensions={0} | all-to-all | bytes 655360 | tf_op jit(solution)/shard_map/all_to_all | solution.py:201
  60.9 3.0 %blocks.1 = bf16[16,8,1024]{2,1,0:T(8,128)(2,1)} custom-call(bf16[16,8,1280]{2,1,0:T(8,128)(2,1)} %all_to_all.21.data_ref), custom_call_target="tpu_custom_call" | custom-call | tf_op jit(solution)/shard_map/blocks/pallas_call | solution.py:224
  63.8 15.2 %all_to_all.22.data_ref = bf16[16,8,1024]{2,1,0:T(8,128)(2,1)} all-to-all(bf16[16,8,1024]{2,1,0:T(8,128)(2,1)} %blocks.1), channel_id=1, replica_groups=mesh['zh'=2,'y'=8,'core'=2,'x'=4,'zl'=4] {'y','core'}, dimensions={0} | all-to-all | bytes 524288 | tf_op jit(solution)/shard_map/all_to_all | solution.py:201
  79.0 2.6 %behind.1 = bf16[32,8,256]{2,1,0:T(8,128)(2,1)} custom-call(bf16[16,8,1024]{2,1,0:T(8,128)(2,1)} %all_to_all.22.data_ref, bf16[2,256,256]{2,1,0:T(8,128)(2,1)} %constant.13.clone.second_ref, f32[128,256]{1,0:T(8,128)} %constant.11.clone.twist_ref, bf16[2,256,512]{2,1,0:T(8,128)(2,1)} %constant.14.clone.first_ref), custom_call_target="tpu_custom_call" | custom-call | tf_op jit(solution)/shard_map/behind/pallas_call | solution.py:231
  81.6 15.1 %all_to_all.23.data_ref = bf16[32,8,256]{2,1,0:T(8,128)(2,1)} all-to-all(bf16[32,8,256]{2,1,0:T(8,128)(2,1)} %behind.1), channel_id=1, replica_groups=mesh['zh'=2,'y'=8,'core'=2,'x'=4,'zl'=4] {'zh','x','zl'}, dimensions={0} | all-to-all | bytes 262144 | tf_op jit(solution)/shard_map/all_to_all | solution.py:201
  96.6 2.2 %gate.1 = f32[512,128]{1,0:T(8,128)} custom-call(bf16[512,384]{1,0:T(8,128)(2,1)} %projected_ref.3, bf16[8,384]{1,0:T(8,128)(2,1)} %copy-done, f32[3,384]{1,0:T(4,128)} %taps_ref.3, f32[1,128]{1,0:T(1,128)} %bitcast.3, bf16[32,8,256]{2,1,0:T(8,128)(2,1)} %all_to_all.23.data_ref), custom_call_target="tpu_custom_call" | custom-call | tf_op jit(solution)/shard_map/gate/pallas_call | solution.py:237
Async XLA Ops:
  0.7 12.5 %collective-permute-start = (bf16[8,384]{1,0:T(8,128)(2,1)S(1)}, bf16[8,384]{1,0:T(8,128)(2,1)S(1)}, u32[]{:S(2)}, u32[]{:S(2)}) collective-permute-start(bf16[8,384]{1,0:T(8,128)(2,1)S(1)} %slice.3), channel_id=1, source_target_pairs={{0,1},{1,2},{2,3},{3,4},{4,5},{5,6},{6,7},{7,8},{8,9},{9,10},{10,1... | collective-permute-start | bytes 18440 | tf_op jit(solution)/shard_map/ppermute | solution.py:209
  13.2 0.6 copy-start

commit v3 on v2

--- a/solution.py
+++ b/solution.py
@@ -53,7 +53,9 @@
     twist = np.concatenate([cos[rows], sin[rows]], axis=1).astype(np.float32)
     cos, sin = turn_of(np.outer(np.arange(LANE), np.arange(LANE)) / LANE)
     second = np.block([[cos, sin], [-sin, cos]])
-    return halves(first), halves(first_back), twist, halves(second), halves(second.T)
+    ahead = halves(np.concatenate([first, second], axis=0))
+    behind = halves(np.concatenate([first_back, second.T], axis=1))
+    return ahead, behind, twist
 
 
 def mxu(left, right):
@@ -65,23 +67,32 @@
     return upper, (value - upper.astype(jnp.float32)).astype(jnp.bfloat16)
 
 
-def short_filter(projected_ref, earlier_ref, taps_ref, ext_ref):
-    seg = projected_ref.shape[0]
-    ext_ref[0:8, :] = earlier_ref[...].astype(jnp.float32)
-    ext_ref[8 : 8 + seg, :] = projected_ref[...].astype(jnp.float32)
-    total = taps_ref[0:1, :] * ext_ref[8 : 8 + seg, :]
-    for tap in range(1, taps_ref.shape[0]):
-        total = total + taps_ref[tap : tap + 1, :] * ext_ref[8 - tap : 8 - tap + seg, :]
+def short_filter(ext_ref, taps, seg):
+    total = taps[0:1, :] * ext_ref[8 : 8 + seg, :]
+    for tap in range(1, taps.shape[0]):
+        total = total + taps[tap : tap + 1, :] * ext_ref[8 - tap : 8 - tap + seg, :]
     return total
 
 
 def mix_of(filtered):
     width = filtered.shape[1] // 3
-    return (filtered[:, width : 2 * width] * filtered[:, 2 * width :]).astype(jnp.bfloat16)
-
-
-def pack_kernel(projected_ref, earlier_ref, taps_ref, filter_ref, out_ref, ext_ref, rows_ref):
-    mixture = mix_of(short_filter(projected_ref, earlier_ref, taps_ref, ext_ref)).astype(jnp.float32)
+    mixture = (filtered[:, width : 2 * width] * filtered[:, 2 * width :]).astype(jnp.bfloat16)
+    return mixture.astype(jnp.float32)
+
+
+def pack_kernel(
+    projected_ref, taps_ref, gain_ref, filter_ref, rows_ref, queries_ref, direct_ref, head_ref, ext_ref
+):
+    seg = projected_ref.shape[0]
+    ext_ref[0:8, :] = jnp.zeros((8, 3 * LANE), jnp.float32)
+    ext_ref[8 : 8 + seg, :] = projected_ref[...].astype(jnp.float32)
+    head_ref[0:8, :] = ext_ref[8:16, :]
+    head_ref[8:11, :] = taps_ref[...]
+    head_ref[16:17, 0:LANE] = gain_ref[...]
+    filtered = short_filter(ext_ref, taps_ref[...], seg)
+    mixture = mix_of(filtered)
+    queries_ref[...] = filtered[:, :LANE]
+    direct_ref[...] = gain_ref[...] * mixture
     for hi in range(HIGH):
         flipped = mixture[hi * LANE : (hi + 1) * LANE, :].T
         for ch in range(4):
@@ -90,11 +101,29 @@
         taps = jnp.broadcast_to(filter_ref[hi : hi + 1, :].astype(jnp.float32), (32, LANE))
         rows_ref[1, pl.ds(4 + hi, 32, stride=8), :] = taps
         rows_ref[2, pl.ds(4 + hi, 32, stride=8), :] = jnp.zeros((32, LANE), jnp.float32)
+
+
+def mend_kernel(rows_ref, head_ref, earlier_ref, out_ref, fixed_ref, ext_ref, block_ref):
+    ext_ref[0:8, :] = earlier_ref[...].astype(jnp.float32)
+    ext_ref[8:16, :] = head_ref[0:8, :]
+    filtered = short_filter(ext_ref, head_ref[8:11, :], 8)
+    mixture = mix_of(filtered)
+    fixed_ref[0:8, :] = filtered[:, :LANE]
+    fixed_ref[8:16, :] = head_ref[16:17, 0:LANE] * mixture
+    block_ref[...] = rows_ref[...]
+    flipped = jnp.concatenate([mixture, jnp.zeros((LANE - 8, LANE), jnp.float32)], axis=0).T
+    fresh = lax.broadcasted_iota(jnp.int32, (32, LANE), 1) < 8
+    for ch in range(4):
+        chh, at = SERIES[ch]
+        where = pl.ds(chh * 4, 32, stride=8)
+        block_ref[at, where, :] = jnp.where(fresh, flipped[ch * 32 : (ch + 1) * 32, :], block_ref[at, where, :])
     for at in range(3):
-        out_ref[:, :, at * LANE : (at + 1) * LANE] = rows_ref[at].reshape(32, 8, LANE).astype(jnp.bfloat16)
-
-
-def ahead_kernel(data_ref, first_ref, twist_ref, second_ref, out_ref):
+        out_ref[:, :, at * LANE : (at + 1) * LANE] = block_ref[at].reshape(32, 8, LANE).astype(jnp.bfloat16)
+
+
+def ahead_kernel(data_ref, table_ref, twist_ref, out_ref):
+    first_ref = table_ref.at[:, :512, :]
+    second_ref = table_ref.at[:, 512:, :]
     data = data_ref[...].astype(jnp.float32).reshape(256, 3 * LANE).astype(jnp.bfloat16)
     waves = mxu(first_ref[0], data) + mxu(first_ref[1], data)
     cos = twist_ref[:, :LANE]
@@ -169,7 +198,9 @@
                             out_ref[yc, :, at : at + LANE] = joined.astype(jnp.bfloat16)
 
 
-def behind_kernel(data_ref, second_ref, twist_ref, first_ref, out_ref):
+def behind_kernel(data_ref, table_ref, twist_ref, out_ref):
+    first_ref = table_ref.at[:, :, :512]
+    second_ref = table_ref.at[:, :, 512:]
     cos = twist_ref[:, :LANE]
     sin = twist_ref[:, LANE:]
     stacks = [[], []]
@@ -185,61 +216,78 @@
     out_ref[...] = value.reshape(32, 8, 2 * LANE).astype(jnp.bfloat16)
 
 
-def gate_kernel(projected_ref, earlier_ref, taps_ref, gain_ref, data_ref, out_ref, ext_ref, rows_ref):
-    filtered = short_filter(projected_ref, earlier_ref, taps_ref, ext_ref)
-    mixture = mix_of(filtered).astype(jnp.float32)
+def gate_kernel(queries_ref, direct_ref, fixed_ref, data_ref, out_ref, rows_ref):
     for at in range(2):
         rows_ref[at] = data_ref[:, :, at * LANE : (at + 1) * LANE].astype(jnp.float32).reshape(256, LANE)
     for hi in range(HIGH):
         rows = [rows_ref[ch % 2, pl.ds(ch // 2 * 4 + hi, 32, stride=8), :] for ch in range(4)]
         convolved = jnp.concatenate(rows, axis=0).T
         span = slice(hi * LANE, (hi + 1) * LANE)
-        out_ref[span, :] = filtered[span, :LANE] * (convolved + gain_ref[...] * mixture[span, :])
+        out_ref[span, :] = queries_ref[span, :] * (convolved + direct_ref[span, :])
+        if hi == 0:
+            out_ref[0:8, :] = fixed_ref[0:8, :] * (convolved[0:8, :] + fixed_ref[8:16, :])
 
 
 def exchange(value, axis):
     return lax.all_to_all(value, axis, split_axis=0, concat_axis=0, tiled=True)
+
+
+def on_chip(kernel, outs, scratch, name, *args):
+    near = pl.BlockSpec(memory_space=pltpu.VMEM)
+    return pl.pallas_call(
+        kernel,
+        in_specs=[near] * len(args),
+        out_specs=tuple(near for _ in outs) if len(outs) > 1 else near,
+        out_shape=outs if len(outs) > 1 else outs[0],
+        scratch_shapes=scratch,
+        name=name,
+    )(*[pltpu.with_memory_space_constraint(arg, pltpu.VMEM) for arg in args])
 
 
 def on_device(projected, short_taps, skip_gain, long_filter):
     seg, wide = projected.shape
     channels = skip_gain.shape[0]
     count = lax.axis_size(EVERY)
-    first, first_back, twist, second, second_back = tables()
+    near = pl.BlockSpec(memory_space=pltpu.VMEM)
+    ahead_table, behind_table, twist = tables()
     earlier = lax.ppermute(projected[seg - 8 :], EVERY, [(s, s + 1) for s in range(count - 1)])
-    ext = pltpu.VMEM((seg + 8, wide), jnp.float32)
-    packed = pl.pallas_call(
+    plane = pltpu.VMEM((seg, channels), jnp.float32)
+    stack = pltpu.VMEM((3, 256, LANE), jnp.float32)
+    rows, queries, direct, head = pl.pallas_call(
         pack_kernel,
-        out_shape=jax.ShapeDtypeStruct((32, 8, 3 * LANE), jnp.bfloat16),
-        scratch_shapes=[ext, pltpu.VMEM((3, 256, LANE), jnp.float32)],
+        out_specs=(near, near, near, near),
+        out_shape=(stack, plane, plane, pltpu.VMEM((24, wide), jnp.float32)),
+        scratch_shapes=[pltpu.VMEM((seg + 8, wide), jnp.float32)],
         name="pack",
-    )(projected, earlier, short_taps, long_filter.reshape(HIGH, LANE))
+    )(projected, short_taps, skip_gain.reshape(1, channels), long_filter.reshape(HIGH, LANE))
+    packed, fixed = on_chip(
+        mend_kernel,
+        (pltpu.VMEM((32, 8, 3 * LANE), jnp.bfloat16), pltpu.VMEM((16, channels), jnp.float32)),
+        [pltpu.VMEM((16, wide), jnp.float32), stack],
+        "mend",
+        rows,
+        head,
+        earlier,
+    )
     arrived = exchange(packed, FIRST)
-    ahead = pl.pallas_call(
-        ahead_kernel,
-        out_shape=jax.ShapeDtypeStruct((16, 8, 5 * 256), jnp.bfloat16),
-        name="ahead",
-    )(arrived, first, twist, second)
+    ahead = on_chip(
+        ahead_kernel, (pltpu.VMEM((16, 8, 5 * 256), jnp.bfloat16),), [], "ahead", arrived, ahead_table, twist
+    )
     lined = exchange(ahead, SECOND)
-    blocks = pl.pallas_call(
-        blocks_kernel,
-        out_shape=jax.ShapeDtypeStruct((16, 8, 4 * 256), jnp.bfloat16),
-        scratch_shapes=[pltpu.VMEM((2, 32, 8, LANE), jnp.float32), pltpu.VMEM((2, 32, 8, LANE), jnp.float32)],
-        name="blocks",
-    )(lined)
+    store = pltpu.VMEM((2, 32, 8, LANE), jnp.float32)
+    blocks = on_chip(blocks_kernel, (pltpu.VMEM((16, 8, 4 * 256), jnp.bfloat16),), [store, store], "blocks", lined)
     returned = exchange(blocks, SECOND)
-    behind = pl.pallas_call(
-        behind_kernel,
-        out_shape=jax.ShapeDtypeStruct((32, 8, 2 * LANE), jnp.bfloat16),
-        name="behind",
-    )(returned, second_back, twist, first_back)
+    behind = on_chip(
+        behind_kernel, (pltpu.VMEM((32, 8, 2 * LANE), jnp.bfloat16),), [], "behind", returned, behind_table, twist
+    )
     home = exchange(behind, FIRST)
     return pl.pallas_call(
         gate_kernel,
+        in_specs=[near] * 4,
         out_shape=jax.ShapeDtypeStruct((seg, channels), jnp.float32),
-        scratch_shapes=[ext, pltpu.VMEM((2, 256, LANE), jnp.float32)],
+        scratch_shapes=[pltpu.VMEM((2, 256, LANE), jnp.float32)],
         name="gate",
-    )(projected, earlier, short_taps, skip_gain.reshape(1, channels), home)
+    )(*[pltpu.with_memory_space_constraint(arg, pltpu.VMEM) for arg in (queries, direct, fixed, home)])
 
 
 def solution(mesh):

time: 99.4 us -> 87.5 us (0.88)
  Pallas kernels: 12.4 us -> 5.12 us
  blocking collectives: 72.7 us -> 70.2 us
  waiting for transfers between devices: 7.67 us -> 6.24 us
    pallas_call x5 -> x6, Pallas kernels: 12.4 us -> 5.12 us  [the longest x4 2.84 us: on_chip(): pl.pallas_call(kernel, in_specs=[near] * len(args), out_specs=tuple((near...]
    all_to_all x4, blocking collectives: 72.7 us -> 70.2 us  [exchange(): return lax.all_to_all(value, axis, split_axis=0, concat_axis=0, tiled=True)]
    ppermute x1, waiting for transfers between devices: 7.67 us -> 6.24 us  [on_device(): lax.ppermute(projected[seg - 8:], EVERY, [(s, s + 1) for s in range(count...]
  transfers between devices with their start and end apart: 1 -> 1, of which waited for: 1 -> 1; matrix products, arithmetic and copies ran while one was open for 0% -> 0% of each run, Pallas kernels for 0% -> 2%
where the time goes in v3:
time: 87.5 us; the launch traced here: 87.2 us
  blocking collectives  70.2 us (80%)
  waiting for transfers between devices  6.24 us (7%)
  Pallas kernels  5.12 us (6%)
  starting transfers between devices  4.81 us (5%)
    all_to_all x4, blocking collectives, exchange(): return lax.all_to_all(value, axis, split_axis=0, concat_axis=0, tiled=True)  70.2 us
    ppermute x1, waiting for transfers between devices, on_device(): lax.ppermute(projected[seg - 8:], EVERY, [(s, s + 1) for s in range(count...  6.24 us
    ppermute x1, starting transfers between devices, on_device(): lax.ppermute(projected[seg - 8:], EVERY, [(s, s + 1) for s in range(count...  4.81 us
    pallas_call x4, Pallas kernels, on_chip(): pl.pallas_call(kernel, in_specs=[near] * len(args), out_specs=tuple((near...  2.84 us
  transfers between devices with their start and end apart: 1, of which 1 were waited for; matrix products, arithmetic and copies ran while one was open for 0% of the time, Pallas kernels for 2%

profile of v3, /device:TPU:1, one launch (start us, length us, event | category | flops | bytes accessed | tf_op | source)
XLA Modules:
  0.0 87.2 jit_solution(9317407443609142922)
XLA Ops:
  0.0 0.0 copy-start.1
  0.0 0.8 slice.3
  0.8 4.8 %collective-permute-start = (bf16[8,384]{1,0:T(8,128)(2,1)S(1)}, bf16[8,384]{1,0:T(8,128)(2,1)S(1)}, u32[]{:S(2)}, u32[]{:S(2)}) collective-permute-start(bf16[8,384]{1,0:T(8,128)(2,1)S(1)} %slice.3), channel_id=1, source_target_pairs={{0,1},{1,2},{2,3},{3,4},{4,5},{5,6},{6,7},{7,8},{8,9},{9,10},{10,1... | collective-permute-start | bytes 18440 | tf_op jit(solution)/shard_map/ppermute | solution.py:253
  5.6 1.4 %pack.1 = (f32[3,256,128]{2,1,0:T(8,128)S(1)}, f32[512,128]{1,0:T(8,128)S(1)}, f32[512,128]{1,0:T(8,128)S(1)}, f32[24,384]{1,0:T(8,128)S(1)}) custom-call(bf16[512,384]{1,0:T(8,128)(2,1)} %projected_ref.1, f32[3,384]{1,0:T(4,128)} %taps_ref.1, f32[1,128]{1,0:T(1,128)} %bitcast.3, bf16[4,128]{1,0:T(4,128)(2,1)} %bitcast.2), custom_call_target="tpu_custom_call" | custom-call | tf_op jit(solution)/shard_map/pack/pallas_call | solution.py:256
  7.0 6.2 %collective-permute-done.earlier_ref = bf16[8,384]{1,0:T(8,128)(2,1)S(1)} collective-permute-done((bf16[8,384]{1,0:T(8,128)(2,1)S(1)}, bf16[8,384]{1,0:T(8,128)(2,1)S(1)}, u32[]{:S(2)}, u32[]{:S(2)}) %collective-permute-start) | collective-permute-done | bytes 6176 | tf_op jit(solution)/shard_map/ppermute | solution.py:253
  13.3 0.1 mend.1
  13.4 0.0 copy-start.2
  13.4 18.7 %all_to_all.20.data_ref = bf16[32,8,384]{2,1,0:T(8,128)(2,1)S(1)} all-to-all(bf16[32,8,384]{2,1,0:T(8,128)(2,1)S(1)} %get-tuple-element.16), channel_id=1, replica_groups=mesh['zh'=2,'y'=8,'core'=2,'x'=4,'zl'=4] {'zh','x','zl'}, dimensions={0} | all-to-all | bytes 393216 | tf_op jit(solution)/shard_map/all_to_all | solution.py:232
  32.1 0.0 copy-done.1
  32.1 0.0 copy-done.2
  32.1 0.7 ahead.1
  32.9 0.0 copy-start
  32.9 23.4 %all_to_all.21.data_ref = bf16[16,8,1280]{2,1,0:T(8,128)(2,1)S(1)} all-to-all(bf16[16,8,1280]{2,1,0:T(8,128)(2,1)S(1)} %ahead.1), channel_id=1, replica_groups=mesh['zh'=2,'y'=8,'core'=2,'x'=4,'zl'=4] {'y','core'}, dimensions={0} | all-to-all | bytes 655360 | tf_op jit(solution)/shard_map/all_to_all | solution.py:232
  56.3 1.3 %blocks.1 = bf16[16,8,1024]{2,1,0:T(8,128)(2,1)S(1)} custom-call(bf16[16,8,1280]{2,1,0:T(8,128)(2,1)S(1)} %all_to_all.21.data_ref), custom_call_target="tpu_custom_call" | custom-call | tf_op jit(solution)/shard_map/blocks/pallas_call | solution.py:237
  57.6 14.4 %all_to_all.22.data_ref = bf16[16,8,1024]{2,1,0:T(8,128)(2,1)S(1)} all-to-all(bf16[16,8,1024]{2,1,0:T(8,128)(2,1)S(1)} %blocks.1), channel_id=1, replica_groups=mesh['zh'=2,'y'=8,'core'=2,'x'=4,'zl'=4] {'y','core'}, dimensions={0} | all-to-all | bytes 524288 | tf_op jit(solution)/shard_map/all_to_all | solution.py:232
  71.9 0.0 copy-done
  71.9 0.7 behind.1
  72.6 13.7 %all_to_all.23.data_ref = bf16[32,8,256]{2,1,0:T(8,128)(2,1)S(1)} all-to-all(bf16[32,8,256]{2,1,0:T(8,128)(2,1)S(1)} %behind.1), channel_id=1, replica_groups=mesh['zh'=2,'y'=8,'core'=2,'x'=4,'zl'=4] {'zh','x','zl'}, dimensions={0} | all-to-all | bytes 262144 | tf_op jit(solution)/shard_map/all_to_all | solution.py:232
  86.3 0.9 gate.1
Async XLA Ops:
  0.0 32.1 %copy-start.1 = (bf16[2,768,256]{2,1,0:T(8,128)(2,1)S(1)}, bf16[2,768,256]{2,1,0:T(8,128)(2,1)}, u32[]{:S(2)}) copy-start(bf16[2,768,256]{2,1,0:T(8,128)(2,1)} %constant.6.clone.table_ref) | copy-start | bytes 2359300
  0.8 12.5 %collective-permute-start = (bf16[8,384]{1,0:T(8,128)(2,1)S(1)}, bf16[8,384]{1,0:T(8,128)(2,1)S(1)}, u32[]{:S(2)}, u32[]{:S(2)}) collective-permute-start(bf16[8,384]{1,0:T(8,128)(2,1)S(1)} %slice.3), channel_id=1, source_target_pairs={{0,1},{1,2},{2,3},{3,4},{4,5},{5,6},{6,7},{7,8},{8,9},{9,10},{10,1... | collective-permute-start | bytes 18440 | tf_op jit(solution)/shard_map/ppermute | solution.py:253
  13.4 18.7 %copy-start.2 = (f32[128,256]{1,0:T(8,128)S(1)}, f32[128,256]{1,0:T(8,128)}, u32[]{:S(2)}) copy-start(f32[128,256]{1,0:T(8,128)} %constant.7.clone.twist_ref) | copy-start | bytes 393220
  32.9 39.1 %copy-start = (bf16[2,256,768]{2,1,0:T(8,128)(2,1)S(1)}, bf16[2,256,768]{2,1,0:T(8,128)(2,1)}, u32[]{:S(2)}) copy-start(bf16[2,256,768]{2,1,0:T(8,128)(2,1)} %constant.8.clone.table_ref) | copy-start | bytes 2359300

commit v4 on v3

v4 whole, which is shorter than its diff:
```python
import numpy as np

import jax
import jax.numpy as jnp
from jax import lax
from jax.experimental import pallas as pl
from jax.experimental.pallas import tpu as pltpu
from jax.sharding import Mesh, PartitionSpec as P

LANE = 128
FIRST = ("zh", "y", "zl")
SECOND = ("core", "x")
EVERY = ("zh", "y", "core", "x", "zl")
SPLIT = (2, 8, 2, 4, 4)
PEERS = 64
BLOCKS = 16
PLANES = 8
HIGH = 4
RUN = 4
SPAN = 2048
LINES = 16
KQ = 2
WAVES = 256


def turn_of(phase):
    turn = 2.0 * np.pi * np.asarray(phase, np.float64)
    return np.cos(turn), np.sin(turn)


def halves(table):
    table = np.asarray(table, np.float32)
    upper = table.astype(jnp.bfloat16)
    lower = (table - upper.astype(np.float32)).astype(jnp.bfloat16)
    return np.stack([upper, lower])


def tables():
    line = np.arange(LINES)
    same = np.eye(BLOCKS)
    cos, sin = turn_of(np.outer(line + 0.25, line) / LINES)

    def forward(part):
        small = part.reshape(PLANES, KQ, RUN, HIGH)
        return np.einsum("jkzr,bc->kjbczr", small, same).reshape(256, 256)

    def backward(part):
        small = part.reshape(PLANES, KQ, RUN, HIGH) / SPAN
        return np.einsum("jkzr,bc->rczkjb", small, same).reshape(256, 256)

    first = np.concatenate([forward(cos), forward(sin)], axis=0)
    first_back = np.concatenate([backward(cos), backward(sin)], axis=1)
    cos, sin = turn_of(np.outer(line + 0.25, np.arange(LANE)) / SPAN)
    rows = np.broadcast_to(line.reshape(PLANES, KQ).T[:, :, None], (KQ, PLANES, BLOCKS)).reshape(-1)
    twist = np.concatenate([cos[rows], sin[rows]], axis=1).astype(np.float32)
    cos, sin = turn_of(np.outer(np.arange(LANE), np.arange(LANE)) / LANE)
    second = np.block([[cos, sin], [-sin, cos]])
    block = (np.arange(BLOCKS)[None, :] * PLANES + np.arange(PLANES)[:, None]).reshape(-1)
    wave = np.arange(WAVES)
    cos, sin = turn_of(np.outer(wave, block) / WAVES)
    over = np.block([[cos, sin], [-sin, cos]])
    cos_before, sin_before = turn_of(np.outer(wave, block - 1) / WAVES)
    real = (cos + sin_before).T / WAVES
    imag = (sin - cos_before).T / WAVES
    under = np.block([[real, -imag], [imag, real]])
    ahead = halves(np.concatenate([first, second], axis=0))
    behind = halves(np.concatenate([first_back, second.T], axis=1))
    return ahead, behind, halves(over), halves(under), twist


def mxu(left, right):
    return jnp.dot(left, right, preferred_element_type=jnp.float32)


def cut(value):
    upper = value.astype(jnp.bfloat16)
    return upper, (value - upper.astype(jnp.float32)).astype(jnp.bfloat16)


def short_filter(ext_ref, taps, seg):
    total = taps[0:1, :] * ext_ref[8 : 8 + seg, :]
    for tap in range(1, taps.shape[0]):
        total = total + taps[tap : tap + 1, :] * ext_ref[8 - tap : 8 - tap + seg, :]
    return total


def mix_of(filtered):
    width = filtered.shape[1] // 3
    mixture = (filtered[:, width : 2 * width] * filtered[:, 2 * width :]).astype(jnp.bfloat16)
    return mixture.astype(jnp.float32)


def pack_kernel(
    projected_ref, taps_ref, gain_ref, filter_ref, rows_ref, queries_ref, direct_ref, head_ref, ext_ref
):
    seg = projected_ref.shape[0]
    ext_ref[0:8, :] = jnp.zeros((8, 3 * LANE), jnp.float32)
    ext_ref[8 : 8 + seg, :] = projected_ref[...].astype(jnp.float32)
    head_ref[0:8, :] = ext_ref[8:16, :]
    head_ref[8:11, :] = taps_ref[...]
    head_ref[16:17, 0:LANE] = gain_ref[...]
    filtered = short_filter(ext_ref, taps_ref[...], seg)
    mixture = mix_of(filtered)
    queries_ref[...] = filtered[:, :LANE]
    direct_ref[...] = gain_ref[...] * mixture
    for hi in range(HIGH):
        flipped = mixture[hi * LANE : (hi + 1) * LANE, :].T
        where = pl.ds(hi, PEERS, stride=HIGH)
        for ch in range(2):
            rows_ref[ch, where, :] = flipped[ch * PEERS : (ch + 1) * PEERS, :]
        taps = filter_ref[hi : hi + 1, :].astype(jnp.float32)
        rows_ref[2, where, :] = jnp.broadcast_to(taps, (PEERS, LANE))


def mend_kernel(rows_ref, head_ref, earlier_ref, out_ref, fixed_ref, ext_ref, block_ref):
    ext_ref[0:8, :] = earlier_ref[...].astype(jnp.float32)
    ext_ref[8:16, :] = head_ref[0:8, :]
    filtered = short_filter(ext_ref, head_ref[8:11, :], 8)
    mixture = mix_of(filtered)
    fixed_ref[0:8, :] = filtered[:, :LANE]
    fixed_ref[8:16, :] = head_ref[16:17, 0:LANE] * mixture
    block_ref[...] = rows_ref[...]
    flipped = jnp.concatenate([mixture, jnp.zeros((LANE - 8, LANE), jnp.float32)], axis=0).T
    fresh = lax.broadcasted_iota(jnp.int32, (PEERS, LANE), 1) < 8
    where = pl.ds(0, PEERS, stride=HIGH)
    for ch in range(2):
        block_ref[ch, where, :] = jnp.where(fresh, flipped[ch * PEERS : (ch + 1) * PEERS, :], block_ref[ch, where, :])
    for at in range(3):
        out_ref[:, :, at * LANE : (at + 1) * LANE] = block_ref[at].reshape(PEERS, HIGH, LANE).astype(jnp.bfloat16)


def ahead_kernel(data_ref, table_ref, twist_ref, out_ref):
    data = data_ref[...].astype(jnp.float32).reshape(256, 3 * LANE).astype(jnp.bfloat16)
    waves = mxu(table_ref[0, :512, :], data) + mxu(table_ref[1, :512, :], data)
    cos = twist_ref[:, :LANE]
    sin = twist_ref[:, LANE:]
    for number in range(3):
        real = waves[:256, number * LANE : (number + 1) * LANE]
        imag = waves[256:, number * LANE : (number + 1) * LANE]
        upper, lower = cut(jnp.concatenate([real * cos - imag * sin, real * sin + imag * cos], axis=1))
        second = table_ref[0, 512:, :]
        freq = mxu(upper, second) + (mxu(lower, second) + mxu(upper, table_ref[1, 512:, :]))
        for kq in range(KQ):
            at = (kq * 3 + number) * 256
            value = freq[kq * 128 : (kq + 1) * 128, :].reshape(PLANES, BLOCKS, 256)
            out_ref[:, :, at : at + 256] = value.astype(jnp.bfloat16)


def blocks_kernel(data_ref, over_ref, under_ref, out_ref):
    def piece(kq, number, part):
        at = ((kq * 3 + number) * 2 + part) * LANE
        return data_ref[:, :, at : at + LANE].astype(jnp.float32).reshape(128, LANE)

    columns = []
    for kq in range(KQ):
        for number in range(3):
            columns.append(jnp.concatenate([piece(kq, number, 0), piece(kq, number, 1)], axis=0))
    data = jnp.concatenate(columns, axis=1).astype(jnp.bfloat16)
    waves = mxu(over_ref[0], data) + mxu(over_ref[1], data)
    products = []
    for kq in range(KQ):
        at = (kq * 3 + 2) * LANE
        tap_real = waves[:WAVES, at : at + LANE]
        tap_imag = waves[WAVES:, at : at + LANE]
        for ch in range(2):
            at = (kq * 3 + ch) * LANE
            real = waves[:WAVES, at : at + LANE]
            imag = waves[WAVES:, at : at + LANE]
            both = [real * tap_real - imag * tap_imag, real * tap_imag + imag * tap_real]
            products.append(jnp.concatenate(both, axis=0))
    upper, lower = cut(jnp.concatenate(products, axis=1))
    sums = mxu(under_ref[0], upper) + (mxu(under_ref[0], lower) + mxu(under_ref[1], upper))
    for kq in range(KQ):
        for ch in range(2):
            for part in range(2):
                at = (kq * 2 + ch) * LANE
                value = sums[part * 128 : (part + 1) * 128, at : at + LANE].reshape(PLANES, BLOCKS, LANE)
                to = (at // LANE * 2 + part) * LANE
                out_ref[:, :, to : to + LANE] = value.astype(jnp.bfloat16)


def behind_kernel(data_ref, table_ref, twist_ref, out_ref, rows_ref):
    columns = []
    for ch in range(2):
        parts = [[], []]
        for kq in range(KQ):
            at = (kq * 2 + ch) * 256
            block = data_ref[:, :, at : at + 256].astype(jnp.float32).reshape(128, 256).astype(jnp.bfloat16)
            lines = mxu(block, table_ref[0, :, 512:]) + mxu(block, table_ref[1, :, 512:])
            cos = twist_ref[kq * 128 : (kq + 1) * 128, :LANE]
            sin = twist_ref[kq * 128 : (kq + 1) * 128, LANE:]
            real = lines[:, :LANE]
            imag = lines[:, LANE:]
            parts[0].append(real * cos + imag * sin)
            parts[1].append(imag * cos - real * sin)
        columns.append(jnp.concatenate(parts[0] + parts[1], axis=0))
    upper, lower = cut(jnp.concatenate(columns, axis=1))
    first = table_ref[0, :, :512]
    value = mxu(first, upper) + (mxu(first, lower) + mxu(table_ref[1, :, :512], upper))
    for hi in range(HIGH):
        for ch in range(2):
            where = pl.ds(ch * HIGH + hi, PEERS, stride=8)
            rows_ref[where, :] = value[hi * PEERS : (hi + 1) * PEERS, ch * LANE : (ch + 1) * LANE]
    out_ref[...] = rows_ref[...].reshape(PEERS, 8, LANE).astype(jnp.bfloat16)


def gate_kernel(queries_ref, direct_ref, fixed_ref, data_ref, out_ref, rows_ref):
    rows_ref[...] = data_ref[...].astype(jnp.float32).reshape(8 * PEERS, LANE)
    for hi in range(HIGH):
        rows = [rows_ref[pl.ds(ch * HIGH + hi, PEERS, stride=8), :] for ch in range(2)]
        convolved = jnp.concatenate(rows, axis=0).T
        span = slice(hi * LANE, (hi + 1) * LANE)
        out_ref[span, :] = queries_ref[span, :] * (convolved + direct_ref[span, :])
        if hi == 0:
            out_ref[0:8, :] = fixed_ref[0:8, :] * (convolved[0:8, :] + fixed_ref[8:16, :])


def exchange(value, axis):
    return lax.all_to_all(value, axis, split_axis=0, concat_axis=0, tiled=True)


def on_chip(kernel, outs, scratch, name, *args):
    near = pl.BlockSpec(memory_space=pltpu.VMEM)
    return pl.pallas_call(
        kernel,
        in_specs=[near] * len(args),
        out_specs=tuple(near for _ in outs) if len(outs) > 1 else near,
        out_shape=outs if len(outs) > 1 else outs[0],
        scratch_shapes=scratch,
        name=name,
    )(*[pltpu.with_memory_space_constraint(arg, pltpu.VMEM) for arg in args])


def on_device(projected, short_taps, skip_gain, long_filter):
    seg, wide = projected.shape
    channels = skip_gain.shape[0]
    count = lax.axis_size(EVERY)
    near = pl.BlockSpec(memory_space=pltpu.VMEM)
    ahead_table, behind_table, over, under, twist = tables()
    earlier = lax.ppermute(projected[seg - 8 :], EVERY, [(s, s + 1) for s in range(count - 1)])
    plane = pltpu.VMEM((seg, channels), jnp.float32)
    stack = pltpu.VMEM((3, 256, LANE), jnp.float32)
    rows, queries, direct, head = pl.pallas_call(
        pack_kernel,
        out_specs=(near, near, near, near),
        out_shape=(stack, plane, plane, pltpu.VMEM((24, wide), jnp.float32)),
        scratch_shapes=[pltpu.VMEM((seg + 8, wide), jnp.float32)],
        name="pack",
    )(projected, short_taps, skip_gain.reshape(1, channels), long_filter.reshape(HIGH, LANE))
    packed, fixed = on_chip(
        mend_kernel,
        (pltpu.VMEM((PEERS, HIGH, 3 * LANE), jnp.bfloat16), pltpu.VMEM((16, channels), jnp.float32)),
        [pltpu.VMEM((16, wide), jnp.float32), stack],
        "mend",
        rows,
        head,
        earlier,
    )
    arrived = exchange(packed, FIRST)
    ahead = on_chip(
        ahead_kernel,
        (pltpu.VMEM((PLANES, BLOCKS, KQ * 3 * 256), jnp.bfloat16),),
        [],
        "ahead",
        arrived,
        ahead_table,
        twist,
    )
    lined = exchange(ahead, SECOND)
    blocks = on_chip(
        blocks_kernel,
        (pltpu.VMEM((PLANES, BLOCKS, KQ * 2 * 256), jnp.bfloat16),),
        [],
        "blocks",
        lined,
        over,
        under,
    )
    returned = exchange(blocks, SECOND)
    behind = on_chip(
        behind_kernel,
        (pltpu.VMEM((PEERS, 8, LANE), jnp.bfloat16),),
        [pltpu.VMEM((8 * PEERS, LANE), jnp.float32)],
        "behind",
        returned,
        behind_table,
        twist,
    )
    home = exchange(behind, FIRST)
    return pl.pallas_call(
        gate_kernel,
        in_specs=[near] * 4,
        out_shape=jax.ShapeDtypeStruct((seg, channels), jnp.float32),
        scratch_shapes=[pltpu.VMEM((8 * PEERS, LANE), jnp.float32)],
        name="gate",
    )(*[pltpu.with_memory_space_constraint(arg, pltpu.VMEM) for arg in (queries, direct, fixed, home)])


def solution(mesh):
    fine = Mesh(mesh.devices.reshape(SPLIT), EVERY)
    placed = (P(EVERY, None), P(), P(), P(EVERY))
    return jax.shard_map(on_device, mesh=fine, in_specs=placed, out_specs=P(EVERY, None), check_vma=False)
```

time: 87.5 us -> 83.4 us (0.953)
  blocking collectives: 70.2 us -> 65.5 us
    all_to_all x4, blocking collectives: 70.2 us -> 65.5 us  [exchange(): return lax.all_to_all(value, axis, split_axis=0, concat_axis=0, tiled=True)]
where the time goes in v4:
time: 83.4 us; the launch traced here: 83.1 us
  blocking collectives  65.5 us (79%)
  waiting for transfers between devices  6.25 us (7%)
  Pallas kernels  5.73 us (7%)
  starting transfers between devices  4.81 us (6%)
    all_to_all x4, blocking collectives, exchange(): return lax.all_to_all(value, axis, split_axis=0, concat_axis=0, tiled=True)  65.5 us
    ppermute x1, waiting for transfers between devices, on_device(): lax.ppermute(projected[seg - 8:], EVERY, [(s, s + 1) for s in range(count...  6.25 us
    ppermute x1, starting transfers between devices, on_device(): lax.ppermute(projected[seg - 8:], EVERY, [(s, s + 1) for s in range(count...  4.81 us
    pallas_call x4, Pallas kernels, on_chip(): pl.pallas_call(kernel, in_specs=[near] * len(args), out_specs=tuple((near...  3.45 us
  transfers between devices with their start and end apart: 1, of which 1 were waited for; matrix products, arithmetic and copies ran while one was open for 0% of the time, Pallas kernels for 2%

profile of v4, /device:TPU:1, one launch (start us, length us, event | category | flops | bytes accessed | tf_op | source)
XLA Modules:
  0.0 83.1 jit_solution(6109324408537019282)
XLA Ops:
  0.0 0.0 copy-start.1
  0.0 0.8 slice.3
  0.8 4.8 %collective-permute-start = (bf16[8,384]{1,0:T(8,128)(2,1)S(1)}, bf16[8,384]{1,0:T(8,128)(2,1)S(1)}, u32[]{:S(2)}, u32[]{:S(2)}) collective-permute-start(bf16[8,384]{1,0:T(8,128)(2,1)S(1)} %slice.3), channel_id=1, source_target_pairs={{0,1},{1,2},{2,3},{3,4},{4,5},{5,6},{6,7},{7,8},{8,9},{9,10},{10,1... | collective-permute-start | bytes 18440 | tf_op jit(solution)/shard_map/ppermute | solution.py:240
  5.6 1.4 %pack.1 = (f32[3,256,128]{2,1,0:T(8,128)S(1)}, f32[512,128]{1,0:T(8,128)S(1)}, f32[512,128]{1,0:T(8,128)S(1)}, f32[24,384]{1,0:T(8,128)S(1)}) custom-call(bf16[512,384]{1,0:T(8,128)(2,1)} %projected_ref.1, f32[3,384]{1,0:T(4,128)} %taps_ref.1, f32[1,128]{1,0:T(1,128)} %bitcast.3, bf16[4,128]{1,0:T(4,128)(2,1)} %bitcast.2), custom_call_target="tpu_custom_call" | custom-call | tf_op jit(solution)/shard_map/pack/pallas_call | solution.py:243
  7.0 6.2 %collective-permute-done.earlier_ref = bf16[8,384]{1,0:T(8,128)(2,1)S(1)} collective-permute-done((bf16[8,384]{1,0:T(8,128)(2,1)S(1)}, bf16[8,384]{1,0:T(8,128)(2,1)S(1)}, u32[]{:S(2)}, u32[]{:S(2)}) %collective-permute-start) | collective-permute-done | bytes 6176 | tf_op jit(solution)/shard_map/ppermute | solution.py:240
  13.3 0.1 mend.1
  13.4 0.0 copy-start
  13.4 25.6 %all_to_all.20.data_ref = bf16[64,4,384]{2,1,0:T(4,128)(2,1)S(1)} all-to-all(bf16[64,4,384]{2,1,0:T(4,128)(2,1)S(1)} %get-tuple-element.16), channel_id=1, replica_groups=mesh['zh'=2,'y'=8,'core'=2,'x'=4,'zl'=4] {'zh','y','zl'}, dimensions={0} | all-to-all | bytes 393216 | tf_op jit(solution)/shard_map/all_to_all | solution.py:219
  39.0 0.0 copy-done.1
  39.0 0.0 copy-done
  39.0 0.0 copy-start.4
  39.0 0.8 %ahead.1 = bf16[8,16,1536]{2,1,0:T(8,128)(2,1)S(1)} custom-call(bf16[64,4,384]{2,1,0:T(4,128)(2,1)S(1)} %all_to_all.20.data_ref, bf16[2,768,256]{2,1,0:T(8,128)(2,1)S(1)} %copy-done.1, f32[256,256]{1,0:T(8,128)S(1)} %copy-done), custom_call_target="tpu_custom_call" | custom-call | tf_op jit(solution)/shard_map/ahead/pallas_call | solution.py:224
  39.9 0.0 copy-start.3
  39.9 14.7 %all_to_all.21.data_ref = bf16[8,16,1536]{2,1,0:T(8,128)(2,1)S(1)} all-to-all(bf16[8,16,1536]{2,1,0:T(8,128)(2,1)S(1)} %ahead.1), channel_id=1, replica_groups=mesh['zh'=2,'y'=8,'core'=2,'x'=4,'zl'=4] {'core','x'}, dimensions={0} | all-to-all | bytes 786432 | tf_op jit(solution)/shard_map/all_to_all | solution.py:219
  54.6 0.0 copy-done.4
  54.6 0.0 copy-done.3
  54.6 0.0 copy-start.2
  54.6 1.8 %blocks.1 = bf16[8,16,1024]{2,1,0:T(8,128)(2,1)S(1)} custom-call(bf16[8,16,1536]{2,1,0:T(8,128)(2,1)S(1)} %all_to_all.21.data_ref, bf16[2,512,256]{2,1,0:T(8,128)(2,1)S(1)} %copy-done.4, bf16[2,256,512]{2,1,0:T(8,128)(2,1)S(1)} %copy-done.3), custom_call_target="tpu_custom_call" | custom-call | tf_op jit(solution)/shard_map/blocks/pallas_call | solution.py:224
  56.3 9.7 %all_to_all.22.data_ref = bf16[8,16,1024]{2,1,0:T(8,128)(2,1)S(1)} all-to-all(bf16[8,16,1024]{2,1,0:T(8,128)(2,1)S(1)} %blocks.1), channel_id=1, replica_groups=mesh['zh'=2,'y'=8,'core'=2,'x'=4,'zl'=4] {'core','x'}, dimensions={0} | all-to-all | bytes 524288 | tf_op jit(solution)/shard_map/all_to_all | solution.py:219
  66.0 0.0 copy-done.2
  66.0 0.7 behind.1
  66.7 15.5 %all_to_all.23.data_ref = bf16[64,8,128]{2,1,0:T(8,128)(2,1)S(1)} all-to-all(bf16[64,8,128]{2,1,0:T(8,128)(2,1)S(1)} %behind.1), channel_id=1, replica_groups=mesh['zh'=2,'y'=8,'core'=2,'x'=4,'zl'=4] {'zh','y','zl'}, dimensions={0} | all-to-all | bytes 262144 | tf_op jit(solution)/shard_map/all_to_all | solution.py:219
  82.2 0.9 %gate.1 = f32[512,128]{1,0:T(8,128)} custom-call(f32[512,128]{1,0:T(8,128)S(1)} %get-tuple-element.11.queries_ref, f32[512,128]{1,0:T(8,128)S(1)} %get-tuple-element.12.direct_ref, f32[16,128]{1,0:T(8,128)S(1)} %get-tuple-element.15.fixed_ref, bf16[64,8,128]{2,1,0:T(8,128)(2,1)S(1)} %all_to_all.23.data_ref), custom_call_target="tpu_custom_call" | custom-call | tf_op jit(solution)/shard_map/gate/pallas_call | solution.py:290
Async XLA Ops:
  0.0 39.0 %copy-start.1 = (bf16[2,768,256]{2,1,0:T(8,128)(2,1)S(1)}, bf16[2,768,256]{2,1,0:T(8,128)(2,1)}, u32[]{:S(2)}) copy-start(bf16[2,768,256]{2,1,0:T(8,128)(2,1)} %constant.10.clone.table_ref) | copy-start | bytes 2359300
  0.8 12.5 %collective-permute-start = (bf16[8,384]{1,0:T(8,128)(2,1)S(1)}, bf16[8,384]{1,0:T(8,128)(2,1)S(1)}, u32[]{:S(2)}, u32[]{:S(2)}) collective-permute-start(bf16[8,384]{1,0:T(8,128)(2,1)S(1)} %slice.3), channel_id=1, source_target_pairs={{0,1},{1,2},{2,3},{3,4},{4,5},{5,6},{6,7},{7,8},{8,9},{9,10},{10,1... | collective-permute-start | bytes 18440 | tf_op jit(solution)/shard_map/ppermute | solution.py:240
  13.4 25.6 %copy-start = (f32[256,256]{1,0:T(8,128)S(1)}, f32[256,256]{1,0:T(8,128)}, u32[]{:S(2)}) copy-start(f32[256,256]{1,0:T(8,128)} %constant.11.clone.twist_ref) | copy-start | bytes 786436
  39.0 15.6 %copy-start.4 = (bf16[2,512,256]{2,1,0:T(8,128)(2,1)S(1)}, bf16[2,512,256]{2,1,0:T(8,128)(2,1)}, u32[]{:S(2)}) copy-start(bf16[2,512,256]{2,1,0:T(8,128)(2,1)} %constant.12.clone.over_ref) | copy-start | bytes 1572868
  39.9 14.7 %copy-start.3 = (bf16[2,256,512]{2,1,0:T(8,128)(2,1)S(1)}, bf16[2,256,512]{2,1,0:T(8,128)(2,1)}, u32[]{:S(2)}) copy-start(bf16[2,256,512]{2,1,0:T(8,128)(2,1)} %constant.13.clone.under_ref) | copy-start | bytes 1572868
  54.6 11.5 %copy-start.2 = (bf16[2,256,768]{2,1,0:T(8,128)(2,1)S(1)}, bf16[2,256,768]{2,1,0:T(8,128)(2,1)}, u32[]{:S(2)}) copy-start(bf16[2,256,768]{2,1,0:T(8,128)(2,1)} %constant.14.clone.table_ref) | copy-start | bytes 2359300

commit v5 on v4

--- a/solution.py
+++ b/solution.py
@@ -21,6 +21,7 @@
 LINES = 16
 KQ = 2
 WAVES = 256
+EDGE = ((0, 0), (1, 0), (0, 1), (1, 1), (2, 0), (3, 0), (2, 1), (3, 1))
 
 
 def turn_of(phase):
@@ -63,9 +64,12 @@
     real = (cos + sin_before).T / WAVES
     imag = (sin - cos_before).T / WAVES
     under = np.block([[real, -imag], [imag, real]])
+    spot = line.reshape(PLANES, KQ, 1) + LINES * np.arange(LANE) + 0.25
+    omega = np.stack(turn_of(spot / SPAN), axis=2).reshape(PLANES, 2 * KQ, LANE)
+    omega = np.concatenate([omega, np.zeros_like(omega)], axis=1).astype(np.float32)
     ahead = halves(np.concatenate([first, second], axis=0))
     behind = halves(np.concatenate([first_back, second.T], axis=1))
-    return ahead, behind, halves(over), halves(under), twist
+    return ahead, behind, halves(over), halves(under), twist, omega
 
 
 def mxu(left, right):
@@ -84,53 +88,78 @@
     return total
 
 
-def mix_of(filtered):
-    width = filtered.shape[1] // 3
-    mixture = (filtered[:, width : 2 * width] * filtered[:, 2 * width :]).astype(jnp.bfloat16)
-    return mixture.astype(jnp.float32)
-
-
-def pack_kernel(
-    projected_ref, taps_ref, gain_ref, filter_ref, rows_ref, queries_ref, direct_ref, head_ref, ext_ref
-):
+def pack_kernel(projected_ref, taps_ref, filter_ref, out_ref, ext_ref, rows_ref):
     seg = projected_ref.shape[0]
-    ext_ref[0:8, :] = jnp.zeros((8, 3 * LANE), jnp.float32)
-    ext_ref[8 : 8 + seg, :] = projected_ref[...].astype(jnp.float32)
-    head_ref[0:8, :] = ext_ref[8:16, :]
-    head_ref[8:11, :] = taps_ref[...]
-    head_ref[16:17, 0:LANE] = gain_ref[...]
-    filtered = short_filter(ext_ref, taps_ref[...], seg)
-    mixture = mix_of(filtered)
-    queries_ref[...] = filtered[:, :LANE]
-    direct_ref[...] = gain_ref[...] * mixture
+    ext_ref[0:8, :] = jnp.zeros((8, 2 * LANE), jnp.float32)
+    ext_ref[8 : 8 + seg, :] = projected_ref[:, LANE:].astype(jnp.float32)
+    taps = taps_ref[:, LANE:]
+    filtered = short_filter(ext_ref, taps, seg)
+    mixture = (filtered[:, :LANE] * filtered[:, LANE:]).astype(jnp.bfloat16).astype(jnp.float32)
+    last = ext_ref[7 + seg : 8 + seg, :]
+    carry = taps[1:2, :] * last + taps[2:3, :] * ext_ref[6 + seg : 7 + seg, :]
+    ends = [filtered[0:1, :], filtered[1:2, :], carry, taps[2:3, :] * last]
+    ends = [ends[row][:, half * LANE : (half + 1) * LANE] for row, half in EDGE]
+    upper, lower = cut(jnp.concatenate(ends, axis=0))
+    pad = jnp.zeros((LANE - 16, LANE), jnp.float32)
+    flipped = jnp.concatenate([upper.astype(jnp.float32), lower.astype(jnp.float32), pad], axis=0).T
+    lane = lax.broadcasted_iota(jnp.int32, (PEERS, LANE), 1)
+    edges = jnp.where(lane < 16, flipped[:PEERS, :], pltpu.roll(flipped[PEERS:, :], 16, 1))
     for hi in range(HIGH):
         flipped = mixture[hi * LANE : (hi + 1) * LANE, :].T
         where = pl.ds(hi, PEERS, stride=HIGH)
         for ch in range(2):
             rows_ref[ch, where, :] = flipped[ch * PEERS : (ch + 1) * PEERS, :]
-        taps = filter_ref[hi : hi + 1, :].astype(jnp.float32)
-        rows_ref[2, where, :] = jnp.broadcast_to(taps, (PEERS, LANE))
-
-
-def mend_kernel(rows_ref, head_ref, earlier_ref, out_ref, fixed_ref, ext_ref, block_ref):
+        taps_row = filter_ref[hi : hi + 1, :].astype(jnp.float32)
+        rows_ref[2, where, :] = jnp.broadcast_to(taps_row, (PEERS, LANE))
+        rows_ref[3, where, :] = edges
+    for at in range(4):
+        out_ref[:, :, at * LANE : (at + 1) * LANE] = rows_ref[at].reshape(PEERS, HIGH, LANE).astype(jnp.bfloat16)
+
+
+def plan_kernel(projected_ref, earlier_ref, taps_ref, gain_ref, queries_ref, direct_ref, ext_ref):
+    seg = projected_ref.shape[0]
     ext_ref[0:8, :] = earlier_ref[...].astype(jnp.float32)
-    ext_ref[8:16, :] = head_ref[0:8, :]
-    filtered = short_filter(ext_ref, head_ref[8:11, :], 8)
-    mixture = mix_of(filtered)
-    fixed_ref[0:8, :] = filtered[:, :LANE]
-    fixed_ref[8:16, :] = head_ref[16:17, 0:LANE] * mixture
-    block_ref[...] = rows_ref[...]
-    flipped = jnp.concatenate([mixture, jnp.zeros((LANE - 8, LANE), jnp.float32)], axis=0).T
-    fresh = lax.broadcasted_iota(jnp.int32, (PEERS, LANE), 1) < 8
+    ext_ref[8 : 8 + seg, :] = projected_ref[...].astype(jnp.float32)
+    filtered = short_filter(ext_ref, taps_ref[...], seg)
+    mixture = (filtered[:, LANE : 2 * LANE] * filtered[:, 2 * LANE :]).astype(jnp.bfloat16)
+    queries_ref[...] = filtered[:, :LANE]
+    direct_ref[...] = gain_ref[...] * mixture.astype(jnp.float32)
+
+
+def back(value, lanes):
+    return pltpu.roll(value, LANE - lanes, 1)
+
+
+def whole_edges(edges):
+    return edges + back(edges, 8)
+
+
+def rows_of(own, before):
+    total = own + before
+    return (total * back(total, 2)).astype(jnp.bfloat16).astype(jnp.float32)
+
+
+def ahead_kernel(data_ref, table_ref, twist_ref, out_ref, rows_ref, edge_ref):
+    for at in range(4):
+        block = data_ref[:, :, at * LANE : (at + 1) * LANE].astype(jnp.float32)
+        rows_ref[at] = block.reshape(256, LANE)
     where = pl.ds(0, PEERS, stride=HIGH)
+    edges = rows_ref[3, where, :]
+    edge_ref[...] = edges
+    own = whole_edges(edges)
+    mixture = rows_of(own, pltpu.roll(back(own, 4), 1, 0))
+    inside = (lax.broadcasted_iota(jnp.int32, (PEERS, LANE), 0) & (RUN - 1)) != 0
+    lane = lax.broadcasted_iota(jnp.int32, (PEERS, LANE), 1)
+    mixture = jnp.where(inside, mixture, 0.0)
     for ch in range(2):
-        block_ref[ch, where, :] = jnp.where(fresh, flipped[ch * PEERS : (ch + 1) * PEERS, :], block_ref[ch, where, :])
-    for at in range(3):
-        out_ref[:, :, at * LANE : (at + 1) * LANE] = block_ref[at].reshape(PEERS, HIGH, LANE).astype(jnp.bfloat16)
-
-
-def ahead_kernel(data_ref, table_ref, twist_ref, out_ref):
-    data = data_ref[...].astype(jnp.float32).reshape(256, 3 * LANE).astype(jnp.bfloat16)
+        fresh = back(mixture, 16 * ch) if ch else mixture
+        rows_ref[ch, where, :] = jnp.where(lane < 2, fresh, rows_ref[ch, where, :])
+    opening = edge_ref[pl.ds(0, BLOCKS, stride=RUN), :]
+    closing = edge_ref[pl.ds(RUN - 1, BLOCKS, stride=RUN), :]
+    outside = jnp.where((lane[:BLOCKS, :] & 4) == 0, opening, closing).astype(jnp.bfloat16)
+    for plane in range(PLANES):
+        out_ref[plane, :, KQ * 3 * 256 :] = outside
+    data = jnp.concatenate([rows_ref[0], rows_ref[1], rows_ref[2]], axis=1).astype(jnp.bfloat16)
     waves = mxu(table_ref[0, :512, :], data) + mxu(table_ref[1, :512, :], data)
     cos = twist_ref[:, :LANE]
     sin = twist_ref[:, LANE:]
@@ -146,17 +175,30 @@
             out_ref[:, :, at : at + 256] = value.astype(jnp.bfloat16)
 
 
-def blocks_kernel(data_ref, over_ref, under_ref, out_ref):
+def blocks_kernel(data_ref, over_ref, under_ref, omega_ref, out_ref):
+    omega = omega_ref[lax.axis_index(SECOND)]
+    owns = [whole_edges(data_ref[plane, :, KQ * 3 * 256 :].astype(jnp.float32)) for plane in range(PLANES)]
+    row = lax.broadcasted_iota(jnp.int32, (BLOCKS, LANE), 0)
+    wrapped = jnp.where(row == 0, 0.0, pltpu.roll(back(owns[PLANES - 1], 4), 1, 0))
+    befores = [wrapped] + [back(own, 4) for own in owns[:-1]]
+    opening = jnp.concatenate([rows_of(own, before) for own, before in zip(owns, befores)], axis=0)
+
     def piece(kq, number, part):
         at = ((kq * 3 + number) * 2 + part) * LANE
-        return data_ref[:, :, at : at + LANE].astype(jnp.float32).reshape(128, LANE)
+        value = data_ref[:, :, at : at + LANE].astype(jnp.float32).reshape(128, LANE)
+        if number == 2:
+            return value
+        second = opening[:, 16 * number + 1 : 16 * number + 2] * omega[2 * kq + part : 2 * kq + part + 1, :]
+        if part == 0:
+            second = second + opening[:, 16 * number : 16 * number + 1]
+        return value + second
 
     columns = []
     for kq in range(KQ):
         for number in range(3):
             columns.append(jnp.concatenate([piece(kq, number, 0), piece(kq, number, 1)], axis=0))
-    data = jnp.concatenate(columns, axis=1).astype(jnp.bfloat16)
-    waves = mxu(over_ref[0], data) + mxu(over_ref[1], data)
+    upper, lower = cut(jnp.concatenate(columns, axis=1))
+    waves = mxu(over_ref[0], upper) + (mxu(over_ref[0], lower) + mxu(over_ref[1], upper))
     products = []
     for kq in range(KQ):
         at = (kq * 3 + 2) * LANE
@@ -204,15 +246,13 @@
     out_ref[...] = rows_ref[...].reshape(PEERS, 8, LANE).astype(jnp.bfloat16)
 
 
-def gate_kernel(queries_ref, direct_ref, fixed_ref, data_ref, out_ref, rows_ref):
+def gate_kernel(queries_ref, direct_ref, data_ref, out_ref, rows_ref):
     rows_ref[...] = data_ref[...].astype(jnp.float32).reshape(8 * PEERS, LANE)
     for hi in range(HIGH):
         rows = [rows_ref[pl.ds(ch * HIGH + hi, PEERS, stride=8), :] for ch in range(2)]
         convolved = jnp.concatenate(rows, axis=0).T
         span = slice(hi * LANE, (hi + 1) * LANE)
         out_ref[span, :] = queries_ref[span, :] * (convolved + direct_ref[span, :])
-        if hi == 0:
-            out_ref[0:8, :] = fixed_ref[0:8, :] * (convolved[0:8, :] + fixed_ref[8:16, :])
 
 
 def exchange(value, axis):
@@ -236,31 +276,29 @@
     channels = skip_gain.shape[0]
     count = lax.axis_size(EVERY)
     near = pl.BlockSpec(memory_space=pltpu.VMEM)
-    ahead_table, behind_table, over, under, twist = tables()
+    ahead_table, behind_table, over, under, twist, omega = tables()
     earlier = lax.ppermute(projected[seg - 8 :], EVERY, [(s, s + 1) for s in range(count - 1)])
     plane = pltpu.VMEM((seg, channels), jnp.float32)
-    stack = pltpu.VMEM((3, 256, LANE), jnp.float32)
-    rows, queries, direct, head = pl.pallas_call(
+    stack = pltpu.VMEM((4, 256, LANE), jnp.float32)
+    packed = pl.pallas_call(
         pack_kernel,
-        out_specs=(near, near, near, near),
-        out_shape=(stack, plane, plane, pltpu.VMEM((24, wide), jnp.float32)),
+        out_specs=near,
+        out_shape=pltpu.VMEM((PEERS, HIGH, 4 * LANE), jnp.bfloat16),
+        scratch_shapes=[pltpu.VMEM((seg + 8, 2 * LANE), jnp.float32), stack],
+        name="pack",
+    )(projected, short_taps, long_filter.reshape(HIGH, LANE))
+    queries, direct = pl.pallas_call(
+        plan_kernel,
+        out_specs=(near, near),
+        out_shape=(plane, plane),
         scratch_shapes=[pltpu.VMEM((seg + 8, wide), jnp.float32)],
-        name="pack",
-    )(projected, short_taps, skip_gain.reshape(1, channels), long_filter.reshape(HIGH, LANE))
-    packed, fixed = on_chip(
-        mend_kernel,
-        (pltpu.VMEM((PEERS, HIGH, 3 * LANE), jnp.bfloat16), pltpu.VMEM((16, channels), jnp.float32)),
-        [pltpu.VMEM((16, wide), jnp.float32), stack],
-        "mend",
-        rows,
-        head,
-        earlier,
-    )
+        name="plan",
+    )(projected, earlier, short_taps, skip_gain.reshape(1, channels))
     arrived = exchange(packed, FIRST)
     ahead = on_chip(
         ahead_kernel,
-        (pltpu.VMEM((PLANES, BLOCKS, KQ * 3 * 256), jnp.bfloat16),),
-        [],
+        (pltpu.VMEM((PLANES, BLOCKS, KQ * 3 * 256 + LANE), jnp.bfloat16),),
+        [stack, pltpu.VMEM((PEERS, LANE), jnp.float32)],
         "ahead",
         arrived,
         ahead_table,
@@ -275,6 +313,7 @@
         lined,
         over,
         under,
+        omega,
     )
     returned = exchange(blocks, SECOND)
     behind = on_chip(
@@ -289,11 +328,11 @@
     home = exchange(behind, FIRST)
     return pl.pallas_call(
         gate_kernel,
-        in_specs=[near] * 4,
+        in_specs=[near] * 3,
         out_shape=jax.ShapeDtypeStruct((seg, channels), jnp.float32),
         scratch_shapes=[pltpu.VMEM((8 * PEERS, LANE), jnp.float32)],
         name="gate",
-    )(*[pltpu.with_memory_space_constraint(arg, pltpu.VMEM) for arg in (queries, direct, fixed, home)])
+    )(*[pltpu.with_memory_space_constraint(arg, pltpu.VMEM) for arg in (queries, direct, home)])
 
 
 def solution(mesh):

time: 83.4 us -> 80.9 us (0.970)
  blocking collectives: 65.5 us -> 55.4 us
  Pallas kernels: 5.73 us -> 8.65 us
  starting transfers between devices: 4.81 us -> 7.41 us
  local copies, waits for them, and re-layouts: 0.79 us -> 2.36 us
    all_to_all x4 -> x3, blocking collectives: 65.5 us -> 55.4 us  [exchange(): return lax.all_to_all(value, axis, split_axis=0, concat_axis=0, tiled=True)]
    all_to_all x0 -> x1, starting transfers between devices: none -> 4.62 us  [exchange(): return lax.all_to_all(value, axis, split_axis=0, concat_axis=0, tiled=True)]
    ppermute x1, starting transfers between devices: 4.81 us -> 2.79 us  [on_device(): lax.ppermute(projected[seg - 8:], EVERY, [(s, s + 1) for s in range(count...]
    unnamed x10 -> x14, local copies, waits for them, and re-layouts: 0.02 us -> 1.66 us
    pallas_call x2 -> x3, Pallas kernels: 2.28 us -> 3.84 us  [the longest x1 1.53 us: on_device(): pl.pallas_call(plan_kernel, out_specs=(near, near), out_shape=(plane, pla...]
    pallas_call x4 -> x3, Pallas kernels: 3.45 us -> 4.81 us  [on_chip(): pl.pallas_call(kernel, in_specs=[near] * len(args), out_specs=tuple((near...]
  transfers between devices with their start and end apart: 1 -> 2, of which waited for: 1 -> 1; matrix products, arithmetic and copies ran while one was open for 0% -> 1% of each run, Pallas kernels for 2% -> 2%
where the time goes in v5:
time: 80.9 us; the launch traced here: 80.2 us
  blocking collectives  55.4 us (68%)
  Pallas kernels  8.65 us (11%)
  starting transfers between devices  7.41 us (9%)
  waiting for transfers between devices  6.38 us (8%)
  local copies, waits for them, and re-layouts  2.36 us (3%)
    all_to_all x3, blocking collectives, exchange(): return lax.all_to_all(value, axis, split_axis=0, concat_axis=0, tiled=True)  55.4 us
    ppermute x1, waiting for transfers between devices, on_device(): lax.ppermute(projected[seg - 8:], EVERY, [(s, s + 1) for s in range(count...  6.37 us
    pallas_call x3, Pallas kernels, on_chip(): pl.pallas_call(kernel, in_specs=[near] * len(args), out_specs=tuple((near...  4.81 us
    all_to_all x1, starting transfers between devices, exchange(): return lax.all_to_all(value, axis, split_axis=0, concat_axis=0, tiled=True)  4.62 us
    ppermute x1, starting transfers between devices, on_device(): lax.ppermute(projected[seg - 8:], EVERY, [(s, s + 1) for s in range(count...  2.79 us
    unnamed x14, local copies, waits for them, and re-layouts  1.66 us
  transfers between devices with their start and end apart: 2, of which 1 were waited for; matrix products, arithmetic and copies ran while one was open for 1% of the time, Pallas kernels for 2%

profile of v5, /device:TPU:1, one launch (start us, length us, event | category | flops | bytes accessed | tf_op | source)
XLA Modules:
  0.0 80.2 jit_solution(12077429862163092815)
XLA Ops:
  0.0 0.0 copy-start.1
  0.0 1.5 %pack.1 = bf16[64,4,512]{2,1,0:T(4,128)(2,1)S(1)} custom-call(bf16[512,384]{1,0:T(8,128)(2,1)} %projected_ref.3, f32[3,384]{1,0:T(4,128)} %taps_ref.3, bf16[4,128]{1,0:T(4,128)(2,1)} %bitcast.2), custom_call_target="tpu_custom_call" | custom-call | tf_op jit(solution)/shard_map/pack/pallas_call | solution.py:283
  1.5 0.0 copy-start
  1.5 29.9 %all_to_all.20.data_ref = bf16[64,4,512]{2,1,0:T(4,128)(2,1)S(1)} all-to-all(bf16[64,4,512]{2,1,0:T(4,128)(2,1)S(1)} %pack.1), channel_id=1, replica_groups=mesh['zh'=2,'y'=8,'core'=2,'x'=4,'zl'=4] {'zh','y','zl'}, dimensions={0} | all-to-all | bytes 524288 | tf_op jit(solution)/shard_map/all_to_all | solution.py:259
  31.4 0.0 copy-done.1
  31.4 0.0 copy-done
  31.4 1.1 %ahead.1 = bf16[8,16,1664]{2,1,0:T(8,128)(2,1)S(1)} custom-call(bf16[64,4,512]{2,1,0:T(4,128)(2,1)S(1)} %all_to_all.20.data_ref, bf16[2,768,256]{2,1,0:T(8,128)(2,1)S(1)} %copy-done.1, f32[256,256]{1,0:T(8,128)S(1)} %copy-done), custom_call_target="tpu_custom_call" | custom-call | tf_op jit(solution)/shard_map/ahead/pallas_call | solution.py:264
  32.5 0.0 copy-start.4
  32.5 0.0 copy-start.5
  32.5 15.7 %all_to_all.21.data_ref = bf16[8,16,1664]{2,1,0:T(8,128)(2,1)S(1)} all-to-all(bf16[8,16,1664]{2,1,0:T(8,128)(2,1)S(1)} %ahead.1), channel_id=1, replica_groups=mesh['zh'=2,'y'=8,'core'=2,'x'=4,'zl'=4] {'core','x'}, dimensions={0} | all-to-all | bytes 851968 | tf_op jit(solution)/shard_map/all_to_all | solution.py:259
  48.3 0.0 copy-done.4
  48.3 0.0 copy-done.5
  48.3 0.0 copy-start.3
  48.3 1.0 %copy-done.3 = bf16[2,256,512]{2,1,0:T(8,128)(2,1)S(1)} copy-done((bf16[2,256,512]{2,1,0:T(8,128)(2,1)S(1)}, bf16[2,256,512]{2,1,0:T(8,128)(2,1)}, u32[]{:S(2)}) %copy-start.3) | copy-done | bytes 524312
  49.3 0.0 copy-start.2
  49.3 2.3 %blocks.1 = bf16[8,16,1024]{2,1,0:T(8,128)(2,1)S(1)} custom-call(bf16[8,16,1664]{2,1,0:T(8,128)(2,1)S(1)} %all_to_all.21.data_ref, bf16[2,512,256]{2,1,0:T(8,128)(2,1)S(1)} %copy-done.4, bf16[2,256,512]{2,1,0:T(8,128)(2,1)S(1)} %copy-done.3, f32[8,8,128]{2,1,0:T(8,128)S(1)} %copy-done.5), custom_call_target="tpu_custom_call" | custom-call | tf_op jit(solution)/shard_map/blocks/pallas_call | solution.py:264
  51.6 9.7 %all_to_all.22.data_ref = bf16[8,16,1024]{2,1,0:T(8,128)(2,1)S(1)} all-to-all(bf16[8,16,1024]{2,1,0:T(8,128)(2,1)S(1)} %blocks.1), channel_id=1, replica_groups=mesh['zh'=2,'y'=8,'core'=2,'x'=4,'zl'=4] {'core','x'}, dimensions={0} | all-to-all | bytes 524288 | tf_op jit(solution)/shard_map/all_to_all | solution.py:259
  61.4 0.0 copy-done.2
  61.4 1.4 %behind.1 = bf16[64,8,128]{2,1,0:T(8,128)(2,1)} custom-call(bf16[8,16,1024]{2,1,0:T(8,128)(2,1)S(1)} %all_to_all.22.data_ref, bf16[2,256,768]{2,1,0:T(8,128)(2,1)S(1)} %copy-done.2, f32[256,256]{1,0:T(8,128)S(1)} %copy-done), custom_call_target="tpu_custom_call" | custom-call | tf_op jit(solution)/shard_map/behind/pallas_call | solution.py:264
  62.7 4.6 %all-to-all-start.3 = ((bf16[64,8,128]{2,1,0:T(8,128)(2,1)}), bf16[64,8,128]{2,1,0:T(8,128)(2,1)S(1)}, u32[]{:S(2)}, u32[]{:S(2)}) async-start(bf16[64,8,128]{2,1,0:T(8,128)(2,1)} %behind.1), calls=%async_computation.3 | async-start | bytes 262144 | tf_op jit(solution)/shard_map/all_to_all | solution.py:259
  67.4 0.7 slice.3
  68.1 2.8 %collective-permute-start = (bf16[8,384]{1,0:T(8,128)(2,1)S(1)}, bf16[8,384]{1,0:T(8,128)(2,1)S(1)}, u32[]{:S(2)}, u32[]{:S(2)}) collective-permute-start(bf16[8,384]{1,0:T(8,128)(2,1)S(1)} %slice.3), channel_id=1, source_target_pairs={{0,1},{1,2},{2,3},{3,4},{4,5},{5,6},{6,7},{7,8},{8,9},{9,10},{10,1... | collective-permute-start | bytes 18440 | tf_op jit(solution)/shard_map/ppermute | solution.py:280
  70.9 6.4 %collective-permute-done.earlier_ref = bf16[8,384]{1,0:T(8,128)(2,1)S(1)} collective-permute-done((bf16[8,384]{1,0:T(8,128)(2,1)S(1)}, bf16[8,384]{1,0:T(8,128)(2,1)S(1)}, u32[]{:S(2)}, u32[]{:S(2)}) %collective-permute-start) | collective-permute-done | bytes 6176 | tf_op jit(solution)/shard_map/ppermute | solution.py:280
  77.2 0.0 copy-start.6
  77.2 0.6 copy-done.6
  77.8 1.5 %plan.1 = (f32[512,128]{1,0:T(8,128)S(1)}, f32[512,128]{1,0:T(8,128)S(1)}) custom-call(bf16[512,384]{1,0:T(8,128)(2,1)} %projected_ref.3, bf16[8,384]{1,0:T(8,128)(2,1)} %copy-done.6, f32[3,384]{1,0:T(4,128)} %taps_ref.3, f32[1,128]{1,0:T(1,128)} %bitcast.3), custom_call_target="tpu_custom_call" | custom-call | tf_op jit(solution)/shard_map/plan/pallas_call | solution.py:290
  79.4 0.0 all-to-all-done.3.data_ref
  79.4 0.9 %gate.1 = f32[512,128]{1,0:T(8,128)} custom-call(f32[512,128]{1,0:T(8,128)S(1)} %get-tuple-element.7.queries_ref, f32[512,128]{1,0:T(8,128)S(1)} %get-tuple-element.8.direct_ref, bf16[64,8,128]{2,1,0:T(8,128)(2,1)S(1)} %all-to-all-done.3.data_ref), custom_call_target="tpu_custom_call" | custom-call | tf_op jit(solution)/shard_map/gate/pallas_call | solution.py:329
Async XLA Ops:
  0.0 31.4 %copy-start.1 = (bf16[2,768,256]{2,1,0:T(8,128)(2,1)S(1)}, bf16[2,768,256]{2,1,0:T(8,128)(2,1)}, u32[]{:S(2)}) copy-start(bf16[2,768,256]{2,1,0:T(8,128)(2,1)} %constant.12.clone.table_ref) | copy-start | bytes 2359300
  1.5 29.9 %copy-start = (f32[256,256]{1,0:T(8,128)S(1)}, f32[256,256]{1,0:T(8,128)}, u32[]{:S(2)}) copy-start(f32[256,256]{1,0:T(8,128)} %constant.13.clone.twist_ref) | copy-start | bytes 786436
  32.5 15.8 %copy-start.4 = (bf16[2,512,256]{2,1,0:T(8,128)(2,1)S(1)}, bf16[2,512,256]{2,1,0:T(8,128)(2,1)}, u32[]{:S(2)}) copy-start(bf16[2,512,256]{2,1,0:T(8,128)(2,1)} %constant.14.clone.over_ref) | copy-start | bytes 1572868
  32.5 15.7 %copy-start.5 = (f32[8,8,128]{2,1,0:T(8,128)S(1)}, f32[8,8,128]{2,1,0:T(8,128)}, u32[]{:S(2)}) copy-start(f32[8,8,128]{2,1,0:T(8,128)} %constant.16.clone.omega_ref) | copy-start | bytes 98308
  48.3 1.0 %copy-start.3 = (bf16[2,256,512]{2,1,0:T(8,128)(2,1)S(1)}, bf16[2,256,512]{2,1,0:T(8,128)(2,1)}, u32[]{:S(2)}) copy-start(bf16[2,256,512]{2,1,0:T(8,128)(2,1)} %constant.15.clone.under_ref) | copy-start | bytes 1572868
  49.3 12.1 %copy-start.2 = (bf16[2,256,768]{2,1,0:T(8,128)(2,1)S(1)}, bf16[2,256,768]{2,1,0:T(8,128)(2,1)}, u32[]{:S(2)}) copy-start(bf16[2,256,768]{2,1,0:T(8,128)(2,1)} %constant.17.clone.table_ref) | copy-start | bytes 2359300
  62.7 16.6 %all-to-all-start.3 = ((bf16[64,8,128]{2,1,0:T(8,128)(2,1)}), bf16[64,8,128]{2,1,0:T(8,128)(2,1)S(1)}, u32[]{:S(2)}, u32[]{:S(2)}) async-start(bf16[64,8,128]{2,1,0:T(8,128)(2,1)} %behind.1), calls=%async_computation.3 | async-start | bytes 262144 | tf_op jit(solution)/shard_map/all_to_all | solution.py:259
  68.1 9.2 %collective-permute-start = (bf16[8,384]{1,0:T(8,128)(2,1)S(1)}, bf16[8,384]{1,0:T(8,128)(2,1)S(1)}, u32[]{:S(2)}, u32[]{:S(2)}) collective-permute-start(bf16[8,384]{1,0:T(8,128)(2,1)S(1)} %slice.3), channel_id=1, source_target_pairs={{0,1},{1,2},{2,3},{3,4},{4,5},{5,6},{6,7},{7,8},{8,9},{9,10},{10,1... | collective-permute-start | bytes 18440 | tf_op jit(solution)/shard_map/ppermute | solution.py:280
  77.2 0.6 copy-start.6

commit v6 on v5

--- a/solution.py
+++ b/solution.py
@@ -21,6 +21,7 @@
 LINES = 16
 KQ = 2
 WAVES = 256
+GRANT = pltpu.CompilerParams(vmem_limit_bytes=12 * 2**20)
 EDGE = ((0, 0), (1, 0), (0, 1), (1, 1), (2, 0), (3, 0), (2, 1), (3, 1))
 
 
@@ -53,7 +54,7 @@
     first_back = np.concatenate([backward(cos), backward(sin)], axis=1)
     cos, sin = turn_of(np.outer(line + 0.25, np.arange(LANE)) / SPAN)
     rows = np.broadcast_to(line.reshape(PLANES, KQ).T[:, :, None], (KQ, PLANES, BLOCKS)).reshape(-1)
-    twist = np.concatenate([cos[rows], sin[rows]], axis=1).astype(np.float32)
+    twist = np.concatenate([cos[rows], sin[rows]], axis=1)
     cos, sin = turn_of(np.outer(np.arange(LANE), np.arange(LANE)) / LANE)
     second = np.block([[cos, sin], [-sin, cos]])
     block = (np.arange(BLOCKS)[None, :] * PLANES + np.arange(PLANES)[:, None]).reshape(-1)
@@ -66,10 +67,11 @@
     under = np.block([[real, -imag], [imag, real]])
     spot = line.reshape(PLANES, KQ, 1) + LINES * np.arange(LANE) + 0.25
     omega = np.stack(turn_of(spot / SPAN), axis=2).reshape(PLANES, 2 * KQ, LANE)
-    omega = np.concatenate([omega, np.zeros_like(omega)], axis=1).astype(np.float32)
+    omega = np.concatenate([omega, np.zeros_like(omega)], axis=1).reshape(8 * PLANES, LANE)
+    twist = np.concatenate([twist, np.concatenate([omega, np.zeros_like(omega)], axis=1)], axis=0).astype(np.float32)
     ahead = halves(np.concatenate([first, second], axis=0))
     behind = halves(np.concatenate([first_back, second.T], axis=1))
-    return ahead, behind, halves(over), halves(under), twist, omega
+    return ahead, behind, halves(over), halves(under), twist
 
 
 def mxu(left, right):
@@ -88,8 +90,9 @@
     return total
 
 
-def pack_kernel(projected_ref, taps_ref, filter_ref, out_ref, ext_ref, rows_ref):
+def pack_kernel(projected_ref, taps_ref, filter_ref, out_ref, tail_ref, ext_ref, rows_ref):
     seg = projected_ref.shape[0]
+    tail_ref[...] = projected_ref[seg - 8 :, :]
     ext_ref[0:8, :] = jnp.zeros((8, 2 * LANE), jnp.float32)
     ext_ref[8 : 8 + seg, :] = projected_ref[:, LANE:].astype(jnp.float32)
     taps = taps_ref[:, LANE:]
@@ -161,8 +164,8 @@
         out_ref[plane, :, KQ * 3 * 256 :] = outside
     data = jnp.concatenate([rows_ref[0], rows_ref[1], rows_ref[2]], axis=1).astype(jnp.bfloat16)
     waves = mxu(table_ref[0, :512, :], data) + mxu(table_ref[1, :512, :], data)
-    cos = twist_ref[:, :LANE]
-    sin = twist_ref[:, LANE:]
+    cos = twist_ref[:256, :LANE]
+    sin = twist_ref[:256, LANE:]
     for number in range(3):
         real = waves[:256, number * LANE : (number + 1) * LANE]
         imag = waves[256:, number * LANE : (number + 1) * LANE]
@@ -175,8 +178,8 @@
             out_ref[:, :, at : at + 256] = value.astype(jnp.bfloat16)
 
 
-def blocks_kernel(data_ref, over_ref, under_ref, omega_ref, out_ref):
-    omega = omega_ref[lax.axis_index(SECOND)]
+def blocks_kernel(data_ref, over_ref, under_ref, twist_ref, out_ref):
+    omega = twist_ref[pl.ds(256 + 8 * lax.axis_index(SECOND), 8), :LANE]
     owns = [whole_edges(data_ref[plane, :, KQ * 3 * 256 :].astype(jnp.float32)) for plane in range(PLANES)]
     row = lax.broadcasted_iota(jnp.int32, (BLOCKS, LANE), 0)
     wrapped = jnp.where(row == 0, 0.0, pltpu.roll(back(owns[PLANES - 1], 4), 1, 0))
@@ -268,6 +271,7 @@
         out_shape=outs if len(outs) > 1 else outs[0],
         scratch_shapes=scratch,
         name=name,
+        compiler_params=GRANT,
     )(*[pltpu.with_memory_space_constraint(arg, pltpu.VMEM) for arg in args])
 
 
@@ -276,25 +280,31 @@
     channels = skip_gain.shape[0]
     count = lax.axis_size(EVERY)
     near = pl.BlockSpec(memory_space=pltpu.VMEM)
-    ahead_table, behind_table, over, under, twist, omega = tables()
-    earlier = lax.ppermute(projected[seg - 8 :], EVERY, [(s, s + 1) for s in range(count - 1)])
+    ahead_table, behind_table, over, under, twist = tables()
     plane = pltpu.VMEM((seg, channels), jnp.float32)
     stack = pltpu.VMEM((4, 256, LANE), jnp.float32)
-    packed = pl.pallas_call(
+    packed, tail = pl.pallas_call(
         pack_kernel,
-        out_specs=near,
-        out_shape=pltpu.VMEM((PEERS, HIGH, 4 * LANE), jnp.bfloat16),
+        out_specs=(near, near),
+        out_shape=(jax.ShapeDtypeStruct((PEERS, HIGH, 4 * LANE), jnp.bfloat16), pltpu.VMEM((8, wide), jnp.bfloat16)),
         scratch_shapes=[pltpu.VMEM((seg + 8, 2 * LANE), jnp.float32), stack],
         name="pack",
     )(projected, short_taps, long_filter.reshape(HIGH, LANE))
+    earlier = lax.ppermute(tail, EVERY, [(s, s + 1) for s in range(count - 1)])
     queries, direct = pl.pallas_call(
         plan_kernel,
         out_specs=(near, near),
         out_shape=(plane, plane),
         scratch_shapes=[pltpu.VMEM((seg + 8, wide), jnp.float32)],
         name="plan",
-    )(projected, earlier, short_taps, skip_gain.reshape(1, channels))
+    )(
+        projected,
+        pltpu.with_memory_space_constraint(earlier, pltpu.VMEM),
+        short_taps,
+        skip_gain.reshape(1, channels),
+    )
     arrived = exchange(packed, FIRST)
+    arrived, queries, direct = lax.optimization_barrier((arrived, queries, direct))
     ahead = on_chip(
         ahead_kernel,
         (pltpu.VMEM((PLANES, BLOCKS, KQ * 3 * 256 + LANE), jnp.bfloat16),),
@@ -313,7 +323,7 @@
         lined,
         over,
         under,
-        omega,
+        twist,
     )
     returned = exchange(blocks, SECOND)
     behind = on_chip(
@@ -332,6 +342,7 @@
         out_shape=jax.ShapeDtypeStruct((seg, channels), jnp.float32),
         scratch_shapes=[pltpu.VMEM((8 * PEERS, LANE), jnp.float32)],
         name="gate",
+        compiler_params=GRANT,
     )(*[pltpu.with_memory_space_constraint(arg, pltpu.VMEM) for arg in (queries, direct, home)])
 
 

time: 80.9 us -> 82.7 us (1.022)
  starting transfers between devices: 7.41 us -> 20.2 us
  blocking collectives: 55.4 us -> 45.2 us
  local copies, waits for them, and re-layouts: 2.36 us -> 0.02 us
  waiting for transfers between devices: 6.38 us -> 8.23 us
    all_to_all x1, starting transfers between devices: 4.62 us -> 17.1 us  [exchange(): return lax.all_to_all(value, axis, split_axis=0, concat_axis=0, tiled=True)]
    all_to_all x3, blocking collectives: 55.4 us -> 45.2 us  [exchange(): return lax.all_to_all(value, axis, split_axis=0, concat_axis=0, tiled=True)]
    unnamed x14 -> x10, local copies, waits for them, and re-layouts: 1.66 us -> 0.02 us
    all_to_all x1, waiting for transfers between devices: 0.01 us -> 1.51 us  [exchange(): return lax.all_to_all(value, axis, split_axis=0, concat_axis=0, tiled=True)]
  transfers between devices with their start and end apart: 2 -> 2, of which waited for: 1 -> 2; matrix products, arithmetic and copies ran while one was open for 1% -> 0% of each run, Pallas kernels for 2% -> 2%
where the time goes in v6:
time: 82.7 us; the launch traced here: 82.4 us
  blocking collectives  45.2 us (55%)
  starting transfers between devices  20.2 us (24%)
  Pallas kernels  8.7 us (11%)
  waiting for transfers between devices  8.23 us (10%)
    all_to_all x3, blocking collectives, exchange(): return lax.all_to_all(value, axis, split_axis=0, concat_axis=0, tiled=True)  45.2 us
    all_to_all x1, starting transfers between devices, exchange(): return lax.all_to_all(value, axis, split_axis=0, concat_axis=0, tiled=True)  17.1 us
    ppermute x1, waiting for transfers between devices, on_device(): earlier = lax.ppermute(tail, EVERY, [(s, s + 1) for s in range(count - 1)])  6.72 us
    pallas_call x3, Pallas kernels, on_chip(): pl.pallas_call(kernel, in_specs=[near] * len(args), out_specs=tuple((near...  4.16 us
    ppermute x1, starting transfers between devices, on_device(): earlier = lax.ppermute(tail, EVERY, [(s, s + 1) for s in range(count - 1)])  3.05 us
    pallas_call x1, Pallas kernels, on_device(): pl.pallas_call(pack_kernel, out_specs=(near, near), out_shape=(jax.ShapeD...  2.16 us
  transfers between devices with their start and end apart: 2, of which 2 were waited for; matrix products, arithmetic and copies ran while one was open for 0% of the time, Pallas kernels for 2%

profile of v6, /device:TPU:1, one launch (start us, length us, event | category | flops | bytes accessed | tf_op | source)
XLA Modules:
  0.0 82.4 jit_solution(16945107225187330340)
XLA Ops:
  0.0 0.0 copy-start.1
  0.0 2.2 %pack.1 = (bf16[64,4,512]{2,1,0:T(4,128)(2,1)}, bf16[8,384]{1,0:T(8,128)(2,1)S(1)}) custom-call(bf16[512,384]{1,0:T(8,128)(2,1)} %projected_ref.3, f32[3,384]{1,0:T(4,128)} %taps_ref.3, bf16[4,128]{1,0:T(4,128)(2,1)} %bitcast.2), custom_call_target="tpu_custom_call" | custom-call | tf_op jit(solution)/shard_map/pack/pallas_call | solution.py:286
  2.2 17.1 %all-to-all-start = ((bf16[64,4,512]{2,1,0:T(4,128)(2,1)}), bf16[64,4,512]{2,1,0:T(4,128)(2,1)S(1)}, u32[]{:S(2)}, u32[]{:S(2)}) async-start(bf16[64,4,512]{2,1,0:T(4,128)(2,1)} %get-tuple-element.12), calls=%async_computation | async-start | bytes 524288 | tf_op jit(solution)/shard_map/all_to_all | solution.py:262
  19.3 0.0 copy-start
  19.3 3.1 %collective-permute-start = (bf16[8,384]{1,0:T(8,128)(2,1)S(1)}, bf16[8,384]{1,0:T(8,128)(2,1)S(1)}, u32[]{:S(2)}, u32[]{:S(2)}) collective-permute-start(bf16[8,384]{1,0:T(8,128)(2,1)S(1)} %get-tuple-element.13), channel_id=1, source_target_pairs={{0,1},{1,2},{2,3},{3,4},{4,5},{5,6},{6,7},{7,8},{8,9},{9,10},{10,1... | collective-permute-start | bytes 18440 | tf_op jit(solution)/shard_map/ppermute | solution.py:293
  22.4 6.7 %collective-permute-done.earlier_ref = bf16[8,384]{1,0:T(8,128)(2,1)S(1)} collective-permute-done((bf16[8,384]{1,0:T(8,128)(2,1)S(1)}, bf16[8,384]{1,0:T(8,128)(2,1)S(1)}, u32[]{:S(2)}, u32[]{:S(2)}) %collective-permute-start) | collective-permute-done | bytes 6176 | tf_op jit(solution)/shard_map/ppermute | solution.py:293
  29.1 1.5 %plan.1 = (f32[512,128]{1,0:T(8,128)S(1)}, f32[512,128]{1,0:T(8,128)S(1)}) custom-call(bf16[512,384]{1,0:T(8,128)(2,1)} %projected_ref.3, bf16[8,384]{1,0:T(8,128)(2,1)S(1)} %collective-permute-done.earlier_ref, f32[3,384]{1,0:T(4,128)} %taps_ref.3, f32[1,128]{1,0:T(1,128)} %bitcast.3), custom_call_target="tpu_custom_call" | custom-call | tf_op jit(solution)/shard_map/plan/pallas_call | solution.py:294
  30.6 1.5 %all-to-all-done.data_ref = bf16[64,4,512]{2,1,0:T(4,128)(2,1)S(1)} async-done(((bf16[64,4,512]{2,1,0:T(4,128)(2,1)}), bf16[64,4,512]{2,1,0:T(4,128)(2,1)S(1)}, u32[]{:S(2)}, u32[]{:S(2)}) %all-to-all-start) | async-done | bytes 262176 | tf_op jit(solution)/shard_map/all_to_all | solution.py:262
  32.1 0.0 copy-done.1
  32.1 0.0 copy-done
  32.1 0.0 copy-start.4
  32.1 1.1 %ahead.1 = bf16[8,16,1664]{2,1,0:T(8,128)(2,1)S(1)} custom-call(bf16[64,4,512]{2,1,0:T(4,128)(2,1)S(1)} %all-to-all-done.data_ref, bf16[2,768,256]{2,1,0:T(8,128)(2,1)S(1)} %copy-done.1, f32[320,256]{1,0:T(8,128)S(1)} %copy-done), custom_call_target="tpu_custom_call" | custom-call | tf_op jit(solution)/shard_map/ahead/pallas_call | solution.py:267
  33.3 0.0 copy-start.3
  33.3 15.7 %all_to_all.20.data_ref = bf16[8,16,1664]{2,1,0:T(8,128)(2,1)S(1)} all-to-all(bf16[8,16,1664]{2,1,0:T(8,128)(2,1)S(1)} %ahead.1), channel_id=1, replica_groups=mesh['zh'=2,'y'=8,'core'=2,'x'=4,'zl'=4] {'core','x'}, dimensions={0} | all-to-all | bytes 851968 | tf_op jit(solution)/shard_map/all_to_all | solution.py:262
  49.0 0.0 copy-done.4
  49.0 0.0 copy-done.3
  49.0 0.0 copy-start.2
  49.0 2.3 %blocks.1 = bf16[8,16,1024]{2,1,0:T(8,128)(2,1)S(1)} custom-call(bf16[8,16,1664]{2,1,0:T(8,128)(2,1)S(1)} %all_to_all.20.data_ref, bf16[2,512,256]{2,1,0:T(8,128)(2,1)S(1)} %copy-done.4, bf16[2,256,512]{2,1,0:T(8,128)(2,1)S(1)} %copy-done.3, f32[320,256]{1,0:T(8,128)S(1)} %copy-done), custom_call_target="tpu_custom_call" | custom-call | tf_op jit(solution)/shard_map/blocks/pallas_call | solution.py:267
  51.3 9.7 %all_to_all.21.data_ref = bf16[8,16,1024]{2,1,0:T(8,128)(2,1)S(1)} all-to-all(bf16[8,16,1024]{2,1,0:T(8,128)(2,1)S(1)} %blocks.1), channel_id=1, replica_groups=mesh['zh'=2,'y'=8,'core'=2,'x'=4,'zl'=4] {'core','x'}, dimensions={0} | all-to-all | bytes 524288 | tf_op jit(solution)/shard_map/all_to_all | solution.py:262
  61.1 0.0 copy-done.2
  61.1 0.7 behind.1
  61.8 19.7 %all_to_all.22.data_ref = bf16[64,8,128]{2,1,0:T(8,128)(2,1)S(1)} all-to-all(bf16[64,8,128]{2,1,0:T(8,128)(2,1)S(1)} %behind.1), channel_id=1, replica_groups=mesh['zh'=2,'y'=8,'core'=2,'x'=4,'zl'=4] {'zh','y','zl'}, dimensions={0} | all-to-all | bytes 262144 | tf_op jit(solution)/shard_map/all_to_all | solution.py:262
  81.6 0.9 %gate.1 = f32[512,128]{1,0:T(8,128)} custom-call(f32[512,128]{1,0:T(8,128)S(1)} %get-tuple-element.16.queries_ref, f32[512,128]{1,0:T(8,128)S(1)} %get-tuple-element.17.direct_ref, bf16[64,8,128]{2,1,0:T(8,128)(2,1)S(1)} %all_to_all.22.data_ref), custom_call_target="tpu_custom_call" | custom-call | tf_op jit(solution)/shard_map/gate/pallas_call | solution.py:339
Async XLA Ops:
  0.0 32.1 %copy-start.1 = (bf16[2,768,256]{2,1,0:T(8,128)(2,1)S(1)}, bf16[2,768,256]{2,1,0:T(8,128)(2,1)}, u32[]{:S(2)}) copy-start(bf16[2,768,256]{2,1,0:T(8,128)(2,1)} %constant.10.clone.table_ref) | copy-start | bytes 2359300
  2.2 30.0 %all-to-all-start = ((bf16[64,4,512]{2,1,0:T(4,128)(2,1)}), bf16[64,4,512]{2,1,0:T(4,128)(2,1)S(1)}, u32[]{:S(2)}, u32[]{:S(2)}) async-start(bf16[64,4,512]{2,1,0:T(4,128)(2,1)} %get-tuple-element.12), calls=%async_computation | async-start | bytes 524288 | tf_op jit(solution)/shard_map/all_to_all | solution.py:262
  19.3 12.8 %copy-start = (f32[320,256]{1,0:T(8,128)S(1)}, f32[320,256]{1,0:T(8,128)}, u32[]{:S(2)}) copy-start(f32[320,256]{1,0:T(8,128)} %constant.11.clone.twist_ref) | copy-start | bytes 983044
  19.3 9.8 %collective-permute-start = (bf16[8,384]{1,0:T(8,128)(2,1)S(1)}, bf16[8,384]{1,0:T(8,128)(2,1)S(1)}, u32[]{:S(2)}, u32[]{:S(2)}) collective-permute-start(bf16[8,384]{1,0:T(8,128)(2,1)S(1)} %get-tuple-element.13), channel_id=1, source_target_pairs={{0,1},{1,2},{2,3},{3,4},{4,5},{5,6},{6,7},{7,8},{8,9},{9,10},{10,1... | collective-permute-start | bytes 18440 | tf_op jit(solution)/shard_map/ppermute | solution.py:293
  32.1 16.9 %copy-start.4 = (bf16[2,512,256]{2,1,0:T(8,128)(2,1)S(1)}, bf16[2,512,256]{2,1,0:T(8,128)(2,1)}, u32[]{:S(2)}) copy-start(bf16[2,512,256]{2,1,0:T(8,128)(2,1)} %constant.12.clone.over_ref) | copy-start | bytes 1572868
  33.3 15.7 %copy-start.3 = (bf16[2,256,512]{2,1,0:T(8,128)(2,1)S(1)}, bf16[2,256,512]{2,1,0:T(8,128)(2,1)}, u32[]{:S(2)}) copy-start(bf16[2,256,512]{2,1,0:T(8,128)(2,1)} %constant.13.clone.under_ref) | copy-start | bytes 1572868
  49.0 12.1 %copy-start.2 = (bf16[2,256,768]{2,1,0:T(8,128)(2,1)S(1)}, bf16[2,256,768]{2,1,0:T(8,128)(2,1)}, u32[]{:S(2)}) copy-start(bf16[2,256,768]{2,1,0:T(8,128)(2,1)} %constant.14.clone.table_ref) | copy-start | bytes 2359300

commit v7 on v6

--- a/solution.py
+++ b/solution.py
@@ -262,6 +262,10 @@
     return lax.all_to_all(value, axis, split_axis=0, concat_axis=0, tiled=True)
 
 
+def far(value):
+    return pltpu.with_memory_space_constraint(value, pltpu.HBM)
+
+
 def on_chip(kernel, outs, scratch, name, *args):
     near = pl.BlockSpec(memory_space=pltpu.VMEM)
     return pl.pallas_call(
@@ -286,10 +290,12 @@
     packed, tail = pl.pallas_call(
         pack_kernel,
         out_specs=(near, near),
-        out_shape=(jax.ShapeDtypeStruct((PEERS, HIGH, 4 * LANE), jnp.bfloat16), pltpu.VMEM((8, wide), jnp.bfloat16)),
+        out_shape=(pltpu.VMEM((PEERS, HIGH, 4 * LANE), jnp.bfloat16), pltpu.VMEM((8, wide), jnp.bfloat16)),
         scratch_shapes=[pltpu.VMEM((seg + 8, 2 * LANE), jnp.float32), stack],
         name="pack",
-    )(projected, short_taps, long_filter.reshape(HIGH, LANE))
+        cost_estimate=pl.CostEstimate(flops=200000000, bytes_accessed=800000, transcendentals=0),
+        compiler_params=GRANT,
+    )(far(projected), far(short_taps), far(long_filter.reshape(HIGH, LANE)))
     earlier = lax.ppermute(tail, EVERY, [(s, s + 1) for s in range(count - 1)])
     queries, direct = pl.pallas_call(
         plan_kernel,
@@ -297,14 +303,14 @@
         out_shape=(plane, plane),
         scratch_shapes=[pltpu.VMEM((seg + 8, wide), jnp.float32)],
         name="plan",
+        compiler_params=GRANT,
     )(
-        projected,
+        far(projected),
         pltpu.with_memory_space_constraint(earlier, pltpu.VMEM),
-        short_taps,
-        skip_gain.reshape(1, channels),
+        far(short_taps),
+        far(skip_gain.reshape(1, channels)),
     )
     arrived = exchange(packed, FIRST)
-    arrived, queries, direct = lax.optimization_barrier((arrived, queries, direct))
     ahead = on_chip(
         ahead_kernel,
         (pltpu.VMEM((PLANES, BLOCKS, KQ * 3 * 256 + LANE), jnp.bfloat16),),

time: 82.7 us -> 79.2 us (0.958)
  starting transfers between devices: 20.2 us -> 7.43 us
  blocking collectives: 45.2 us -> 55.4 us
  waiting for transfers between devices: 8.23 us -> 7.33 us
    all_to_all x1, starting transfers between devices: 17.1 us -> 4.62 us  [exchange(): return lax.all_to_all(value, axis, split_axis=0, concat_axis=0, tiled=True)]
    all_to_all x3, blocking collectives: 45.2 us -> 55.4 us  [exchange(): return lax.all_to_all(value, axis, split_axis=0, concat_axis=0, tiled=True)]
where the time goes in v7:
time: 79.2 us; the launch traced here: 78.9 us
  blocking collectives  55.4 us (70%)
  Pallas kernels  8.67 us (11%)
  starting transfers between devices  7.43 us (9%)
  waiting for transfers between devices  7.33 us (9%)
    all_to_all x3, blocking collectives, exchange(): return lax.all_to_all(value, axis, split_axis=0, concat_axis=0, tiled=True)  55.4 us
    ppermute x1, waiting for transfers between devices, on_device(): earlier = lax.ppermute(tail, EVERY, [(s, s + 1) for s in range(count - 1)])  6.35 us
    pallas_call x3, Pallas kernels, on_chip(): pl.pallas_call(kernel, in_specs=[near] * len(args), out_specs=tuple((near...  4.82 us
    all_to_all x1, starting transfers between devices, exchange(): return lax.all_to_all(value, axis, split_axis=0, concat_axis=0, tiled=True)  4.62 us
    ppermute x1, starting transfers between devices, on_device(): earlier = lax.ppermute(tail, EVERY, [(s, s + 1) for s in range(count - 1)])  2.81 us
  transfers between devices with their start and end apart: 2, of which 2 were waited for; matrix products, arithmetic and copies ran while one was open for 0% of the time, Pallas kernels for 2%

profile of v7, /device:TPU:1, one launch (start us, length us, event | category | flops | bytes accessed | tf_op | source)
XLA Modules:
  0.0 78.9 jit_solution(6343164292902385162)
XLA Ops:
  0.0 0.0 copy-start.1
  0.0 1.5 %pack.1 = (bf16[64,4,512]{2,1,0:T(4,128)(2,1)S(1)}, bf16[8,384]{1,0:T(8,128)(2,1)S(1)}) custom-call(bf16[512,384]{1,0:T(8,128)(2,1)} %projected_ref.3, f32[3,384]{1,0:T(4,128)} %taps_ref.3, bf16[4,128]{1,0:T(4,128)(2,1)} %bitcast.3), custom_call_target="tpu_custom_call" | custom-call | flops 200000000 | bytes 800000 | tf_op jit(solution)/shard_map/pack/pallas_call | solution.py:290
  1.5 0.0 copy-start
  1.5 29.9 %all_to_all.20.data_ref = bf16[64,4,512]{2,1,0:T(4,128)(2,1)S(1)} all-to-all(bf16[64,4,512]{2,1,0:T(4,128)(2,1)S(1)} %get-tuple-element.12), channel_id=1, replica_groups=mesh['zh'=2,'y'=8,'core'=2,'x'=4,'zl'=4] {'zh','y','zl'}, dimensions={0} | all-to-all | bytes 524288 | tf_op jit(solution)/shard_map/all_to_all | solution.py:262
  31.4 0.0 copy-done.1
  31.4 0.0 copy-done
  31.4 0.0 copy-start.4
  31.4 1.1 %ahead.1 = bf16[8,16,1664]{2,1,0:T(8,128)(2,1)S(1)} custom-call(bf16[64,4,512]{2,1,0:T(4,128)(2,1)S(1)} %all_to_all.20.data_ref, bf16[2,768,256]{2,1,0:T(8,128)(2,1)S(1)} %copy-done.1, f32[320,256]{1,0:T(8,128)S(1)} %copy-done), custom_call_target="tpu_custom_call" | custom-call | tf_op jit(solution)/shard_map/ahead/pallas_call | solution.py:271
  32.5 0.0 copy-start.3
  32.5 15.7 %all_to_all.21.data_ref = bf16[8,16,1664]{2,1,0:T(8,128)(2,1)S(1)} all-to-all(bf16[8,16,1664]{2,1,0:T(8,128)(2,1)S(1)} %ahead.1), channel_id=1, replica_groups=mesh['zh'=2,'y'=8,'core'=2,'x'=4,'zl'=4] {'core','x'}, dimensions={0} | all-to-all | bytes 851968 | tf_op jit(solution)/shard_map/all_to_all | solution.py:262
  48.3 0.0 copy-done.4
  48.3 0.0 copy-done.3
  48.3 0.0 copy-start.2
  48.3 2.3 %blocks.1 = bf16[8,16,1024]{2,1,0:T(8,128)(2,1)S(1)} custom-call(bf16[8,16,1664]{2,1,0:T(8,128)(2,1)S(1)} %all_to_all.21.data_ref, bf16[2,512,256]{2,1,0:T(8,128)(2,1)S(1)} %copy-done.4, bf16[2,256,512]{2,1,0:T(8,128)(2,1)S(1)} %copy-done.3, f32[320,256]{1,0:T(8,128)S(1)} %copy-done), custom_call_target="tpu_custom_call" | custom-call | tf_op jit(solution)/shard_map/blocks/pallas_call | solution.py:271
  50.6 9.7 %all_to_all.22.data_ref = bf16[8,16,1024]{2,1,0:T(8,128)(2,1)S(1)} all-to-all(bf16[8,16,1024]{2,1,0:T(8,128)(2,1)S(1)} %blocks.1), channel_id=1, replica_groups=mesh['zh'=2,'y'=8,'core'=2,'x'=4,'zl'=4] {'core','x'}, dimensions={0} | all-to-all | bytes 524288 | tf_op jit(solution)/shard_map/all_to_all | solution.py:262
  60.3 0.0 copy-done.2
  60.3 1.4 %behind.1 = bf16[64,8,128]{2,1,0:T(8,128)(2,1)} custom-call(bf16[8,16,1024]{2,1,0:T(8,128)(2,1)S(1)} %all_to_all.22.data_ref, bf16[2,256,768]{2,1,0:T(8,128)(2,1)S(1)} %copy-done.2, f32[320,256]{1,0:T(8,128)S(1)} %copy-done), custom_call_target="tpu_custom_call" | custom-call | tf_op jit(solution)/shard_map/behind/pallas_call | solution.py:271
  61.7 4.6 %all-to-all-start.3 = ((bf16[64,8,128]{2,1,0:T(8,128)(2,1)}), bf16[64,8,128]{2,1,0:T(8,128)(2,1)S(1)}, u32[]{:S(2)}, u32[]{:S(2)}) async-start(bf16[64,8,128]{2,1,0:T(8,128)(2,1)} %behind.1), calls=%async_computation.3 | async-start | bytes 262144 | tf_op jit(solution)/shard_map/all_to_all | solution.py:262
  66.3 2.8 %collective-permute-start = (bf16[8,384]{1,0:T(8,128)(2,1)S(1)}, bf16[8,384]{1,0:T(8,128)(2,1)S(1)}, u32[]{:S(2)}, u32[]{:S(2)}) collective-permute-start(bf16[8,384]{1,0:T(8,128)(2,1)S(1)} %get-tuple-element.9), channel_id=1, source_target_pairs={{0,1},{1,2},{2,3},{3,4},{4,5},{5,6},{6,7},{7,8},{8,9},{9,10},{10,1... | collective-permute-start | bytes 18440 | tf_op jit(solution)/shard_map/ppermute | solution.py:299
  69.1 6.3 %collective-permute-done.earlier_ref = bf16[8,384]{1,0:T(8,128)(2,1)S(1)} collective-permute-done((bf16[8,384]{1,0:T(8,128)(2,1)S(1)}, bf16[8,384]{1,0:T(8,128)(2,1)S(1)}, u32[]{:S(2)}, u32[]{:S(2)}) %collective-permute-start) | collective-permute-done | bytes 6176 | tf_op jit(solution)/shard_map/ppermute | solution.py:299
  75.5 1.5 %plan.1 = (f32[512,128]{1,0:T(8,128)S(1)}, f32[512,128]{1,0:T(8,128)S(1)}) custom-call(bf16[512,384]{1,0:T(8,128)(2,1)} %projected_ref.3, bf16[8,384]{1,0:T(8,128)(2,1)S(1)} %collective-permute-done.earlier_ref, f32[3,384]{1,0:T(4,128)} %taps_ref.3, f32[1,128]{1,0:T(1,128)} %bitcast.2), custom_call_target="tpu_custom_call" | custom-call | tf_op jit(solution)/shard_map/plan/pallas_call | solution.py:300
  77.0 1.0 %all-to-all-done.3.data_ref = bf16[64,8,128]{2,1,0:T(8,128)(2,1)S(1)} async-done(((bf16[64,8,128]{2,1,0:T(8,128)(2,1)}), bf16[64,8,128]{2,1,0:T(8,128)(2,1)S(1)}, u32[]{:S(2)}, u32[]{:S(2)}) %all-to-all-start.3) | async-done | bytes 131104 | tf_op jit(solution)/shard_map/all_to_all | solution.py:262
  78.0 0.9 %gate.1 = f32[512,128]{1,0:T(8,128)} custom-call(f32[512,128]{1,0:T(8,128)S(1)} %get-tuple-element.10.queries_ref, f32[512,128]{1,0:T(8,128)S(1)} %get-tuple-element.11.direct_ref, bf16[64,8,128]{2,1,0:T(8,128)(2,1)S(1)} %all-to-all-done.3.data_ref), custom_call_target="tpu_custom_call" | custom-call | tf_op jit(solution)/shard_map/gate/pallas_call | solution.py:345
Async XLA Ops:
  0.0 31.4 %copy-start.1 = (bf16[2,768,256]{2,1,0:T(8,128)(2,1)S(1)}, bf16[2,768,256]{2,1,0:T(8,128)(2,1)}, u32[]{:S(2)}) copy-start(bf16[2,768,256]{2,1,0:T(8,128)(2,1)} %constant.10.clone.table_ref) | copy-start | bytes 2359300
  1.5 29.9 %copy-start = (f32[320,256]{1,0:T(8,128)S(1)}, f32[320,256]{1,0:T(8,128)}, u32[]{:S(2)}) copy-start(f32[320,256]{1,0:T(8,128)} %constant.11.clone.twist_ref) | copy-start | bytes 983044
  31.4 16.9 %copy-start.4 = (bf16[2,512,256]{2,1,0:T(8,128)(2,1)S(1)}, bf16[2,512,256]{2,1,0:T(8,128)(2,1)}, u32[]{:S(2)}) copy-start(bf16[2,512,256]{2,1,0:T(8,128)(2,1)} %constant.12.clone.over_ref) | copy-start | bytes 1572868
  32.5 15.7 %copy-start.3 = (bf16[2,256,512]{2,1,0:T(8,128)(2,1)S(1)}, bf16[2,256,512]{2,1,0:T(8,128)(2,1)}, u32[]{:S(2)}) copy-start(bf16[2,256,512]{2,1,0:T(8,128)(2,1)} %constant.13.clone.under_ref) | copy-start | bytes 1572868
  48.3 12.1 %copy-start.2 = (bf16[2,256,768]{2,1,0:T(8,128)(2,1)S(1)}, bf16[2,256,768]{2,1,0:T(8,128)(2,1)}, u32[]{:S(2)}) copy-start(bf16[2,256,768]{2,1,0:T(8,128)(2,1)} %constant.14.clone.table_ref) | copy-start | bytes 2359300
  61.7 16.3 %all-to-all-start.3 = ((bf16[64,8,128]{2,1,0:T(8,128)(2,1)}), bf16[64,8,128]{2,1,0:T(8,128)(2,1)S(1)}, u32[]{:S(2)}, u32[]{:S(2)}) async-start(bf16[64,8,128]{2,1,0:T(8,128)(2,1)} %behind.1), calls=%async_computation.3 | async-start | bytes 262144 | tf_op jit(solution)/shard_map/all_to_all | solution.py:262
  66.3 9.2 %collective-permute-start = (bf16[8,384]{1,0:T(8,128)(2,1)S(1)}, bf16[8,384]{1,0:T(8,128)(2,1)S(1)}, u32[]{:S(2)}, u32[]{:S(2)}) collective-permute-start(bf16[8,384]{1,0:T(8,128)(2,1)S(1)} %get-tuple-element.9), channel_id=1, source_target_pairs={{0,1},{1,2},{2,3},{3,4},{4,5},{5,6},{6,7},{7,8},{8,9},{9,10},{10,1... | collective-permute-start | bytes 18440 | tf_op jit(solution)/shard_map/ppermute | solution.py:299

commit v8 on v7

--- a/solution.py
+++ b/solution.py
@@ -119,14 +119,21 @@
         out_ref[:, :, at * LANE : (at + 1) * LANE] = rows_ref[at].reshape(PEERS, HIGH, LANE).astype(jnp.bfloat16)
 
 
-def plan_kernel(projected_ref, earlier_ref, taps_ref, gain_ref, queries_ref, direct_ref, ext_ref):
+def plan_kernel(projected_ref, taps_ref, gain_ref, queries_ref, direct_ref, head_ref, ext_ref):
     seg = projected_ref.shape[0]
-    ext_ref[0:8, :] = earlier_ref[...].astype(jnp.float32)
+    ext_ref[0:8, :] = jnp.zeros((8, 3 * LANE), jnp.float32)
     ext_ref[8 : 8 + seg, :] = projected_ref[...].astype(jnp.float32)
+    head_ref[0:8, :] = ext_ref[8:16, :]
+    head_ref[8:11, :] = taps_ref[...]
+    head_ref[16:17, 0:LANE] = gain_ref[...]
     filtered = short_filter(ext_ref, taps_ref[...], seg)
+    queries_ref[...] = filtered[:, :LANE]
+    direct_ref[...] = gain_ref[...] * mix_of(filtered)
+
+
+def mix_of(filtered):
     mixture = (filtered[:, LANE : 2 * LANE] * filtered[:, 2 * LANE :]).astype(jnp.bfloat16)
-    queries_ref[...] = filtered[:, :LANE]
-    direct_ref[...] = gain_ref[...] * mixture.astype(jnp.float32)
+    return mixture.astype(jnp.float32)
 
 
 def back(value, lanes):
@@ -188,27 +195,27 @@
 
     def piece(kq, number, part):
         at = ((kq * 3 + number) * 2 + part) * LANE
-        value = data_ref[:, :, at : at + LANE].astype(jnp.float32).reshape(128, LANE)
-        if number == 2:
-            return value
-        second = opening[:, 16 * number + 1 : 16 * number + 2] * omega[2 * kq + part : 2 * kq + part + 1, :]
-        if part == 0:
-            second = second + opening[:, 16 * number : 16 * number + 1]
-        return value + second
+        return data_ref[:, :, at : at + LANE].astype(jnp.float32).reshape(128, LANE)
 
     columns = []
-    for kq in range(KQ):
-        for number in range(3):
-            columns.append(jnp.concatenate([piece(kq, number, 0), piece(kq, number, 1)], axis=0))
+    for ch in range(2):
+        zeroth = jnp.broadcast_to(opening[:, 16 * ch : 16 * ch + 1], (128, LANE))
+        second = jnp.broadcast_to(opening[:, 16 * ch + 1 : 16 * ch + 2], (128, LANE))
+        for kq in range(KQ):
+            real = piece(kq, ch, 0) + (zeroth + second * omega[2 * kq : 2 * kq + 1, :])
+            imag = piece(kq, ch, 1) + second * omega[2 * kq + 1 : 2 * kq + 2, :]
+            columns.append(jnp.concatenate([real, imag], axis=0))
     upper, lower = cut(jnp.concatenate(columns, axis=1))
     waves = mxu(over_ref[0], upper) + (mxu(over_ref[0], lower) + mxu(over_ref[1], upper))
+    taps = [jnp.concatenate([piece(kq, 2, 0), piece(kq, 2, 1)], axis=0) for kq in range(KQ)]
+    taps = jnp.concatenate(taps, axis=1).astype(jnp.bfloat16)
+    taps = mxu(over_ref[0], taps) + mxu(over_ref[1], taps)
     products = []
     for kq in range(KQ):
-        at = (kq * 3 + 2) * LANE
-        tap_real = waves[:WAVES, at : at + LANE]
-        tap_imag = waves[WAVES:, at : at + LANE]
+        tap_real = taps[:WAVES, kq * LANE : (kq + 1) * LANE]
+        tap_imag = taps[WAVES:, kq * LANE : (kq + 1) * LANE]
         for ch in range(2):
-            at = (kq * 3 + ch) * LANE
+            at = (ch * KQ + kq) * LANE
             real = waves[:WAVES, at : at + LANE]
             imag = waves[WAVES:, at : at + LANE]
             both = [real * tap_real - imag * tap_imag, real * tap_imag + imag * tap_real]
@@ -249,13 +256,19 @@
     out_ref[...] = rows_ref[...].reshape(PEERS, 8, LANE).astype(jnp.bfloat16)
 
 
-def gate_kernel(queries_ref, direct_ref, data_ref, out_ref, rows_ref):
+def gate_kernel(queries_ref, direct_ref, head_ref, earlier_ref, data_ref, out_ref, rows_ref, ext_ref):
+    ext_ref[0:8, :] = earlier_ref[...].astype(jnp.float32)
+    ext_ref[8:16, :] = head_ref[0:8, :]
+    filtered = short_filter(ext_ref, head_ref[8:11, :], 8)
     rows_ref[...] = data_ref[...].astype(jnp.float32).reshape(8 * PEERS, LANE)
     for hi in range(HIGH):
         rows = [rows_ref[pl.ds(ch * HIGH + hi, PEERS, stride=8), :] for ch in range(2)]
         convolved = jnp.concatenate(rows, axis=0).T
         span = slice(hi * LANE, (hi + 1) * LANE)
         out_ref[span, :] = queries_ref[span, :] * (convolved + direct_ref[span, :])
+        if hi == 0:
+            direct = head_ref[16:17, 0:LANE] * mix_of(filtered)
+            out_ref[0:8, :] = filtered[:, :LANE] * (convolved[0:8, :] + direct)
 
 
 def exchange(value, axis):
@@ -297,19 +310,14 @@
         compiler_params=GRANT,
     )(far(projected), far(short_taps), far(long_filter.reshape(HIGH, LANE)))
     earlier = lax.ppermute(tail, EVERY, [(s, s + 1) for s in range(count - 1)])
-    queries, direct = pl.pallas_call(
+    queries, direct, head = pl.pallas_call(
         plan_kernel,
-        out_specs=(near, near),
-        out_shape=(plane, plane),
+        out_specs=(near, near, near),
+        out_shape=(plane, plane, pltpu.VMEM((24, wide), jnp.float32)),
         scratch_shapes=[pltpu.VMEM((seg + 8, wide), jnp.float32)],
         name="plan",
         compiler_params=GRANT,
-    )(
-        far(projected),
-        pltpu.with_memory_space_constraint(earlier, pltpu.VMEM),
-        far(short_taps),
-        far(skip_gain.reshape(1, channels)),
-    )
+    )(far(projected), far(short_taps), far(skip_gain.reshape(1, channels)))
     arrived = exchange(packed, FIRST)
     ahead = on_chip(
         ahead_kernel,
@@ -344,12 +352,12 @@
     home = exchange(behind, FIRST)
     return pl.pallas_call(
         gate_kernel,
-        in_specs=[near] * 3,
+        in_specs=[near] * 5,
         out_shape=jax.ShapeDtypeStruct((seg, channels), jnp.float32),
-        scratch_shapes=[pltpu.VMEM((8 * PEERS, LANE), jnp.float32)],
+        scratch_shapes=[pltpu.VMEM((8 * PEERS, LANE), jnp.float32), pltpu.VMEM((16, wide), jnp.float32)],
         name="gate",
         compiler_params=GRANT,
-    )(*[pltpu.with_memory_space_constraint(arg, pltpu.VMEM) for arg in (queries, direct, home)])
+    )(*[pltpu.with_memory_space_constraint(arg, pltpu.VMEM) for arg in (queries, direct, head, earlier, home)])
 
 
 def solution(mesh):

time: 79.2 us -> 79.3 us (level)
    ppermute x1, waiting for transfers between devices: 6.35 us -> 4.81 us  [on_device(): earlier = lax.ppermute(tail, EVERY, [(s, s + 1) for s in range(count - 1)])]
    all_to_all x1, waiting for transfers between devices: 0.98 us -> 2.51 us  [exchange(): return lax.all_to_all(value, axis, split_axis=0, concat_axis=0, tiled=True)]
where the time goes in v8:
time: 79.3 us; the launch traced here: 78.9 us
  blocking collectives  55.3 us (70%)
  Pallas kernels  8.74 us (11%)
  starting transfers between devices  7.43 us (9%)
  waiting for transfers between devices  7.32 us (9%)
    all_to_all x3, blocking collectives, exchange(): return lax.all_to_all(value, axis, split_axis=0, concat_axis=0, tiled=True)  55.3 us
    pallas_call x3, Pallas kernels, on_chip(): pl.pallas_call(kernel, in_specs=[near] * len(args), out_specs=tuple((near...  4.89 us
    ppermute x1, waiting for transfers between devices, on_device(): earlier = lax.ppermute(tail, EVERY, [(s, s + 1) for s in range(count - 1)])  4.81 us
    all_to_all x1, starting transfers between devices, exchange(): return lax.all_to_all(value, axis, split_axis=0, concat_axis=0, tiled=True)  4.62 us
    ppermute x1, starting transfers between devices, on_device(): earlier = lax.ppermute(tail, EVERY, [(s, s + 1) for s in range(count - 1)])  2.81 us
    all_to_all x1, waiting for transfers between devices, exchange(): return lax.all_to_all(value, axis, split_axis=0, concat_axis=0, tiled=True)  2.51 us
  transfers between devices with their start and end apart: 2, of which 2 were waited for; matrix products, arithmetic and copies ran while one was open for 0% of the time, Pallas kernels for 2%

profile of v8, /device:TPU:1, one launch (start us, length us, event | category | flops | bytes accessed | tf_op | source)
XLA Modules:
  0.0 78.9 jit_solution(6524330808721058502)
XLA Ops:
  0.0 0.0 copy-start.1
  0.0 1.5 %pack.1 = (bf16[64,4,512]{2,1,0:T(4,128)(2,1)S(1)}, bf16[8,384]{1,0:T(8,128)(2,1)S(1)}) custom-call(bf16[512,384]{1,0:T(8,128)(2,1)} %projected_ref.3, f32[3,384]{1,0:T(4,128)} %taps_ref.3, bf16[4,128]{1,0:T(4,128)(2,1)} %bitcast.3), custom_call_target="tpu_custom_call" | custom-call | flops 200000000 | bytes 800000 | tf_op jit(solution)/shard_map/pack/pallas_call | solution.py:303
  1.5 0.0 copy-start
  1.5 29.9 %all_to_all.20.data_ref = bf16[64,4,512]{2,1,0:T(4,128)(2,1)S(1)} all-to-all(bf16[64,4,512]{2,1,0:T(4,128)(2,1)S(1)} %get-tuple-element.14), channel_id=1, replica_groups=mesh['zh'=2,'y'=8,'core'=2,'x'=4,'zl'=4] {'zh','y','zl'}, dimensions={0} | all-to-all | bytes 524288 | tf_op jit(solution)/shard_map/all_to_all | solution.py:275
  31.4 0.0 copy-done.1
  31.4 0.0 copy-done
  31.4 0.0 copy-start.4
  31.4 1.1 %ahead.1 = bf16[8,16,1664]{2,1,0:T(8,128)(2,1)S(1)} custom-call(bf16[64,4,512]{2,1,0:T(4,128)(2,1)S(1)} %all_to_all.20.data_ref, bf16[2,768,256]{2,1,0:T(8,128)(2,1)S(1)} %copy-done.1, f32[320,256]{1,0:T(8,128)S(1)} %copy-done), custom_call_target="tpu_custom_call" | custom-call | tf_op jit(solution)/shard_map/ahead/pallas_call | solution.py:284
  32.5 0.0 copy-start.3
  32.5 15.7 %all_to_all.21.data_ref = bf16[8,16,1664]{2,1,0:T(8,128)(2,1)S(1)} all-to-all(bf16[8,16,1664]{2,1,0:T(8,128)(2,1)S(1)} %ahead.1), channel_id=1, replica_groups=mesh['zh'=2,'y'=8,'core'=2,'x'=4,'zl'=4] {'core','x'}, dimensions={0} | all-to-all | bytes 851968 | tf_op jit(solution)/shard_map/all_to_all | solution.py:275
  48.3 0.0 copy-done.4
  48.3 0.0 copy-done.3
  48.3 0.0 copy-start.2
  48.3 2.4 %blocks.1 = bf16[8,16,1024]{2,1,0:T(8,128)(2,1)S(1)} custom-call(bf16[8,16,1664]{2,1,0:T(8,128)(2,1)S(1)} %all_to_all.21.data_ref, bf16[2,512,256]{2,1,0:T(8,128)(2,1)S(1)} %copy-done.4, bf16[2,256,512]{2,1,0:T(8,128)(2,1)S(1)} %copy-done.3, f32[320,256]{1,0:T(8,128)S(1)} %copy-done), custom_call_target="tpu_custom_call" | custom-call | tf_op jit(solution)/shard_map/blocks/pallas_call | solution.py:284
  50.7 9.7 %all_to_all.22.data_ref = bf16[8,16,1024]{2,1,0:T(8,128)(2,1)S(1)} all-to-all(bf16[8,16,1024]{2,1,0:T(8,128)(2,1)S(1)} %blocks.1), channel_id=1, replica_groups=mesh['zh'=2,'y'=8,'core'=2,'x'=4,'zl'=4] {'core','x'}, dimensions={0} | all-to-all | bytes 524288 | tf_op jit(solution)/shard_map/all_to_all | solution.py:275
  60.4 0.0 copy-done.2
  60.4 1.4 %behind.1 = bf16[64,8,128]{2,1,0:T(8,128)(2,1)} custom-call(bf16[8,16,1024]{2,1,0:T(8,128)(2,1)S(1)} %all_to_all.22.data_ref, bf16[2,256,768]{2,1,0:T(8,128)(2,1)S(1)} %copy-done.2, f32[320,256]{1,0:T(8,128)S(1)} %copy-done), custom_call_target="tpu_custom_call" | custom-call | tf_op jit(solution)/shard_map/behind/pallas_call | solution.py:284
  61.8 4.6 %all-to-all-start.3 = ((bf16[64,8,128]{2,1,0:T(8,128)(2,1)}), bf16[64,8,128]{2,1,0:T(8,128)(2,1)S(1)}, u32[]{:S(2)}, u32[]{:S(2)}) async-start(bf16[64,8,128]{2,1,0:T(8,128)(2,1)} %behind.1), calls=%async_computation.3 | async-start | bytes 262144 | tf_op jit(solution)/shard_map/all_to_all | solution.py:275
  66.4 2.8 %collective-permute-start = (bf16[8,384]{1,0:T(8,128)(2,1)S(1)}, bf16[8,384]{1,0:T(8,128)(2,1)S(1)}, u32[]{:S(2)}, u32[]{:S(2)}) collective-permute-start(bf16[8,384]{1,0:T(8,128)(2,1)S(1)} %get-tuple-element.13), channel_id=1, source_target_pairs={{0,1},{1,2},{2,3},{3,4},{4,5},{5,6},{6,7},{7,8},{8,9},{9,10},{10,1... | collective-permute-start | bytes 18440 | tf_op jit(solution)/shard_map/ppermute | solution.py:312
  69.2 1.5 %plan.1 = (f32[512,128]{1,0:T(8,128)S(1)}, f32[512,128]{1,0:T(8,128)S(1)}, f32[24,384]{1,0:T(8,128)S(1)}) custom-call(bf16[512,384]{1,0:T(8,128)(2,1)} %projected_ref.3, f32[3,384]{1,0:T(4,128)} %taps_ref.3, f32[1,128]{1,0:T(1,128)} %bitcast.2), custom_call_target="tpu_custom_call" | custom-call | tf_op jit(solution)/shard_map/plan/pallas_call | solution.py:313
  70.7 4.8 %collective-permute-done.earlier_ref = bf16[8,384]{1,0:T(8,128)(2,1)S(1)} collective-permute-done((bf16[8,384]{1,0:T(8,128)(2,1)S(1)}, bf16[8,384]{1,0:T(8,128)(2,1)S(1)}, u32[]{:S(2)}, u32[]{:S(2)}) %collective-permute-start) | collective-permute-done | bytes 6176 | tf_op jit(solution)/shard_map/ppermute | solution.py:312
  75.6 2.5 %all-to-all-done.3.data_ref = bf16[64,8,128]{2,1,0:T(8,128)(2,1)S(1)} async-done(((bf16[64,8,128]{2,1,0:T(8,128)(2,1)}), bf16[64,8,128]{2,1,0:T(8,128)(2,1)S(1)}, u32[]{:S(2)}, u32[]{:S(2)}) %all-to-all-start.3) | async-done | bytes 131104 | tf_op jit(solution)/shard_map/all_to_all | solution.py:275
  78.1 0.9 %gate.1 = f32[512,128]{1,0:T(8,128)} custom-call(f32[512,128]{1,0:T(8,128)S(1)} %get-tuple-element.10.queries_ref, f32[512,128]{1,0:T(8,128)S(1)} %get-tuple-element.11.direct_ref, f32[24,384]{1,0:T(8,128)S(1)} %get-tuple-element.12.head_ref, bf16[8,384]{1,0:T(8,128)(2,1)S(1)} %collective-permute-done.earlier_ref, ...), custom_call_target="tpu_custom_call" | custom-call | tf_op jit(solution)/shard_map/gate/pallas_call | solution.py:353
Async XLA Ops:
  0.0 31.4 %copy-start.1 = (bf16[2,768,256]{2,1,0:T(8,128)(2,1)S(1)}, bf16[2,768,256]{2,1,0:T(8,128)(2,1)}, u32[]{:S(2)}) copy-start(bf16[2,768,256]{2,1,0:T(8,128)(2,1)} %constant.10.clone.table_ref) | copy-start | bytes 2359300
  1.5 29.9 %copy-start = (f32[320,256]{1,0:T(8,128)S(1)}, f32[320,256]{1,0:T(8,128)}, u32[]{:S(2)}) copy-start(f32[320,256]{1,0:T(8,128)} %constant.11.clone.twist_ref) | copy-start | bytes 983044
  31.4 16.9 %copy-start.4 = (bf16[2,512,256]{2,1,0:T(8,128)(2,1)S(1)}, bf16[2,512,256]{2,1,0:T(8,128)(2,1)}, u32[]{:S(2)}) copy-start(bf16[2,512,256]{2,1,0:T(8,128)(2,1)} %constant.12.clone.over_ref) | copy-start | bytes 1572868
  32.5 15.7 %copy-start.3 = (bf16[2,256,512]{2,1,0:T(8,128)(2,1)S(1)}, bf16[2,256,512]{2,1,0:T(8,128)(2,1)}, u32[]{:S(2)}) copy-start(bf16[2,256,512]{2,1,0:T(8,128)(2,1)} %constant.13.clone.under_ref) | copy-start | bytes 1572868
  48.3 12.2 %copy-start.2 = (bf16[2,256,768]{2,1,0:T(8,128)(2,1)S(1)}, bf16[2,256,768]{2,1,0:T(8,128)(2,1)}, u32[]{:S(2)}) copy-start(bf16[2,256,768]{2,1,0:T(8,128)(2,1)} %constant.14.clone.table_ref) | copy-start | bytes 2359300
  61.8 16.3 %all-to-all-start.3 = ((bf16[64,8,128]{2,1,0:T(8,128)(2,1)}), bf16[64,8,128]{2,1,0:T(8,128)(2,1)S(1)}, u32[]{:S(2)}, u32[]{:S(2)}) async-start(bf16[64,8,128]{2,1,0:T(8,128)(2,1)} %behind.1), calls=%async_computation.3 | async-start | bytes 262144 | tf_op jit(solution)/shard_map/all_to_all | solution.py:275
  66.4 9.2 %collective-permute-start = (bf16[8,384]{1,0:T(8,128)(2,1)S(1)}, bf16[8,384]{1,0:T(8,128)(2,1)S(1)}, u32[]{:S(2)}, u32[]{:S(2)}) collective-permute-start(bf16[8,384]{1,0:T(8,128)(2,1)S(1)} %get-tuple-element.13), channel_id=1, source_target_pairs={{0,1},{1,2},{2,3},{3,4},{4,5},{5,6},{6,7},{7,8},{8,9},{9,10},{10,1... | collective-permute-start | bytes 18440 | tf_op jit(solution)/shard_map/ppermute | solution.py:312

commit v9 on v8

--- a/solution.py
+++ b/solution.py
@@ -90,23 +90,40 @@
     return total
 
 
-def pack_kernel(projected_ref, taps_ref, filter_ref, out_ref, tail_ref, ext_ref, rows_ref):
+def mix_of(filtered):
+    mixture = (filtered[:, LANE : 2 * LANE] * filtered[:, 2 * LANE :]).astype(jnp.bfloat16)
+    return mixture.astype(jnp.float32)
+
+
+def pack_kernel(
+    projected_ref, taps_ref, gain_ref, filter_ref, out_ref, queries_ref, direct_ref, head_ref, ext_ref, rows_ref
+):
     seg = projected_ref.shape[0]
-    tail_ref[...] = projected_ref[seg - 8 :, :]
-    ext_ref[0:8, :] = jnp.zeros((8, 2 * LANE), jnp.float32)
-    ext_ref[8 : 8 + seg, :] = projected_ref[:, LANE:].astype(jnp.float32)
+    ext_ref[0:8, :] = jnp.zeros((8, 3 * LANE), jnp.float32)
+    ext_ref[8 : 8 + seg, :] = projected_ref[...].astype(jnp.float32)
+    head_ref[0:8, :] = ext_ref[8:16, :LANE]
+    head_ref[8:11, :] = taps_ref[:, :LANE]
+    head_ref[16:17, :] = gain_ref[...]
+    filtered = short_filter(ext_ref, taps_ref[...], seg)
+    mixture = mix_of(filtered)
+    queries_ref[...] = filtered[:, :LANE]
+    direct = gain_ref[...] * mixture
+    direct_ref[...] = direct
+    direct_ref[0:8, :] = jnp.where(lax.broadcasted_iota(jnp.int32, (8, LANE), 0) < 2, 0.0, direct[0:8, :])
     taps = taps_ref[:, LANE:]
-    filtered = short_filter(ext_ref, taps, seg)
-    mixture = (filtered[:, :LANE] * filtered[:, LANE:]).astype(jnp.bfloat16).astype(jnp.float32)
-    last = ext_ref[7 + seg : 8 + seg, :]
-    carry = taps[1:2, :] * last + taps[2:3, :] * ext_ref[6 + seg : 7 + seg, :]
-    ends = [filtered[0:1, :], filtered[1:2, :], carry, taps[2:3, :] * last]
+    last = ext_ref[7 + seg : 8 + seg, LANE:]
+    carry = taps[1:2, :] * last + taps[2:3, :] * ext_ref[6 + seg : 7 + seg, LANE:]
+    ends = [filtered[0:1, LANE:], filtered[1:2, LANE:], carry, taps[2:3, :] * last]
     ends = [ends[row][:, half * LANE : (half + 1) * LANE] for row, half in EDGE]
     upper, lower = cut(jnp.concatenate(ends, axis=0))
     pad = jnp.zeros((LANE - 16, LANE), jnp.float32)
     flipped = jnp.concatenate([upper.astype(jnp.float32), lower.astype(jnp.float32), pad], axis=0).T
     lane = lax.broadcasted_iota(jnp.int32, (PEERS, LANE), 1)
     edges = jnp.where(lane < 16, flipped[:PEERS, :], pltpu.roll(flipped[PEERS:, :], 16, 1))
+    extra = [edges]
+    for row in (6 + seg, 7 + seg):
+        extra.append(jnp.broadcast_to(ext_ref[row : row + 1, :LANE], (PEERS, LANE)))
+    extra.append(jnp.zeros((PEERS, LANE), jnp.float32))
     for hi in range(HIGH):
         flipped = mixture[hi * LANE : (hi + 1) * LANE, :].T
         where = pl.ds(hi, PEERS, stride=HIGH)
@@ -114,26 +131,9 @@
             rows_ref[ch, where, :] = flipped[ch * PEERS : (ch + 1) * PEERS, :]
         taps_row = filter_ref[hi : hi + 1, :].astype(jnp.float32)
         rows_ref[2, where, :] = jnp.broadcast_to(taps_row, (PEERS, LANE))
-        rows_ref[3, where, :] = edges
+        rows_ref[3, where, :] = extra[hi]
     for at in range(4):
         out_ref[:, :, at * LANE : (at + 1) * LANE] = rows_ref[at].reshape(PEERS, HIGH, LANE).astype(jnp.bfloat16)
-
-
-def plan_kernel(projected_ref, taps_ref, gain_ref, queries_ref, direct_ref, head_ref, ext_ref):
-    seg = projected_ref.shape[0]
-    ext_ref[0:8, :] = jnp.zeros((8, 3 * LANE), jnp.float32)
-    ext_ref[8 : 8 + seg, :] = projected_ref[...].astype(jnp.float32)
-    head_ref[0:8, :] = ext_ref[8:16, :]
-    head_ref[8:11, :] = taps_ref[...]
-    head_ref[16:17, 0:LANE] = gain_ref[...]
-    filtered = short_filter(ext_ref, taps_ref[...], seg)
-    queries_ref[...] = filtered[:, :LANE]
-    direct_ref[...] = gain_ref[...] * mix_of(filtered)
-
-
-def mix_of(filtered):
-    mixture = (filtered[:, LANE : 2 * LANE] * filtered[:, 2 * LANE :]).astype(jnp.bfloat16)
-    return mixture.astype(jnp.float32)
 
 
 def back(value, lanes):
@@ -149,7 +149,7 @@
     return (total * back(total, 2)).astype(jnp.bfloat16).astype(jnp.float32)
 
 
-def ahead_kernel(data_ref, table_ref, twist_ref, out_ref, rows_ref, edge_ref):
+def ahead_kernel(data_ref, table_ref, twist_ref, out_ref, mix_ref, tail_ref, rows_ref, edge_ref):
     for at in range(4):
         block = data_ref[:, :, at * LANE : (at + 1) * LANE].astype(jnp.float32)
         rows_ref[at] = block.reshape(256, LANE)
@@ -161,12 +161,24 @@
     inside = (lax.broadcasted_iota(jnp.int32, (PEERS, LANE), 0) & (RUN - 1)) != 0
     lane = lax.broadcasted_iota(jnp.int32, (PEERS, LANE), 1)
     mixture = jnp.where(inside, mixture, 0.0)
+    mix_ref[...] = mixture
+    own_place = lax.axis_index(FIRST)
+    before = jnp.maximum(own_place - 1, 0)
+    ending = jnp.where(lax.axis_index(SECOND) == PLANES - 1, before, jnp.minimum(own_place + RUN - 1, PEERS - 1))
+    for row in range(2):
+        tail_ref[row : row + 1, :] = rows_ref[3, pl.ds(before * HIGH + 1 + row, 1), :]
+    relay = []
+    for row in range(2):
+        value = rows_ref[3, pl.ds(ending * HIGH + 1 + row, 1), :]
+        relay += [pltpu.roll(value, LANE // 2, 1), value]
+    relay = jnp.concatenate(relay + [jnp.zeros((BLOCKS - 4, LANE), jnp.float32)], axis=0)
     for ch in range(2):
         fresh = back(mixture, 16 * ch) if ch else mixture
         rows_ref[ch, where, :] = jnp.where(lane < 2, fresh, rows_ref[ch, where, :])
     opening = edge_ref[pl.ds(0, BLOCKS, stride=RUN), :]
     closing = edge_ref[pl.ds(RUN - 1, BLOCKS, stride=RUN), :]
-    outside = jnp.where((lane[:BLOCKS, :] & 4) == 0, opening, closing).astype(jnp.bfloat16)
+    outside = jnp.where((lane[:BLOCKS, :] & 4) == 0, opening, closing)
+    outside = jnp.where(lane[:BLOCKS, :] < LANE // 2, outside, relay).astype(jnp.bfloat16)
     for plane in range(PLANES):
         out_ref[plane, :, KQ * 3 * 256 :] = outside
     data = jnp.concatenate([rows_ref[0], rows_ref[1], rows_ref[2]], axis=1).astype(jnp.bfloat16)
@@ -185,13 +197,22 @@
             out_ref[:, :, at : at + 256] = value.astype(jnp.bfloat16)
 
 
-def blocks_kernel(data_ref, over_ref, under_ref, twist_ref, out_ref):
-    omega = twist_ref[pl.ds(256 + 8 * lax.axis_index(SECOND), 8), :LANE]
+def blocks_kernel(data_ref, over_ref, under_ref, twist_ref, out_ref, start_ref, tail_ref, open_ref):
+    plane = lax.axis_index(SECOND)
+    omega = twist_ref[pl.ds(256 + 8 * plane, 8), :LANE]
+    before = jnp.where(plane == 0, PLANES - 1, plane - 1)
+    relay = data_ref[pl.ds(before, 1), :, KQ * 3 * 256 :].astype(jnp.float32).reshape(BLOCKS, LANE)
+    low = lax.broadcasted_iota(jnp.int32, (1, LANE), 1) < LANE // 2
+    for row in range(2):
+        value = pltpu.roll(relay[2 * row : 2 * row + 1, :], LANE // 2, 1)
+        tail_ref[row : row + 1, :] = jnp.where(low, value, relay[2 * row + 1 : 2 * row + 2, :])
     owns = [whole_edges(data_ref[plane, :, KQ * 3 * 256 :].astype(jnp.float32)) for plane in range(PLANES)]
     row = lax.broadcasted_iota(jnp.int32, (BLOCKS, LANE), 0)
     wrapped = jnp.where(row == 0, 0.0, pltpu.roll(back(owns[PLANES - 1], 4), 1, 0))
     befores = [wrapped] + [back(own, 4) for own in owns[:-1]]
     opening = jnp.concatenate([rows_of(own, before) for own, before in zip(owns, befores)], axis=0)
+    open_ref[...] = opening
+    start_ref[...] = open_ref[pl.ds(pl.multiple_of(plane * BLOCKS, BLOCKS), BLOCKS), :]
 
     def piece(kq, number, part):
         at = ((kq * 3 + number) * 2 + part) * LANE
@@ -231,7 +252,7 @@
                 out_ref[:, :, to : to + LANE] = value.astype(jnp.bfloat16)
 
 
-def behind_kernel(data_ref, table_ref, twist_ref, out_ref, rows_ref):
+def behind_kernel(data_ref, table_ref, twist_ref, head_ref, mix_ref, start_ref, out_ref, rows_ref, fix_ref):
     columns = []
     for ch in range(2):
         parts = [[], []]
@@ -253,13 +274,33 @@
         for ch in range(2):
             where = pl.ds(ch * HIGH + hi, PEERS, stride=8)
             rows_ref[where, :] = value[hi * PEERS : (hi + 1) * PEERS, ch * LANE : (ch + 1) * LANE]
+    fix_ref[...] = mix_ref[...]
+    fix_ref[pl.ds(0, BLOCKS, stride=RUN), :] = start_ref[...]
+    mixture = fix_ref[...]
+    lane = lax.broadcasted_iota(jnp.int32, (PEERS, LANE), 1)
+    for ch in range(2):
+        mine = lane[0:1, :] == ch * PEERS + lax.axis_index(FIRST)
+        gain = jnp.sum(jnp.where(mine, head_ref[16:17, :], 0.0), axis=1, keepdims=True)
+        fresh = back(mixture, 16 * ch) if ch else mixture
+        where = pl.ds(ch * HIGH, PEERS, stride=8)
+        rows_ref[where, :] = rows_ref[where, :] + jnp.where(lane < 2, gain * fresh, 0.0)
     out_ref[...] = rows_ref[...].reshape(PEERS, 8, LANE).astype(jnp.bfloat16)
 
 
-def gate_kernel(queries_ref, direct_ref, head_ref, earlier_ref, data_ref, out_ref, rows_ref, ext_ref):
-    ext_ref[0:8, :] = earlier_ref[...].astype(jnp.float32)
+def gate_kernel(queries_ref, direct_ref, head_ref, inside_ref, outside_ref, data_ref, out_ref, rows_ref, ext_ref):
+    place = lax.axis_index(FIRST)
+    ext_ref[0:8, :] = jnp.zeros((8, LANE), jnp.float32)
+
+    @pl.when((place & (RUN - 1)) != 0)
+    def _():
+        ext_ref[6:8, :] = inside_ref[0:2, :]
+
+    @pl.when(((place & (RUN - 1)) == 0) & (place + lax.axis_index(SECOND) > 0))
+    def _():
+        ext_ref[6:8, :] = outside_ref[0:2, :]
+
     ext_ref[8:16, :] = head_ref[0:8, :]
-    filtered = short_filter(ext_ref, head_ref[8:11, :], 8)
+    queries = short_filter(ext_ref, head_ref[8:11, :], 8)
     rows_ref[...] = data_ref[...].astype(jnp.float32).reshape(8 * PEERS, LANE)
     for hi in range(HIGH):
         rows = [rows_ref[pl.ds(ch * HIGH + hi, PEERS, stride=8), :] for ch in range(2)]
@@ -267,8 +308,7 @@
         span = slice(hi * LANE, (hi + 1) * LANE)
         out_ref[span, :] = queries_ref[span, :] * (convolved + direct_ref[span, :])
         if hi == 0:
-            direct = head_ref[16:17, 0:LANE] * mix_of(filtered)
-            out_ref[0:8, :] = filtered[:, :LANE] * (convolved[0:8, :] + direct)
+            out_ref[0:8, :] = queries * (convolved[0:8, :] + direct_ref[0:8, :])
 
 
 def exchange(value, axis):
@@ -295,44 +335,50 @@
 def on_device(projected, short_taps, skip_gain, long_filter):
     seg, wide = projected.shape
     channels = skip_gain.shape[0]
-    count = lax.axis_size(EVERY)
     near = pl.BlockSpec(memory_space=pltpu.VMEM)
     ahead_table, behind_table, over, under, twist = tables()
     plane = pltpu.VMEM((seg, channels), jnp.float32)
     stack = pltpu.VMEM((4, 256, LANE), jnp.float32)
-    packed, tail = pl.pallas_call(
+    corner = pltpu.VMEM((8, LANE), jnp.float32)
+    wide_rows = pltpu.VMEM((PEERS, LANE), jnp.float32)
+    packed, queries, direct, head = pl.pallas_call(
         pack_kernel,
-        out_specs=(near, near),
-        out_shape=(pltpu.VMEM((PEERS, HIGH, 4 * LANE), jnp.bfloat16), pltpu.VMEM((8, wide), jnp.bfloat16)),
-        scratch_shapes=[pltpu.VMEM((seg + 8, 2 * LANE), jnp.float32), stack],
+        out_specs=(near,) * 4,
+        out_shape=(
+            pltpu.VMEM((PEERS, HIGH, 4 * LANE), jnp.bfloat16),
+            plane,
+            plane,
+            pltpu.VMEM((24, LANE), jnp.float32),
+        ),
+        scratch_shapes=[pltpu.VMEM((seg + 8, wide), jnp.float32), stack],
         name="pack",
         cost_estimate=pl.CostEstimate(flops=200000000, bytes_accessed=800000, transcendentals=0),
         compiler_params=GRANT,
-    )(far(projected), far(short_taps), far(long_filter.reshape(HIGH, LANE)))
-    earlier = lax.ppermute(tail, EVERY, [(s, s + 1) for s in range(count - 1)])
-    queries, direct, head = pl.pallas_call(
-        plan_kernel,
-        out_specs=(near, near, near),
-        out_shape=(plane, plane, pltpu.VMEM((24, wide), jnp.float32)),
-        scratch_shapes=[pltpu.VMEM((seg + 8, wide), jnp.float32)],
-        name="plan",
-        compiler_params=GRANT,
-    )(far(projected), far(short_taps), far(skip_gain.reshape(1, channels)))
+    )(
+        far(projected),
+        far(short_taps),
+        far(skip_gain.reshape(1, channels)),
+        far(long_filter.reshape(HIGH, LANE)),
+    )
     arrived = exchange(packed, FIRST)
-    ahead = on_chip(
+    ahead, mixture, inside = on_chip(
         ahead_kernel,
-        (pltpu.VMEM((PLANES, BLOCKS, KQ * 3 * 256 + LANE), jnp.bfloat16),),
-        [stack, pltpu.VMEM((PEERS, LANE), jnp.float32)],
+        (pltpu.VMEM((PLANES, BLOCKS, KQ * 3 * 256 + LANE), jnp.bfloat16), wide_rows, corner),
+        [stack, wide_rows],
         "ahead",
         arrived,
         ahead_table,
         twist,
     )
     lined = exchange(ahead, SECOND)
-    blocks = on_chip(
+    blocks, start, outside = on_chip(
         blocks_kernel,
-        (pltpu.VMEM((PLANES, BLOCKS, KQ * 2 * 256), jnp.bfloat16),),
-        [],
+        (
+            pltpu.VMEM((PLANES, BLOCKS, KQ * 2 * 256), jnp.bfloat16),
+            pltpu.VMEM((BLOCKS, LANE), jnp.float32),
+            corner,
+        ),
+        [pltpu.VMEM((128, LANE), jnp.float32)],
         "blocks",
         lined,
         over,
@@ -343,21 +389,24 @@
     behind = on_chip(
         behind_kernel,
         (pltpu.VMEM((PEERS, 8, LANE), jnp.bfloat16),),
-        [pltpu.VMEM((8 * PEERS, LANE), jnp.float32)],
+        [pltpu.VMEM((8 * PEERS, LANE), jnp.float32), wide_rows],
         "behind",
         returned,
         behind_table,
         twist,
+        head,
+        mixture,
+        start,
     )
     home = exchange(behind, FIRST)
     return pl.pallas_call(
         gate_kernel,
-        in_specs=[near] * 5,
+        in_specs=[near] * 6,
         out_shape=jax.ShapeDtypeStruct((seg, channels), jnp.float32),
-        scratch_shapes=[pltpu.VMEM((8 * PEERS, LANE), jnp.float32), pltpu.VMEM((16, wide), jnp.float32)],
+        scratch_shapes=[pltpu.VMEM((8 * PEERS, LANE), jnp.float32), pltpu.VMEM((16, LANE), jnp.float32)],
         name="gate",
         compiler_params=GRANT,
-    )(*[pltpu.with_memory_space_constraint(arg, pltpu.VMEM) for arg in (queries, direct, head, earlier, home)])
+    )(*[pltpu.with_memory_space_constraint(arg, pltpu.VMEM) for arg in (queries, direct, head, inside, outside, home)])
 
 
 def solution(mesh):

time: 79.3 us -> 77.9 us (0.982)
  blocking collectives: 55.3 us -> 70.8 us
  starting transfers between devices: 7.43 us -> 0 us
  waiting for transfers between devices: 7.32 us -> 0 us
  Pallas kernels: 8.74 us -> 6.76 us
    all_to_all x3 -> x4, blocking collectives: 55.3 us -> 70.8 us  [exchange(): return lax.all_to_all(value, axis, split_axis=0, concat_axis=0, tiled=True)]
    ppermute x1 -> x0, waiting for transfers between devices: 4.81 us -> none  [on_device(): earlier = lax.ppermute(tail, EVERY, [(s, s + 1) for s in range(count - 1)])]
    all_to_all x1 -> x0, starting transfers between devices: 4.62 us -> none  [exchange(): return lax.all_to_all(value, axis, split_axis=0, concat_axis=0, tiled=True)]
    ppermute x1 -> x0, starting transfers between devices: 2.81 us -> none  [on_device(): earlier = lax.ppermute(tail, EVERY, [(s, s + 1) for s in range(count - 1)])]
    all_to_all x1 -> x0, waiting for transfers between devices: 2.51 us -> none  [exchange(): return lax.all_to_all(value, axis, split_axis=0, concat_axis=0, tiled=True)]
    pallas_call x3 -> x2, Pallas kernels: 3.85 us -> 2.46 us  [the longest x1 1.59 us: on_device(): pl.pallas_call(pack_kernel, out_specs=(near,) * 4, out_shape=(pltpu.VMEM(...]
  transfers between devices with their start and end apart: 2 -> 0, of which waited for: 2 -> 0; matrix products, arithmetic and copies ran while one was open for 0% -> 0% of each run, Pallas kernels for 2% -> 0%
where the time goes in v9:
time: 77.9 us; the launch traced here: 77.7 us
  blocking collectives  70.8 us (91%)
  Pallas kernels  6.76 us (9%)
    all_to_all x4, blocking collectives, exchange(): return lax.all_to_all(value, axis, split_axis=0, concat_axis=0, tiled=True)  70.8 us
    pallas_call x3, Pallas kernels, on_chip(): pl.pallas_call(kernel, in_specs=[near] * len(args), out_specs=tuple((near...  4.3 us
    pallas_call x1, Pallas kernels, on_device(): pl.pallas_call(pack_kernel, out_specs=(near,) * 4, out_shape=(pltpu.VMEM(...  1.59 us

profile of v9, /device:TPU:1, one launch (start us, length us, event | category | flops | bytes accessed | tf_op | source)
XLA Modules:
  0.0 77.7 jit_solution(9536070232374083401)
XLA Ops:
  0.0 0.0 copy-start.2
  0.0 1.6 %pack.1 = (bf16[64,4,512]{2,1,0:T(4,128)(2,1)S(1)}, f32[512,128]{1,0:T(8,128)S(1)}, f32[512,128]{1,0:T(8,128)S(1)}, f32[24,128]{1,0:T(8,128)S(1)}) custom-call(bf16[512,384]{1,0:T(8,128)(2,1)} %projected_ref.1, f32[3,384]{1,0:T(4,128)} %taps_ref.1, f32[1,128]{1,0:T(1,128)} %bitcast.3, bf16[4,128]{1,0:T(4,128)(2,1)} %bitcast.2), custom_call_target="tpu_custom_call" | custom-call | flops 200000000 | bytes 800000 | tf_op jit(solution)/shard_map/pack/pallas_call | solution.py:344
  1.6 0.0 copy-start
  1.6 29.9 %all_to_all.20.data_ref = bf16[64,4,512]{2,1,0:T(4,128)(2,1)S(1)} all-to-all(bf16[64,4,512]{2,1,0:T(4,128)(2,1)S(1)} %get-tuple-element.18), channel_id=1, replica_groups=mesh['zh'=2,'y'=8,'core'=2,'x'=4,'zl'=4] {'zh','y','zl'}, dimensions={0} | all-to-all | bytes 524288 | tf_op jit(solution)/shard_map/all_to_all | solution.py:315
  31.5 0.0 copy-done.2
  31.5 0.0 copy-done
  31.5 0.0 copy-start.4
  31.5 1.2 %ahead.1 = (bf16[8,16,1664]{2,1,0:T(8,128)(2,1)S(1)}, f32[64,128]{1,0:T(8,128)S(1)}, f32[8,128]{1,0:T(8,128)S(1)}) custom-call(bf16[64,4,512]{2,1,0:T(4,128)(2,1)S(1)} %all_to_all.20.data_ref, bf16[2,768,256]{2,1,0:T(8,128)(2,1)S(1)} %copy-done.2, f32[320,256]{1,0:T(8,128)S(1)} %copy-done), custom_call_target="tpu_custom_call" | custom-call | tf_op jit(solution)/shard_map/ahead/pallas_call | solution.py:324
  32.7 0.0 copy-start.3
  32.7 15.7 %all_to_all.21.data_ref = bf16[8,16,1664]{2,1,0:T(8,128)(2,1)S(1)} all-to-all(bf16[8,16,1664]{2,1,0:T(8,128)(2,1)S(1)} %get-tuple-element.20), channel_id=1, replica_groups=mesh['zh'=2,'y'=8,'core'=2,'x'=4,'zl'=4] {'core','x'}, dimensions={0} | all-to-all | bytes 851968 | tf_op jit(solution)/shard_map/all_to_all | solution.py:315
  48.4 0.0 copy-done.4
  48.4 0.0 copy-done.3
  48.4 0.0 copy-start.1
  48.4 2.4 %blocks.1 = (bf16[8,16,1024]{2,1,0:T(8,128)(2,1)S(1)}, f32[16,128]{1,0:T(8,128)S(1)}, f32[8,128]{1,0:T(8,128)S(1)}) custom-call(bf16[8,16,1664]{2,1,0:T(8,128)(2,1)S(1)} %all_to_all.21.data_ref, bf16[2,512,256]{2,1,0:T(8,128)(2,1)S(1)} %copy-done.4, bf16[2,256,512]{2,1,0:T(8,128)(2,1)S(1)} %copy-done.3, f32[320,256]{1,0:T(8,128)S(1)} %copy-done), custom_call_target="tpu_custom_call" | custom-call | tf_op jit(solution)/shard_map/blocks/pallas_call | solution.py:324
  50.8 9.7 %all_to_all.22.data_ref = bf16[8,16,1024]{2,1,0:T(8,128)(2,1)S(1)} all-to-all(bf16[8,16,1024]{2,1,0:T(8,128)(2,1)S(1)} %get-tuple-element.22), channel_id=1, replica_groups=mesh['zh'=2,'y'=8,'core'=2,'x'=4,'zl'=4] {'core','x'}, dimensions={0} | all-to-all | bytes 524288 | tf_op jit(solution)/shard_map/all_to_all | solution.py:315
  60.6 0.0 copy-done.1
  60.6 0.7 behind.1
  61.3 15.5 %all_to_all.23.data_ref = bf16[64,8,128]{2,1,0:T(8,128)(2,1)S(1)} all-to-all(bf16[64,8,128]{2,1,0:T(8,128)(2,1)S(1)} %behind.1), channel_id=1, replica_groups=mesh['zh'=2,'y'=8,'core'=2,'x'=4,'zl'=4] {'zh','y','zl'}, dimensions={0} | all-to-all | bytes 262144 | tf_op jit(solution)/shard_map/all_to_all | solution.py:315
  76.8 0.9 %gate.1 = f32[512,128]{1,0:T(8,128)} custom-call(f32[512,128]{1,0:T(8,128)S(1)} %get-tuple-element.15.queries_ref, f32[512,128]{1,0:T(8,128)S(1)} %get-tuple-element.16.direct_ref, f32[24,128]{1,0:T(8,128)S(1)} %get-tuple-element.17.head_ref, f32[8,128]{1,0:T(8,128)S(1)} %get-tuple-element.19.inside_ref, f32[8,128]{1,0:T(8,128)S(1)} %get-tuple-element.21.outside_ref, ...), custom_call_target="tpu_custom_call" | custom-call | tf_op jit(solution)/shard_map/gate/pallas_call | solution.py:402
Async XLA Ops:
  0.0 31.5 %copy-start.2 = (bf16[2,768,256]{2,1,0:T(8,128)(2,1)S(1)}, bf16[2,768,256]{2,1,0:T(8,128)(2,1)}, u32[]{:S(2)}) copy-start(bf16[2,768,256]{2,1,0:T(8,128)(2,1)} %constant.10.clone.table_ref) | copy-start | bytes 2359300
  1.6 29.9 %copy-start = (f32[320,256]{1,0:T(8,128)S(1)}, f32[320,256]{1,0:T(8,128)}, u32[]{:S(2)}) copy-start(f32[320,256]{1,0:T(8,128)} %constant.11.clone.twist_ref) | copy-start | bytes 983044
  31.5 16.9 %copy-start.4 = (bf16[2,512,256]{2,1,0:T(8,128)(2,1)S(1)}, bf16[2,512,256]{2,1,0:T(8,128)(2,1)}, u32[]{:S(2)}) copy-start(bf16[2,512,256]{2,1,0:T(8,128)(2,1)} %constant.12.clone.over_ref) | copy-start | bytes 1572868
  32.7 15.7 %copy-start.3 = (bf16[2,256,512]{2,1,0:T(8,128)(2,1)S(1)}, bf16[2,256,512]{2,1,0:T(8,128)(2,1)}, u32[]{:S(2)}) copy-start(bf16[2,256,512]{2,1,0:T(8,128)(2,1)} %constant.13.clone.under_ref) | copy-start | bytes 1572868
  48.4 12.2 %copy-start.1 = (bf16[2,256,768]{2,1,0:T(8,128)(2,1)S(1)}, bf16[2,256,768]{2,1,0:T(8,128)(2,1)}, u32[]{:S(2)}) copy-start(bf16[2,256,768]{2,1,0:T(8,128)(2,1)} %constant.14.clone.table_ref) | copy-start | bytes 2359300

commit v10 on v9

--- a/solution.py
+++ b/solution.py
@@ -218,38 +218,32 @@
         at = ((kq * 3 + number) * 2 + part) * LANE
         return data_ref[:, :, at : at + LANE].astype(jnp.float32).reshape(128, LANE)
 
-    columns = []
+    taps = [jnp.concatenate([piece(kq, 2, 0), piece(kq, 2, 1)], axis=0) for kq in range(KQ)]
+    taps = jnp.concatenate(taps, axis=1).astype(jnp.bfloat16)
+    taps = mxu(over_ref[0], taps) + mxu(over_ref[1], taps)
     for ch in range(2):
         zeroth = jnp.broadcast_to(opening[:, 16 * ch : 16 * ch + 1], (128, LANE))
         second = jnp.broadcast_to(opening[:, 16 * ch + 1 : 16 * ch + 2], (128, LANE))
+        columns = []
         for kq in range(KQ):
             real = piece(kq, ch, 0) + (zeroth + second * omega[2 * kq : 2 * kq + 1, :])
             imag = piece(kq, ch, 1) + second * omega[2 * kq + 1 : 2 * kq + 2, :]
             columns.append(jnp.concatenate([real, imag], axis=0))
-    upper, lower = cut(jnp.concatenate(columns, axis=1))
-    waves = mxu(over_ref[0], upper) + (mxu(over_ref[0], lower) + mxu(over_ref[1], upper))
-    taps = [jnp.concatenate([piece(kq, 2, 0), piece(kq, 2, 1)], axis=0) for kq in range(KQ)]
-    taps = jnp.concatenate(taps, axis=1).astype(jnp.bfloat16)
-    taps = mxu(over_ref[0], taps) + mxu(over_ref[1], taps)
-    products = []
-    for kq in range(KQ):
-        tap_real = taps[:WAVES, kq * LANE : (kq + 1) * LANE]
-        tap_imag = taps[WAVES:, kq * LANE : (kq + 1) * LANE]
-        for ch in range(2):
-            at = (ch * KQ + kq) * LANE
-            real = waves[:WAVES, at : at + LANE]
-            imag = waves[WAVES:, at : at + LANE]
-            both = [real * tap_real - imag * tap_imag, real * tap_imag + imag * tap_real]
-            products.append(jnp.concatenate(both, axis=0))
-    upper, lower = cut(jnp.concatenate(products, axis=1))
-    sums = mxu(under_ref[0], upper) + (mxu(under_ref[0], lower) + mxu(under_ref[1], upper))
-    for kq in range(KQ):
-        for ch in range(2):
-            for part in range(2):
-                at = (kq * 2 + ch) * LANE
-                value = sums[part * 128 : (part + 1) * 128, at : at + LANE].reshape(PLANES, BLOCKS, LANE)
-                to = (at // LANE * 2 + part) * LANE
-                out_ref[:, :, to : to + LANE] = value.astype(jnp.bfloat16)
+        upper, lower = cut(jnp.concatenate(columns, axis=1))
+        real, imag = (
+            mxu(over_ref[0, half], upper) + (mxu(over_ref[0, half], lower) + mxu(over_ref[1, half], upper))
+            for half in (slice(0, WAVES), slice(WAVES, 2 * WAVES))
+        )
+        tap_real, tap_imag = taps[:WAVES], taps[WAVES:]
+        both = [real * tap_real - imag * tap_imag, real * tap_imag + imag * tap_real]
+        upper, lower = cut(jnp.concatenate(both, axis=0))
+        for part in range(2):
+            half = slice(part * 128, (part + 1) * 128)
+            sums = mxu(under_ref[0, half], upper) + (mxu(under_ref[0, half], lower) + mxu(under_ref[1, half], upper))
+            for kq in range(KQ):
+                value = sums[:, kq * LANE : (kq + 1) * LANE]
+                to = ((kq * 2 + ch) * 2 + part) * LANE
+                out_ref[:, :, to : to + LANE] = value.reshape(PLANES, BLOCKS, LANE).astype(jnp.bfloat16)
 
 
 def behind_kernel(data_ref, table_ref, twist_ref, head_ref, mix_ref, start_ref, out_ref, rows_ref, fix_ref):

time: 77.9 us -> 77.2 us (level)
  no operation moved by 1% of the time
where the time goes in v10:
time: 77.2 us; the launch traced here: 77 us
  blocking collectives  70.8 us (92%)
  Pallas kernels  6.08 us (8%)
    all_to_all x4, blocking collectives, exchange(): return lax.all_to_all(value, axis, split_axis=0, concat_axis=0, tiled=True)  70.8 us
    pallas_call x3, Pallas kernels, on_chip(): pl.pallas_call(kernel, in_specs=[near] * len(args), out_specs=tuple((near...  3.62 us
    pallas_call x1, Pallas kernels, on_device(): pl.pallas_call(pack_kernel, out_specs=(near,) * 4, out_shape=(pltpu.VMEM(...  1.59 us

profile of v10, /device:TPU:1, one launch (start us, length us, event | category | flops | bytes accessed | tf_op | source)
XLA Modules:
  0.0 77.0 jit_solution(2565134760781942404)
XLA Ops:
  0.0 0.0 copy-start.2
  0.0 1.6 %pack.1 = (bf16[64,4,512]{2,1,0:T(4,128)(2,1)S(1)}, f32[512,128]{1,0:T(8,128)S(1)}, f32[512,128]{1,0:T(8,128)S(1)}, f32[24,128]{1,0:T(8,128)S(1)}) custom-call(bf16[512,384]{1,0:T(8,128)(2,1)} %projected_ref.1, f32[3,384]{1,0:T(4,128)} %taps_ref.1, f32[1,128]{1,0:T(1,128)} %bitcast.3, bf16[4,128]{1,0:T(4,128)(2,1)} %bitcast.2), custom_call_target="tpu_custom_call" | custom-call | flops 200000000 | bytes 800000 | tf_op jit(solution)/shard_map/pack/pallas_call | solution.py:338
  1.6 0.0 copy-start
  1.6 29.9 %all_to_all.20.data_ref = bf16[64,4,512]{2,1,0:T(4,128)(2,1)S(1)} all-to-all(bf16[64,4,512]{2,1,0:T(4,128)(2,1)S(1)} %get-tuple-element.18), channel_id=1, replica_groups=mesh['zh'=2,'y'=8,'core'=2,'x'=4,'zl'=4] {'zh','y','zl'}, dimensions={0} | all-to-all | bytes 524288 | tf_op jit(solution)/shard_map/all_to_all | solution.py:309
  31.5 0.0 copy-done.2
  31.5 0.0 copy-done
  31.5 0.0 copy-start.4
  31.5 1.2 %ahead.1 = (bf16[8,16,1664]{2,1,0:T(8,128)(2,1)S(1)}, f32[64,128]{1,0:T(8,128)S(1)}, f32[8,128]{1,0:T(8,128)S(1)}) custom-call(bf16[64,4,512]{2,1,0:T(4,128)(2,1)S(1)} %all_to_all.20.data_ref, bf16[2,768,256]{2,1,0:T(8,128)(2,1)S(1)} %copy-done.2, f32[320,256]{1,0:T(8,128)S(1)} %copy-done), custom_call_target="tpu_custom_call" | custom-call | tf_op jit(solution)/shard_map/ahead/pallas_call | solution.py:318
  32.7 0.0 copy-start.3
  32.7 15.7 %all_to_all.21.data_ref = bf16[8,16,1664]{2,1,0:T(8,128)(2,1)S(1)} all-to-all(bf16[8,16,1664]{2,1,0:T(8,128)(2,1)S(1)} %get-tuple-element.20), channel_id=1, replica_groups=mesh['zh'=2,'y'=8,'core'=2,'x'=4,'zl'=4] {'core','x'}, dimensions={0} | all-to-all | bytes 851968 | tf_op jit(solution)/shard_map/all_to_all | solution.py:309
  48.4 0.0 copy-done.4
  48.4 0.0 copy-done.3
  48.4 0.0 copy-start.1
  48.4 1.7 %blocks.1 = (bf16[8,16,1024]{2,1,0:T(8,128)(2,1)S(1)}, f32[16,128]{1,0:T(8,128)S(1)}, f32[8,128]{1,0:T(8,128)S(1)}) custom-call(bf16[8,16,1664]{2,1,0:T(8,128)(2,1)S(1)} %all_to_all.21.data_ref, bf16[2,512,256]{2,1,0:T(8,128)(2,1)S(1)} %copy-done.4, bf16[2,256,512]{2,1,0:T(8,128)(2,1)S(1)} %copy-done.3, f32[320,256]{1,0:T(8,128)S(1)} %copy-done), custom_call_target="tpu_custom_call" | custom-call | tf_op jit(solution)/shard_map/blocks/pallas_call | solution.py:318
  50.2 9.8 %all_to_all.22.data_ref = bf16[8,16,1024]{2,1,0:T(8,128)(2,1)S(1)} all-to-all(bf16[8,16,1024]{2,1,0:T(8,128)(2,1)S(1)} %get-tuple-element.22), channel_id=1, replica_groups=mesh['zh'=2,'y'=8,'core'=2,'x'=4,'zl'=4] {'core','x'}, dimensions={0} | all-to-all | bytes 524288 | tf_op jit(solution)/shard_map/all_to_all | solution.py:309
  59.9 0.0 copy-done.1
  59.9 0.7 behind.1
  60.6 15.5 %all_to_all.23.data_ref = bf16[64,8,128]{2,1,0:T(8,128)(2,1)S(1)} all-to-all(bf16[64,8,128]{2,1,0:T(8,128)(2,1)S(1)} %behind.1), channel_id=1, replica_groups=mesh['zh'=2,'y'=8,'core'=2,'x'=4,'zl'=4] {'zh','y','zl'}, dimensions={0} | all-to-all | bytes 262144 | tf_op jit(solution)/shard_map/all_to_all | solution.py:309
  76.1 0.9 %gate.1 = f32[512,128]{1,0:T(8,128)} custom-call(f32[512,128]{1,0:T(8,128)S(1)} %get-tuple-element.15.queries_ref, f32[512,128]{1,0:T(8,128)S(1)} %get-tuple-element.16.direct_ref, f32[24,128]{1,0:T(8,128)S(1)} %get-tuple-element.17.head_ref, f32[8,128]{1,0:T(8,128)S(1)} %get-tuple-element.19.inside_ref, f32[8,128]{1,0:T(8,128)S(1)} %get-tuple-element.21.outside_ref, ...), custom_call_target="tpu_custom_call" | custom-call | tf_op jit(solution)/shard_map/gate/pallas_call | solution.py:396
Async XLA Ops:
  0.0 31.5 %copy-start.2 = (bf16[2,768,256]{2,1,0:T(8,128)(2,1)S(1)}, bf16[2,768,256]{2,1,0:T(8,128)(2,1)}, u32[]{:S(2)}) copy-start(bf16[2,768,256]{2,1,0:T(8,128)(2,1)} %constant.10.clone.table_ref) | copy-start | bytes 2359300
  1.6 29.9 %copy-start = (f32[320,256]{1,0:T(8,128)S(1)}, f32[320,256]{1,0:T(8,128)}, u32[]{:S(2)}) copy-start(f32[320,256]{1,0:T(8,128)} %constant.11.clone.twist_ref) | copy-start | bytes 983044
  31.5 16.9 %copy-start.4 = (bf16[2,512,256]{2,1,0:T(8,128)(2,1)S(1)}, bf16[2,512,256]{2,1,0:T(8,128)(2,1)}, u32[]{:S(2)}) copy-start(bf16[2,512,256]{2,1,0:T(8,128)(2,1)} %constant.12.clone.over_ref) | copy-start | bytes 1572868
  32.7 15.7 %copy-start.3 = (bf16[2,256,512]{2,1,0:T(8,128)(2,1)S(1)}, bf16[2,256,512]{2,1,0:T(8,128)(2,1)}, u32[]{:S(2)}) copy-start(bf16[2,256,512]{2,1,0:T(8,128)(2,1)} %constant.13.clone.under_ref) | copy-start | bytes 1572868
  48.4 11.5 %copy-start.1 = (bf16[2,256,768]{2,1,0:T(8,128)(2,1)S(1)}, bf16[2,256,768]{2,1,0:T(8,128)(2,1)}, u32[]{:S(2)}) copy-start(bf16[2,256,768]{2,1,0:T(8,128)(2,1)} %constant.14.clone.table_ref) | copy-start | bytes 2359300

commit v11 on v10

--- a/solution.py
+++ b/solution.py
@@ -150,9 +150,32 @@
 
 
 def ahead_kernel(data_ref, table_ref, twist_ref, out_ref, mix_ref, tail_ref, rows_ref, edge_ref):
-    for at in range(4):
-        block = data_ref[:, :, at * LANE : (at + 1) * LANE].astype(jnp.float32)
-        rows_ref[at] = block.reshape(256, LANE)
+    def lines_of(at):
+        return data_ref[:, :, at * LANE : (at + 1) * LANE].astype(jnp.float32).reshape(256, LANE)
+
+    cos = twist_ref[:256, :LANE]
+    sin = twist_ref[:256, LANE:]
+
+    def transform(numbers, data):
+        data = data.astype(jnp.bfloat16)
+        waves = [
+            mxu(table_ref[0, half, :], data) + mxu(table_ref[1, half, :], data)
+            for half in (slice(0, 256), slice(256, 512))
+        ]
+        for spot, number in enumerate(numbers):
+            real = waves[0][:, spot * LANE : (spot + 1) * LANE]
+            imag = waves[1][:, spot * LANE : (spot + 1) * LANE]
+            upper, lower = cut(jnp.concatenate([real * cos - imag * sin, real * sin + imag * cos], axis=1))
+            second = table_ref[0, 512:, :]
+            for kq in range(KQ):
+                rows = slice(kq * 128, (kq + 1) * 128)
+                freq = mxu(upper[rows], second) + (mxu(lower[rows], second) + mxu(upper[rows], table_ref[1, 512:, :]))
+                at = (kq * 3 + number) * 256
+                out_ref[:, :, at : at + 256] = freq.reshape(PLANES, BLOCKS, 256).astype(jnp.bfloat16)
+
+    transform((2,), lines_of(2))
+    for at in (0, 1, 3):
+        rows_ref[at] = lines_of(at)
     where = pl.ds(0, PEERS, stride=HIGH)
     edges = rows_ref[3, where, :]
     edge_ref[...] = edges
@@ -181,23 +204,19 @@
     outside = jnp.where(lane[:BLOCKS, :] < LANE // 2, outside, relay).astype(jnp.bfloat16)
     for plane in range(PLANES):
         out_ref[plane, :, KQ * 3 * 256 :] = outside
-    data = jnp.concatenate([rows_ref[0], rows_ref[1], rows_ref[2]], axis=1).astype(jnp.bfloat16)
-    waves = mxu(table_ref[0, :512, :], data) + mxu(table_ref[1, :512, :], data)
-    cos = twist_ref[:256, :LANE]
-    sin = twist_ref[:256, LANE:]
-    for number in range(3):
-        real = waves[:256, number * LANE : (number + 1) * LANE]
-        imag = waves[256:, number * LANE : (number + 1) * LANE]
-        upper, lower = cut(jnp.concatenate([real * cos - imag * sin, real * sin + imag * cos], axis=1))
-        second = table_ref[0, 512:, :]
-        freq = mxu(upper, second) + (mxu(lower, second) + mxu(upper, table_ref[1, 512:, :]))
-        for kq in range(KQ):
-            at = (kq * 3 + number) * 256
-            value = freq[kq * 128 : (kq + 1) * 128, :].reshape(PLANES, BLOCKS, 256)
-            out_ref[:, :, at : at + 256] = value.astype(jnp.bfloat16)
+    transform((0, 1), jnp.concatenate([rows_ref[0], rows_ref[1]], axis=1))
 
 
 def blocks_kernel(data_ref, over_ref, under_ref, twist_ref, out_ref, start_ref, tail_ref, open_ref):
+    def piece(kq, number, part):
+        at = ((kq * 3 + number) * 2 + part) * LANE
+        return data_ref[:, :, at : at + LANE].astype(jnp.float32).reshape(128, LANE)
+
+    taps = [jnp.concatenate([piece(kq, 2, 0), piece(kq, 2, 1)], axis=0) for kq in range(KQ)]
+    taps = jnp.concatenate(taps, axis=1).astype(jnp.bfloat16)
+    tap_real, tap_imag = (
+        mxu(over_ref[0, half], taps) + mxu(over_ref[1, half], taps) for half in (slice(0, WAVES), slice(WAVES, 2 * WAVES))
+    )
     plane = lax.axis_index(SECOND)
     omega = twist_ref[pl.ds(256 + 8 * plane, 8), :LANE]
     before = jnp.where(plane == 0, PLANES - 1, plane - 1)
@@ -214,13 +233,6 @@
     open_ref[...] = opening
     start_ref[...] = open_ref[pl.ds(pl.multiple_of(plane * BLOCKS, BLOCKS), BLOCKS), :]
 
-    def piece(kq, number, part):
-        at = ((kq * 3 + number) * 2 + part) * LANE
-        return data_ref[:, :, at : at + LANE].astype(jnp.float32).reshape(128, LANE)
-
-    taps = [jnp.concatenate([piece(kq, 2, 0), piece(kq, 2, 1)], axis=0) for kq in range(KQ)]
-    taps = jnp.concatenate(taps, axis=1).astype(jnp.bfloat16)
-    taps = mxu(over_ref[0], taps) + mxu(over_ref[1], taps)
     for ch in range(2):
         zeroth = jnp.broadcast_to(opening[:, 16 * ch : 16 * ch + 1], (128, LANE))
         second = jnp.broadcast_to(opening[:, 16 * ch + 1 : 16 * ch + 2], (128, LANE))
@@ -234,7 +246,6 @@
             mxu(over_ref[0, half], upper) + (mxu(over_ref[0, half], lower) + mxu(over_ref[1, half], upper))
             for half in (slice(0, WAVES), slice(WAVES, 2 * WAVES))
         )
-        tap_real, tap_imag = taps[:WAVES], taps[WAVES:]
         both = [real * tap_real - imag * tap_imag, real * tap_imag + imag * tap_real]
         upper, lower = cut(jnp.concatenate(both, axis=0))
         for part in range(2):

time: 77.2 us -> 76.9 us (level)
  no operation moved by 1% of the time
where the time goes in v11:
time: 76.9 us; the launch traced here: 76.7 us
  blocking collectives  70.8 us (92%)
  Pallas kernels  5.77 us (8%)
    all_to_all x4, blocking collectives, exchange(): return lax.all_to_all(value, axis, split_axis=0, concat_axis=0, tiled=True)  70.8 us
    pallas_call x3, Pallas kernels, on_chip(): pl.pallas_call(kernel, in_specs=[near] * len(args), out_specs=tuple((near...  3.31 us
    pallas_call x1, Pallas kernels, on_device(): pl.pallas_call(pack_kernel, out_specs=(near,) * 4, out_shape=(pltpu.VMEM(...  1.59 us

profile of v11, /device:TPU:1, one launch (start us, length us, event | category | flops | bytes accessed | tf_op | source)
XLA Modules:
  0.0 76.7 jit_solution(1818346991806207359)
XLA Ops:
  0.0 0.0 copy-start.2
  0.0 1.6 %pack.1 = (bf16[64,4,512]{2,1,0:T(4,128)(2,1)S(1)}, f32[512,128]{1,0:T(8,128)S(1)}, f32[512,128]{1,0:T(8,128)S(1)}, f32[24,128]{1,0:T(8,128)S(1)}) custom-call(bf16[512,384]{1,0:T(8,128)(2,1)} %projected_ref.1, f32[3,384]{1,0:T(4,128)} %taps_ref.1, f32[1,128]{1,0:T(1,128)} %bitcast.3, bf16[4,128]{1,0:T(4,128)(2,1)} %bitcast.2), custom_call_target="tpu_custom_call" | custom-call | flops 200000000 | bytes 800000 | tf_op jit(solution)/shard_map/pack/pallas_call | solution.py:349
  1.6 0.0 copy-start
  1.6 29.9 %all_to_all.20.data_ref = bf16[64,4,512]{2,1,0:T(4,128)(2,1)S(1)} all-to-all(bf16[64,4,512]{2,1,0:T(4,128)(2,1)S(1)} %get-tuple-element.18), channel_id=1, replica_groups=mesh['zh'=2,'y'=8,'core'=2,'x'=4,'zl'=4] {'zh','y','zl'}, dimensions={0} | all-to-all | bytes 524288 | tf_op jit(solution)/shard_map/all_to_all | solution.py:320
  31.5 0.0 copy-done.2
  31.5 0.0 copy-done
  31.5 0.0 copy-start.4
  31.5 1.0 %ahead.1 = (bf16[8,16,1664]{2,1,0:T(8,128)(2,1)S(1)}, f32[64,128]{1,0:T(8,128)S(1)}, f32[8,128]{1,0:T(8,128)S(1)}) custom-call(bf16[64,4,512]{2,1,0:T(4,128)(2,1)S(1)} %all_to_all.20.data_ref, bf16[2,768,256]{2,1,0:T(8,128)(2,1)S(1)} %copy-done.2, f32[320,256]{1,0:T(8,128)S(1)} %copy-done), custom_call_target="tpu_custom_call" | custom-call | tf_op jit(solution)/shard_map/ahead/pallas_call | solution.py:329
  32.5 0.0 copy-start.3
  32.5 15.7 %all_to_all.21.data_ref = bf16[8,16,1664]{2,1,0:T(8,128)(2,1)S(1)} all-to-all(bf16[8,16,1664]{2,1,0:T(8,128)(2,1)S(1)} %get-tuple-element.20), channel_id=1, replica_groups=mesh['zh'=2,'y'=8,'core'=2,'x'=4,'zl'=4] {'core','x'}, dimensions={0} | all-to-all | bytes 851968 | tf_op jit(solution)/shard_map/all_to_all | solution.py:320
  48.2 0.0 copy-done.4
  48.2 0.0 copy-done.3
  48.2 0.0 copy-start.1
  48.2 1.6 %blocks.1 = (bf16[8,16,1024]{2,1,0:T(8,128)(2,1)S(1)}, f32[16,128]{1,0:T(8,128)S(1)}, f32[8,128]{1,0:T(8,128)S(1)}) custom-call(bf16[8,16,1664]{2,1,0:T(8,128)(2,1)S(1)} %all_to_all.21.data_ref, bf16[2,512,256]{2,1,0:T(8,128)(2,1)S(1)} %copy-done.4, bf16[2,256,512]{2,1,0:T(8,128)(2,1)S(1)} %copy-done.3, f32[320,256]{1,0:T(8,128)S(1)} %copy-done), custom_call_target="tpu_custom_call" | custom-call | tf_op jit(solution)/shard_map/blocks/pallas_call | solution.py:329
  49.8 9.8 %all_to_all.22.data_ref = bf16[8,16,1024]{2,1,0:T(8,128)(2,1)S(1)} all-to-all(bf16[8,16,1024]{2,1,0:T(8,128)(2,1)S(1)} %get-tuple-element.22), channel_id=1, replica_groups=mesh['zh'=2,'y'=8,'core'=2,'x'=4,'zl'=4] {'core','x'}, dimensions={0} | all-to-all | bytes 524288 | tf_op jit(solution)/shard_map/all_to_all | solution.py:320
  59.6 0.0 copy-done.1
  59.6 0.7 behind.1
  60.3 15.5 %all_to_all.23.data_ref = bf16[64,8,128]{2,1,0:T(8,128)(2,1)S(1)} all-to-all(bf16[64,8,128]{2,1,0:T(8,128)(2,1)S(1)} %behind.1), channel_id=1, replica_groups=mesh['zh'=2,'y'=8,'core'=2,'x'=4,'zl'=4] {'zh','y','zl'}, dimensions={0} | all-to-all | bytes 262144 | tf_op jit(solution)/shard_map/all_to_all | solution.py:320
  75.8 0.9 %gate.1 = f32[512,128]{1,0:T(8,128)} custom-call(f32[512,128]{1,0:T(8,128)S(1)} %get-tuple-element.15.queries_ref, f32[512,128]{1,0:T(8,128)S(1)} %get-tuple-element.16.direct_ref, f32[24,128]{1,0:T(8,128)S(1)} %get-tuple-element.17.head_ref, f32[8,128]{1,0:T(8,128)S(1)} %get-tuple-element.19.inside_ref, f32[8,128]{1,0:T(8,128)S(1)} %get-tuple-element.21.outside_ref, ...), custom_call_target="tpu_custom_call" | custom-call | tf_op jit(solution)/shard_map/gate/pallas_call | solution.py:407
Async XLA Ops:
  0.0 31.5 %copy-start.2 = (bf16[2,768,256]{2,1,0:T(8,128)(2,1)S(1)}, bf16[2,768,256]{2,1,0:T(8,128)(2,1)}, u32[]{:S(2)}) copy-start(bf16[2,768,256]{2,1,0:T(8,128)(2,1)} %constant.10.clone.table_ref) | copy-start | bytes 2359300
  1.6 29.9 %copy-start = (f32[320,256]{1,0:T(8,128)S(1)}, f32[320,256]{1,0:T(8,128)}, u32[]{:S(2)}) copy-start(f32[320,256]{1,0:T(8,128)} %constant.11.clone.twist_ref) | copy-start | bytes 983044
  31.5 16.7 %copy-start.4 = (bf16[2,512,256]{2,1,0:T(8,128)(2,1)S(1)}, bf16[2,512,256]{2,1,0:T(8,128)(2,1)}, u32[]{:S(2)}) copy-start(bf16[2,512,256]{2,1,0:T(8,128)(2,1)} %constant.12.clone.over_ref) | copy-start | bytes 1572868
  32.5 15.7 %copy-start.3 = (bf16[2,256,512]{2,1,0:T(8,128)(2,1)S(1)}, bf16[2,256,512]{2,1,0:T(8,128)(2,1)}, u32[]{:S(2)}) copy-start(bf16[2,256,512]{2,1,0:T(8,128)(2,1)} %constant.13.clone.under_ref) | copy-start | bytes 1572868
  48.2 11.4 %copy-start.1 = (bf16[2,256,768]{2,1,0:T(8,128)(2,1)S(1)}, bf16[2,256,768]{2,1,0:T(8,128)(2,1)}, u32[]{:S(2)}) copy-start(bf16[2,256,768]{2,1,0:T(8,128)(2,1)} %constant.14.clone.table_ref) | copy-start | bytes 2359300

commit v12 on v11

--- a/solution.py
+++ b/solution.py
@@ -83,10 +83,10 @@
     return upper, (value - upper.astype(jnp.float32)).astype(jnp.bfloat16)
 
 
-def short_filter(ext_ref, taps, seg):
-    total = taps[0:1, :] * ext_ref[8 : 8 + seg, :]
+def short_filter(ext_ref, taps, seg, start=0):
+    total = taps[0:1, :] * ext_ref[8 + start : 8 + start + seg, :]
     for tap in range(1, taps.shape[0]):
-        total = total + taps[tap : tap + 1, :] * ext_ref[8 - tap : 8 - tap + seg, :]
+        total = total + taps[tap : tap + 1, :] * ext_ref[8 + start - tap : 8 + start - tap + seg, :]
     return total
 
 
@@ -96,24 +96,39 @@
 
 
 def pack_kernel(
-    projected_ref, taps_ref, gain_ref, filter_ref, out_ref, queries_ref, direct_ref, head_ref, ext_ref, rows_ref
+    projected_ref, taps_ref, gain_ref, filter_ref, out_ref, queries_ref, direct_ref, head_ref, ext_ref, rows_ref, near_ref, sems
 ):
     seg = projected_ref.shape[0]
+    copies = []
+    for hi in range(HIGH):
+        span = pl.ds(hi * LANE, LANE)
+        copies.append(pltpu.make_async_copy(projected_ref.at[span, :], near_ref.at[span, :], sems.at[hi]))
+        copies[hi].start()
     ext_ref[0:8, :] = jnp.zeros((8, 3 * LANE), jnp.float32)
-    ext_ref[8 : 8 + seg, :] = projected_ref[...].astype(jnp.float32)
-    head_ref[0:8, :] = ext_ref[8:16, :LANE]
     head_ref[8:11, :] = taps_ref[:, :LANE]
     head_ref[16:17, :] = gain_ref[...]
-    filtered = short_filter(ext_ref, taps_ref[...], seg)
-    mixture = mix_of(filtered)
-    queries_ref[...] = filtered[:, :LANE]
-    direct = gain_ref[...] * mixture
-    direct_ref[...] = direct
-    direct_ref[0:8, :] = jnp.where(lax.broadcasted_iota(jnp.int32, (8, LANE), 0) < 2, 0.0, direct[0:8, :])
+    for hi in range(HIGH):
+        span = slice(hi * LANE, (hi + 1) * LANE)
+        copies[hi].wait()
+        ext_ref[8 + hi * LANE : 8 + (hi + 1) * LANE, :] = near_ref[span, :].astype(jnp.float32)
+        filtered = short_filter(ext_ref, taps_ref[...], LANE, hi * LANE)
+        mixture = mix_of(filtered)
+        queries_ref[span, :] = filtered[:, :LANE]
+        direct = gain_ref[...] * mixture
+        direct_ref[span, :] = direct
+        if hi == 0:
+            direct_ref[0:8, :] = jnp.where(lax.broadcasted_iota(jnp.int32, (8, LANE), 0) < 2, 0.0, direct[0:8, :])
+        flipped = mixture.T
+        where = pl.ds(hi, PEERS, stride=HIGH)
+        for ch in range(2):
+            rows_ref[ch, where, :] = flipped[ch * PEERS : (ch + 1) * PEERS, :]
+        taps_row = filter_ref[hi : hi + 1, :].astype(jnp.float32)
+        rows_ref[2, where, :] = jnp.broadcast_to(taps_row, (PEERS, LANE))
     taps = taps_ref[:, LANE:]
     last = ext_ref[7 + seg : 8 + seg, LANE:]
     carry = taps[1:2, :] * last + taps[2:3, :] * ext_ref[6 + seg : 7 + seg, LANE:]
-    ends = [filtered[0:1, LANE:], filtered[1:2, LANE:], carry, taps[2:3, :] * last]
+    opening = short_filter(ext_ref, taps_ref[...], 8)
+    ends = [opening[0:1, LANE:], opening[1:2, LANE:], carry, taps[2:3, :] * last]
     ends = [ends[row][:, half * LANE : (half + 1) * LANE] for row, half in EDGE]
     upper, lower = cut(jnp.concatenate(ends, axis=0))
     pad = jnp.zeros((LANE - 16, LANE), jnp.float32)
@@ -125,13 +140,8 @@
         extra.append(jnp.broadcast_to(ext_ref[row : row + 1, :LANE], (PEERS, LANE)))
     extra.append(jnp.zeros((PEERS, LANE), jnp.float32))
     for hi in range(HIGH):
-        flipped = mixture[hi * LANE : (hi + 1) * LANE, :].T
-        where = pl.ds(hi, PEERS, stride=HIGH)
-        for ch in range(2):
-            rows_ref[ch, where, :] = flipped[ch * PEERS : (ch + 1) * PEERS, :]
-        taps_row = filter_ref[hi : hi + 1, :].astype(jnp.float32)
-        rows_ref[2, where, :] = jnp.broadcast_to(taps_row, (PEERS, LANE))
-        rows_ref[3, where, :] = extra[hi]
+        rows_ref[3, pl.ds(hi, PEERS, stride=HIGH), :] = extra[hi]
+    head_ref[0:8, :] = ext_ref[8:16, :LANE]
     for at in range(4):
         out_ref[:, :, at * LANE : (at + 1) * LANE] = rows_ref[at].reshape(PEERS, HIGH, LANE).astype(jnp.bfloat16)
 
@@ -355,7 +365,13 @@
             plane,
             pltpu.VMEM((24, LANE), jnp.float32),
         ),
-        scratch_shapes=[pltpu.VMEM((seg + 8, wide), jnp.float32), stack],
+        in_specs=[pl.BlockSpec(memory_space=pltpu.HBM), near, near, near],
+        scratch_shapes=[
+            pltpu.VMEM((seg + 8, wide), jnp.float32),
+            stack,
+            pltpu.VMEM((seg, wide), jnp.bfloat16),
+            pltpu.SemaphoreType.DMA((HIGH,)),
+        ],
         name="pack",
         cost_estimate=pl.CostEstimate(flops=200000000, bytes_accessed=800000, transcendentals=0),
         compiler_params=GRANT,

time: 76.9 us -> 77.8 us (1.012)
  Pallas kernels: 5.77 us -> 6.6 us
    pallas_call x1, Pallas kernels: 1.59 us -> 2.41 us  [on_device(): pl.pallas_call(pack_kernel, out_specs=(near,) * 4, out_shape=(pltpu.VMEM(...]
where the time goes in v12:
time: 77.8 us; the launch traced here: 77.5 us
  blocking collectives  70.8 us (91%)
  Pallas kernels  6.6 us (8%)
    all_to_all x4, blocking collectives, exchange(): return lax.all_to_all(value, axis, split_axis=0, concat_axis=0, tiled=True)  70.8 us
    pallas_call x3, Pallas kernels, on_chip(): pl.pallas_call(kernel, in_specs=[near] * len(args), out_specs=tuple((near...  3.32 us
    pallas_call x1, Pallas kernels, on_device(): pl.pallas_call(pack_kernel, out_specs=(near,) * 4, out_shape=(pltpu.VMEM(...  2.41 us

profile of v12, /device:TPU:1, one launch (start us, length us, event | category | flops | bytes accessed | tf_op | source)
XLA Modules:
  0.0 77.5 jit_solution(5936484202657452938)
XLA Ops:
  0.0 0.0 copy-start.2
  0.0 2.4 %pack.1 = (bf16[64,4,512]{2,1,0:T(4,128)(2,1)S(1)}, f32[512,128]{1,0:T(8,128)S(1)}, f32[512,128]{1,0:T(8,128)S(1)}, f32[24,128]{1,0:T(8,128)S(1)}) custom-call(bf16[512,384]{1,0:T(8,128)(2,1)} %projected_ref.1, f32[3,384]{1,0:T(4,128)} %taps_ref.1, f32[1,128]{1,0:T(1,128)} %bitcast.3, bf16[4,128]{1,0:T(4,128)(2,1)} %bitcast.2), custom_call_target="tpu_custom_call" | custom-call | flops 200000000 | bytes 800000 | tf_op jit(solution)/shard_map/pack/pallas_call | solution.py:359
  2.4 0.0 copy-start
  2.4 29.9 %all_to_all.20.data_ref = bf16[64,4,512]{2,1,0:T(4,128)(2,1)S(1)} all-to-all(bf16[64,4,512]{2,1,0:T(4,128)(2,1)S(1)} %get-tuple-element.18), channel_id=1, replica_groups=mesh['zh'=2,'y'=8,'core'=2,'x'=4,'zl'=4] {'zh','y','zl'}, dimensions={0} | all-to-all | bytes 524288 | tf_op jit(solution)/shard_map/all_to_all | solution.py:330
  32.3 0.0 copy-done.2
  32.3 0.0 copy-done
  32.3 0.0 copy-start.4
  32.3 1.0 %ahead.1 = (bf16[8,16,1664]{2,1,0:T(8,128)(2,1)S(1)}, f32[64,128]{1,0:T(8,128)S(1)}, f32[8,128]{1,0:T(8,128)S(1)}) custom-call(bf16[64,4,512]{2,1,0:T(4,128)(2,1)S(1)} %all_to_all.20.data_ref, bf16[2,768,256]{2,1,0:T(8,128)(2,1)S(1)} %copy-done.2, f32[320,256]{1,0:T(8,128)S(1)} %copy-done), custom_call_target="tpu_custom_call" | custom-call | tf_op jit(solution)/shard_map/ahead/pallas_call | solution.py:339
  33.3 0.0 copy-start.3
  33.3 15.7 %all_to_all.21.data_ref = bf16[8,16,1664]{2,1,0:T(8,128)(2,1)S(1)} all-to-all(bf16[8,16,1664]{2,1,0:T(8,128)(2,1)S(1)} %get-tuple-element.20), channel_id=1, replica_groups=mesh['zh'=2,'y'=8,'core'=2,'x'=4,'zl'=4] {'core','x'}, dimensions={0} | all-to-all | bytes 851968 | tf_op jit(solution)/shard_map/all_to_all | solution.py:330
  49.1 0.0 copy-done.4
  49.1 0.0 copy-done.3
  49.1 0.0 copy-start.1
  49.1 1.6 %blocks.1 = (bf16[8,16,1024]{2,1,0:T(8,128)(2,1)S(1)}, f32[16,128]{1,0:T(8,128)S(1)}, f32[8,128]{1,0:T(8,128)S(1)}) custom-call(bf16[8,16,1664]{2,1,0:T(8,128)(2,1)S(1)} %all_to_all.21.data_ref, bf16[2,512,256]{2,1,0:T(8,128)(2,1)S(1)} %copy-done.4, bf16[2,256,512]{2,1,0:T(8,128)(2,1)S(1)} %copy-done.3, f32[320,256]{1,0:T(8,128)S(1)} %copy-done), custom_call_target="tpu_custom_call" | custom-call | tf_op jit(solution)/shard_map/blocks/pallas_call | solution.py:339
  50.7 9.7 %all_to_all.22.data_ref = bf16[8,16,1024]{2,1,0:T(8,128)(2,1)S(1)} all-to-all(bf16[8,16,1024]{2,1,0:T(8,128)(2,1)S(1)} %get-tuple-element.22), channel_id=1, replica_groups=mesh['zh'=2,'y'=8,'core'=2,'x'=4,'zl'=4] {'core','x'}, dimensions={0} | all-to-all | bytes 524288 | tf_op jit(solution)/shard_map/all_to_all | solution.py:330
  60.4 0.0 copy-done.1
  60.4 0.7 behind.1
  61.1 15.5 %all_to_all.23.data_ref = bf16[64,8,128]{2,1,0:T(8,128)(2,1)S(1)} all-to-all(bf16[64,8,128]{2,1,0:T(8,128)(2,1)S(1)} %behind.1), channel_id=1, replica_groups=mesh['zh'=2,'y'=8,'core'=2,'x'=4,'zl'=4] {'zh','y','zl'}, dimensions={0} | all-to-all | bytes 262144 | tf_op jit(solution)/shard_map/all_to_all | solution.py:330
  76.6 0.9 %gate.1 = f32[512,128]{1,0:T(8,128)} custom-call(f32[512,128]{1,0:T(8,128)S(1)} %get-tuple-element.15.queries_ref, f32[512,128]{1,0:T(8,128)S(1)} %get-tuple-element.16.direct_ref, f32[24,128]{1,0:T(8,128)S(1)} %get-tuple-element.17.head_ref, f32[8,128]{1,0:T(8,128)S(1)} %get-tuple-element.19.inside_ref, f32[8,128]{1,0:T(8,128)S(1)} %get-tuple-element.21.outside_ref, ...), custom_call_target="tpu_custom_call" | custom-call | tf_op jit(solution)/shard_map/gate/pallas_call | solution.py:423
Async XLA Ops:
  0.0 32.3 %copy-start.2 = (bf16[2,768,256]{2,1,0:T(8,128)(2,1)S(1)}, bf16[2,768,256]{2,1,0:T(8,128)(2,1)}, u32[]{:S(2)}) copy-start(bf16[2,768,256]{2,1,0:T(8,128)(2,1)} %constant.10.clone.table_ref) | copy-start | bytes 2359300
  2.4 29.9 %copy-start = (f32[320,256]{1,0:T(8,128)S(1)}, f32[320,256]{1,0:T(8,128)}, u32[]{:S(2)}) copy-start(f32[320,256]{1,0:T(8,128)} %constant.11.clone.twist_ref) | copy-start | bytes 983044
  32.3 16.7 %copy-start.4 = (bf16[2,512,256]{2,1,0:T(8,128)(2,1)S(1)}, bf16[2,512,256]{2,1,0:T(8,128)(2,1)}, u32[]{:S(2)}) copy-start(bf16[2,512,256]{2,1,0:T(8,128)(2,1)} %constant.12.clone.over_ref) | copy-start | bytes 1572868
  33.3 15.7 %copy-start.3 = (bf16[2,256,512]{2,1,0:T(8,128)(2,1)S(1)}, bf16[2,256,512]{2,1,0:T(8,128)(2,1)}, u32[]{:S(2)}) copy-start(bf16[2,256,512]{2,1,0:T(8,128)(2,1)} %constant.13.clone.under_ref) | copy-start | bytes 1572868
  49.1 11.4 %copy-start.1 = (bf16[2,256,768]{2,1,0:T(8,128)(2,1)S(1)}, bf16[2,256,768]{2,1,0:T(8,128)(2,1)}, u32[]{:S(2)}) copy-start(bf16[2,256,768]{2,1,0:T(8,128)(2,1)} %constant.14.clone.table_ref) | copy-start | bytes 2359300

commit v13 on v11

--- a/solution.py
+++ b/solution.py
@@ -83,10 +83,10 @@
     return upper, (value - upper.astype(jnp.float32)).astype(jnp.bfloat16)
 
 
-def short_filter(ext_ref, taps, seg):
-    total = taps[0:1, :] * ext_ref[8 : 8 + seg, :]
+def short_filter(ext_ref, taps, seg, start=0):
+    total = taps[0:1, :] * ext_ref[8 + start : 8 + start + seg, :]
     for tap in range(1, taps.shape[0]):
-        total = total + taps[tap : tap + 1, :] * ext_ref[8 - tap : 8 - tap + seg, :]
+        total = total + taps[tap : tap + 1, :] * ext_ref[8 + start - tap : 8 + start - tap + seg, :]
     return total
 
 
@@ -104,16 +104,11 @@
     head_ref[0:8, :] = ext_ref[8:16, :LANE]
     head_ref[8:11, :] = taps_ref[:, :LANE]
     head_ref[16:17, :] = gain_ref[...]
-    filtered = short_filter(ext_ref, taps_ref[...], seg)
-    mixture = mix_of(filtered)
-    queries_ref[...] = filtered[:, :LANE]
-    direct = gain_ref[...] * mixture
-    direct_ref[...] = direct
-    direct_ref[0:8, :] = jnp.where(lax.broadcasted_iota(jnp.int32, (8, LANE), 0) < 2, 0.0, direct[0:8, :])
     taps = taps_ref[:, LANE:]
     last = ext_ref[7 + seg : 8 + seg, LANE:]
     carry = taps[1:2, :] * last + taps[2:3, :] * ext_ref[6 + seg : 7 + seg, LANE:]
-    ends = [filtered[0:1, LANE:], filtered[1:2, LANE:], carry, taps[2:3, :] * last]
+    opening = short_filter(ext_ref, taps_ref[...], 8)
+    ends = [opening[0:1, LANE:], opening[1:2, LANE:], carry, taps[2:3, :] * last]
     ends = [ends[row][:, half * LANE : (half + 1) * LANE] for row, half in EDGE]
     upper, lower = cut(jnp.concatenate(ends, axis=0))
     pad = jnp.zeros((LANE - 16, LANE), jnp.float32)
@@ -125,7 +120,15 @@
         extra.append(jnp.broadcast_to(ext_ref[row : row + 1, :LANE], (PEERS, LANE)))
     extra.append(jnp.zeros((PEERS, LANE), jnp.float32))
     for hi in range(HIGH):
-        flipped = mixture[hi * LANE : (hi + 1) * LANE, :].T
+        span = slice(hi * LANE, (hi + 1) * LANE)
+        filtered = short_filter(ext_ref, taps_ref[...], LANE, hi * LANE)
+        mixture = mix_of(filtered)
+        queries_ref[span, :] = filtered[:, :LANE]
+        direct = gain_ref[...] * mixture
+        direct_ref[span, :] = direct
+        if hi == 0:
+            direct_ref[0:8, :] = jnp.where(lax.broadcasted_iota(jnp.int32, (8, LANE), 0) < 2, 0.0, direct[0:8, :])
+        flipped = mixture.T
         where = pl.ds(hi, PEERS, stride=HIGH)
         for ch in range(2):
             rows_ref[ch, where, :] = flipped[ch * PEERS : (ch + 1) * PEERS, :]

time: 76.9 us -> 76.9 us (level)
  no operation moved by 1% of the time
where the time goes in v13:
time: 76.9 us; the launch traced here: 76.7 us
  blocking collectives  70.8 us (92%)
  Pallas kernels  5.79 us (8%)
    all_to_all x4, blocking collectives, exchange(): return lax.all_to_all(value, axis, split_axis=0, concat_axis=0, tiled=True)  70.8 us
    pallas_call x3, Pallas kernels, on_chip(): pl.pallas_call(kernel, in_specs=[near] * len(args), out_specs=tuple((near...  3.32 us
    pallas_call x1, Pallas kernels, on_device(): pl.pallas_call(pack_kernel, out_specs=(near,) * 4, out_shape=(pltpu.VMEM(...  1.6 us

profile of v13, /device:TPU:1, one launch (start us, length us, event | category | flops | bytes accessed | tf_op | source)
XLA Modules:
  0.0 76.7 jit_solution(14344850352691050613)
XLA Ops:
  0.0 0.0 copy-start.2
  0.0 1.6 %pack.1 = (bf16[64,4,512]{2,1,0:T(4,128)(2,1)S(1)}, f32[512,128]{1,0:T(8,128)S(1)}, f32[512,128]{1,0:T(8,128)S(1)}, f32[24,128]{1,0:T(8,128)S(1)}) custom-call(bf16[512,384]{1,0:T(8,128)(2,1)} %projected_ref.1, f32[3,384]{1,0:T(4,128)} %taps_ref.1, f32[1,128]{1,0:T(1,128)} %bitcast.3, bf16[4,128]{1,0:T(4,128)(2,1)} %bitcast.2), custom_call_target="tpu_custom_call" | custom-call | flops 200000000 | bytes 800000 | tf_op jit(solution)/shard_map/pack/pallas_call | solution.py:352
  1.6 0.0 copy-start
  1.6 29.9 %all_to_all.20.data_ref = bf16[64,4,512]{2,1,0:T(4,128)(2,1)S(1)} all-to-all(bf16[64,4,512]{2,1,0:T(4,128)(2,1)S(1)} %get-tuple-element.18), channel_id=1, replica_groups=mesh['zh'=2,'y'=8,'core'=2,'x'=4,'zl'=4] {'zh','y','zl'}, dimensions={0} | all-to-all | bytes 524288 | tf_op jit(solution)/shard_map/all_to_all | solution.py:323
  31.5 0.0 copy-done.2
  31.5 0.0 copy-done
  31.5 0.0 copy-start.4
  31.5 1.0 %ahead.1 = (bf16[8,16,1664]{2,1,0:T(8,128)(2,1)S(1)}, f32[64,128]{1,0:T(8,128)S(1)}, f32[8,128]{1,0:T(8,128)S(1)}) custom-call(bf16[64,4,512]{2,1,0:T(4,128)(2,1)S(1)} %all_to_all.20.data_ref, bf16[2,768,256]{2,1,0:T(8,128)(2,1)S(1)} %copy-done.2, f32[320,256]{1,0:T(8,128)S(1)} %copy-done), custom_call_target="tpu_custom_call" | custom-call | tf_op jit(solution)/shard_map/ahead/pallas_call | solution.py:332
  32.5 0.0 copy-start.3
  32.5 15.7 %all_to_all.21.data_ref = bf16[8,16,1664]{2,1,0:T(8,128)(2,1)S(1)} all-to-all(bf16[8,16,1664]{2,1,0:T(8,128)(2,1)S(1)} %get-tuple-element.20), channel_id=1, replica_groups=mesh['zh'=2,'y'=8,'core'=2,'x'=4,'zl'=4] {'core','x'}, dimensions={0} | all-to-all | bytes 851968 | tf_op jit(solution)/shard_map/all_to_all | solution.py:323
  48.2 0.0 copy-done.4
  48.2 0.0 copy-done.3
  48.2 0.0 copy-start.1
  48.3 1.6 %blocks.1 = (bf16[8,16,1024]{2,1,0:T(8,128)(2,1)S(1)}, f32[16,128]{1,0:T(8,128)S(1)}, f32[8,128]{1,0:T(8,128)S(1)}) custom-call(bf16[8,16,1664]{2,1,0:T(8,128)(2,1)S(1)} %all_to_all.21.data_ref, bf16[2,512,256]{2,1,0:T(8,128)(2,1)S(1)} %copy-done.4, bf16[2,256,512]{2,1,0:T(8,128)(2,1)S(1)} %copy-done.3, f32[320,256]{1,0:T(8,128)S(1)} %copy-done), custom_call_target="tpu_custom_call" | custom-call | tf_op jit(solution)/shard_map/blocks/pallas_call | solution.py:332
  49.9 9.7 %all_to_all.22.data_ref = bf16[8,16,1024]{2,1,0:T(8,128)(2,1)S(1)} all-to-all(bf16[8,16,1024]{2,1,0:T(8,128)(2,1)S(1)} %get-tuple-element.22), channel_id=1, replica_groups=mesh['zh'=2,'y'=8,'core'=2,'x'=4,'zl'=4] {'core','x'}, dimensions={0} | all-to-all | bytes 524288 | tf_op jit(solution)/shard_map/all_to_all | solution.py:323
  59.6 0.0 copy-done.1
  59.6 0.7 behind.1
  60.3 15.5 %all_to_all.23.data_ref = bf16[64,8,128]{2,1,0:T(8,128)(2,1)S(1)} all-to-all(bf16[64,8,128]{2,1,0:T(8,128)(2,1)S(1)} %behind.1), channel_id=1, replica_groups=mesh['zh'=2,'y'=8,'core'=2,'x'=4,'zl'=4] {'zh','y','zl'}, dimensions={0} | all-to-all | bytes 262144 | tf_op jit(solution)/shard_map/all_to_all | solution.py:323
  75.8 0.9 %gate.1 = f32[512,128]{1,0:T(8,128)} custom-call(f32[512,128]{1,0:T(8,128)S(1)} %get-tuple-element.15.queries_ref, f32[512,128]{1,0:T(8,128)S(1)} %get-tuple-element.16.direct_ref, f32[24,128]{1,0:T(8,128)S(1)} %get-tuple-element.17.head_ref, f32[8,128]{1,0:T(8,128)S(1)} %get-tuple-element.19.inside_ref, f32[8,128]{1,0:T(8,128)S(1)} %get-tuple-element.21.outside_ref, ...), custom_call_target="tpu_custom_call" | custom-call | tf_op jit(solution)/shard_map/gate/pallas_call | solution.py:410
Async XLA Ops:
  0.0 31.5 %copy-start.2 = (bf16[2,768,256]{2,1,0:T(8,128)(2,1)S(1)}, bf16[2,768,256]{2,1,0:T(8,128)(2,1)}, u32[]{:S(2)}) copy-start(bf16[2,768,256]{2,1,0:T(8,128)(2,1)} %constant.10.clone.table_ref) | copy-start | bytes 2359300
  1.6 29.9 %copy-start = (f32[320,256]{1,0:T(8,128)S(1)}, f32[320,256]{1,0:T(8,128)}, u32[]{:S(2)}) copy-start(f32[320,256]{1,0:T(8,128)} %constant.11.clone.twist_ref) | copy-start | bytes 983044
  31.5 16.7 %copy-start.4 = (bf16[2,512,256]{2,1,0:T(8,128)(2,1)S(1)}, bf16[2,512,256]{2,1,0:T(8,128)(2,1)}, u32[]{:S(2)}) copy-start(bf16[2,512,256]{2,1,0:T(8,128)(2,1)} %constant.12.clone.over_ref) | copy-start | bytes 1572868
  32.5 15.7 %copy-start.3 = (bf16[2,256,512]{2,1,0:T(8,128)(2,1)S(1)}, bf16[2,256,512]{2,1,0:T(8,128)(2,1)}, u32[]{:S(2)}) copy-start(bf16[2,256,512]{2,1,0:T(8,128)(2,1)} %constant.13.clone.under_ref) | copy-start | bytes 1572868
  48.2 11.4 %copy-start.1 = (bf16[2,256,768]{2,1,0:T(8,128)(2,1)S(1)}, bf16[2,256,768]{2,1,0:T(8,128)(2,1)}, u32[]{:S(2)}) copy-start(bf16[2,256,768]{2,1,0:T(8,128)(2,1)} %constant.14.clone.table_ref) | copy-start | bytes 2359300
